TPU v7x, 32 devices: a whole 2x2x4 slice. The times are simulated.
32 devices in a mesh: dp: 8 (over z, core), expert: 4 (over y, x).
Axes of the slice: x: 2, y: 2, z: 4, core: 2. Of those that a mesh axis runs over, the one named last changes fastest.
Arguments:
- history: bfloat16 [64, 1024, 2048], P(('dp', 'expert')), may hold values from -6 to 6
- lengths: int32 [64], P(('dp', 'expert')), may hold values from 64 to 1024, as said below
- user_query: bfloat16 [64, 2048], P(('dp', 'expert')), may hold values from -1000 to 1000
- pos_item: bfloat16 [64, 2048], P(('dp', 'expert')), may hold values from -6 to 6
- neg_index: int32 [64, 63], P(('dp', 'expert')), may hold values from 0 to 63
- routes: int32 [4096, 2], P(('dp', 'expert')), may hold values from 0 to 3, all different within a row; in each aligned block of 128 rows (0 to 127, 128 to 255, ...) at most 128 rows name the same one
- w_router: bfloat16 [2048, 4], replicated, may hold values from -0.125 to 0.125
- w_gate: bfloat16 [4, 2048, 768], P('expert', 'dp'), may hold values from -0.125 to 0.125
- w_up: bfloat16 [4, 2048, 768], P('expert', 'dp'), may hold values from -0.125 to 0.125
- w_down: bfloat16 [4, 768, 2048], P('expert', None, 'dp'), may hold values from -0.21875 to 0.21875
- out_gain: float32 [2048], replicated, may hold values from 0.25 to 1.75
Outputs:
- losses: float32 [64], P(('dp', 'expert'))
- grad_gate: float32 [4, 2048, 768], P('expert', 'dp')
- grad_up: float32 [4, 2048, 768], P('expert', 'dp')
- grad_down: float32 [4, 768, 2048], P('expert', None, 'dp')
- grad_router: float32 [2048, 4], replicated
Inputs may be any that keep to these rules, and one draw needn't show every extreme that they name: `lengths`: every device's block of 2 users holds one user with all 1024 events. `neg_index`: indices of users anywhere in the batch. `routes`: each row names two different experts; among the rows of one device no expert is named more than 128 times, a bound that some block reaches.
All inputs are finite; a program needn't handle non-finite values.
Results may differ from a plain program's by a relative error of at most 0.017.
Values may be sent and summed in bfloat16 or wider, within the bound.
No kernel may reach another device: no remote copies, remote signals or barrier semaphores. Data moves between devices by JAX's collectives and lax.ppermute only.
A program may use at most 128 MiB of HBM per device.

v0:
```python
import math

import jax
import jax.numpy as jnp
from jax import lax
from jax.sharding import PartitionSpec as P


CANDS = 64
HEAD = 128

norm_eps = 1e-06
loss_scale = 1024.0


def silu_pair(pre_act):
    sigma_val = jax.nn.sigmoid(pre_act)
    return (pre_act * sigma_val, sigma_val * (1.0 + pre_act * (1.0 - sigma_val)))


def rms_round(values):
    scale_inv = lax.rsqrt(jnp.mean(values * values, axis=-1, keepdims=True) + norm_eps)
    return (values * scale_inv).astype(jnp.bfloat16)


def dp_shift(value, step):
    size = lax.axis_size("dp")
    nz = size // 2
    return lax.ppermute(
        value, "dp", [(2 * z + c, 2 * ((z + step) % nz) + c) for z in range(nz) for c in range(2)]
    )


def dp_pairs(value, targets):
    return lax.ppermute(
        value, "dp", [(2 * z + c, 2 * t + c) for z, t in enumerate(targets) for c in range(2)]
    )


def core_swap(value):
    size = lax.axis_size("dp")
    return lax.ppermute(value, "dp", [(i, i ^ 1) for i in range(size)])


def dp_xor(value, mask):
    size = lax.axis_size("dp")
    return lax.ppermute(value, "dp", [(i, i ^ mask) for i in range(size)])


def expert_xor(value, mask):
    size = lax.axis_size("expert")
    return lax.ppermute(value, "expert", [(i, i ^ mask) for i in range(size)])


RELAY_OUT = (2, 0, 3, 1)
RELAY_BACK = (1, 3, 0, 2)


def column_order(nz):
    return (0, 1, 3, 2) if nz == 4 else tuple(range(nz))


def add_up(*terms):
    total = terms[0].astype(jnp.float32)
    for term in terms[1:]:
        total = total + term.astype(jnp.float32)
    return total


def local(
    history,
    lengths,
    user_query,
    pos_item,
    neg_index,
    routes,
    w_router,
    w_gate,
    w_up,
    w_down,
    out_gain,
):
    user_count, hist_len, model_width = history.shape
    head_count = model_width // HEAD
    experts = w_router.shape[1]
    hidden_width = w_gate.shape[2]
    dp_size = lax.axis_size("dp")
    ep_size = lax.axis_size("expert")
    nz = dp_size // 2
    relay = nz == 4
    me_dp = lax.axis_index("dp")
    me_ep = lax.axis_index("expert")
    z = me_dp // 2
    core = me_dp % 2
    row_total = user_count * CANDS
    slice_width = model_width // dp_size
    order = column_order(nz)
    blocks = [(j, o) for j in order for o in range(2)]
    early = model_width - 2 * slice_width

    def block_index(j, other):
        return ((z - j) % nz) * 2 + (core ^ other)

    def arrange(value, axis):
        return jnp.concatenate(
            [
                lax.dynamic_slice_in_dim(
                    value, block_index(j, o) * slice_width, slice_width, axis
                )
                for j, o in blocks
            ],
            axis=axis,
        )

    def shifts(own):
        if relay:
            return {0: own, 1: dp_shift(own, 1), 3: dp_shift(own, 3)}
        return {j: dp_shift(own, j) if j else own for j in range(nz)}

    def relays(slots):
        if not relay:
            return slots
        payload = jnp.where(z == 1, slots[3], jnp.where(z == 2, slots[1], slots[0]))
        return {**slots, 2: dp_pairs(payload, RELAY_OUT)}

    items = jnp.stack([pos_item] + [expert_xor(pos_item, k) for k in range(1, ep_size)])
    items = jnp.stack([items] + [dp_shift(items, j) for j in range(1, nz)])
    items = jnp.stack([items, core_swap(items)]).reshape(-1, model_width)

    gu_own = jnp.concatenate([w_gate[0], w_up[0]], axis=1)
    gu_slots = relays(shifts(gu_own))
    down_slots = relays(shifts(w_down[0]))

    query_heads = user_query.reshape(user_count, head_count, HEAD)
    key_heads = history.reshape(user_count, hist_len, head_count, HEAD)
    scores = jnp.einsum(
        "uhd,uthd->uht", query_heads, key_heads, preferred_element_type=jnp.float32
    ) / math.sqrt(HEAD)
    live_mask = jnp.arange(hist_len, dtype=jnp.int32)[None, None, :] < lengths[:, None, None]
    scores = jnp.where(live_mask, scores, -1e30)
    top_val = jnp.max(scores, axis=-1, keepdims=True)
    weights = jnp.where(live_mask, jnp.exp(scores - top_val), 0.0)
    attn_probs = (weights / jnp.sum(weights, axis=-1, keepdims=True)).astype(jnp.bfloat16)
    context = jnp.einsum(
        "uht,uthd->uhd", attn_probs, key_heads, preferred_element_type=jnp.float32
    ).reshape(user_count, model_width)

    owner = neg_index // user_count
    owner_dp, owner_ep = owner // ep_size, owner % ep_size
    slot = (((owner_dp % 2) ^ core) * nz + (z - owner_dp // 2) % nz) * ep_size + (owner_ep ^ me_ep)
    table = arrange(items, 1)
    negatives = table[slot * user_count + neg_index % user_count]
    candidates = jnp.concatenate([table[:user_count, None, :], negatives], axis=1)
    x_sum = candidates.astype(jnp.float32) + arrange(context, 1)[:, None, :]
    x_sum = x_sum.reshape(row_total, model_width)
    normed = rms_round(x_sum)
    gain = arrange(out_gain, 0)
    query_f = arrange(user_query, 1).astype(jnp.float32)
    router = arrange(w_router, 0)
    rows_in = jnp.concatenate([normed] + [expert_xor(normed, k) for k in range(1, ep_size)])

    logits = jnp.dot(normed, router, preferred_element_type=jnp.float32)
    route_hot = routes[:, :, None] == jnp.arange(experts, dtype=jnp.int32)
    affinity = jax.nn.sigmoid(jnp.sum(jnp.where(route_hot, logits[:, None, :], 0.0), axis=-1))
    aff_total = jnp.sum(affinity, axis=1, keepdims=True)
    mix = affinity / aff_total
    mix_dense = jnp.sum(jnp.where(route_hot, mix[:, :, None], 0.0), axis=1)
    mix_rows = mix_dense.T
    mix_slots = jnp.stack([mix_rows] + [expert_xor(mix_rows, k) for k in range(1, ep_size)])
    mix_here = lax.dynamic_index_in_dim(mix_slots, me_ep, 1, keepdims=False).reshape(-1, 1)
    mix_cols = [
        lax.dynamic_index_in_dim(mix_dense, me_ep ^ k, 1, keepdims=True)
        for k in range(ep_size)
    ]

    def lay(slots, js, axis):
        return jnp.concatenate(
            [part for j in js for part in (slots[j], core_swap(slots[j]))], axis=axis
        )

    gu_full = lay(gu_slots, order, 0)
    pre = jnp.dot(rows_in, gu_full, preferred_element_type=jnp.float32)
    gate_pre, up_pre = pre[:, :hidden_width], pre[:, hidden_width:]
    silu_val, silu_grad = silu_pair(gate_pre)
    hidden = (silu_val * up_pre).astype(jnp.bfloat16)
    hidden_mix = (mix_here * hidden.astype(jnp.float32)).astype(jnp.bfloat16)
    gate_slope = (mix_here * (up_pre * silu_grad)).astype(jnp.bfloat16)
    up_slope = (mix_here * silu_val).astype(jnp.bfloat16)
    hidden, hidden_mix, gate_slope, up_slope = lax.optimization_barrier(
        (hidden, hidden_mix, gate_slope, up_slope)
    )

    def returned(columns):
        out = jnp.dot(hidden, columns, preferred_element_type=jnp.float32)
        out = out.astype(jnp.bfloat16).reshape(ep_size, row_total, columns.shape[1])
        return [out[0]] + [expert_xor(out[k], k) for k in range(1, ep_size)]

    down_a = lay(down_slots, order[:-1], 1)
    out_a = returned(down_a)
    down_b = lay(down_slots, order[-1:], 1)
    out_b = returned(down_b)
    moe_a, moe_b = x_sum[:, :early], x_sum[:, early:]
    for col, a, b in zip(mix_cols, out_a, out_b):
        moe_a = moe_a + col * a.astype(jnp.float32)
        moe_b = moe_b + col * b.astype(jnp.float32)
    h_rows = jnp.concatenate([moe_a, moe_b], axis=1).reshape(user_count, CANDS, model_width)
    inv_rms = lax.rsqrt(jnp.mean(h_rows * h_rows, axis=-1, keepdims=True) + norm_eps)
    unit_rows = h_rows * inv_rms
    scored = unit_rows * gain
    listwise = jnp.sum(scored * query_f[:, None, :], axis=-1) / math.sqrt(model_width)
    top_list = jnp.max(listwise, axis=-1, keepdims=True)
    expo = jnp.exp(listwise - top_list)
    expo_total = jnp.sum(expo, axis=-1, keepdims=True)
    losses = jnp.log(expo_total[:, 0]) + top_list[:, 0] - listwise[:, 0]
    first_one = (jnp.arange(CANDS, dtype=jnp.int32) == 0).astype(jnp.float32)[None, :]
    d_list = loss_scale * (expo / expo_total - first_one)
    d_scored = d_list[..., None] * query_f[:, None, :] / math.sqrt(model_width)
    d_unit = d_scored * gain
    d_h = inv_rms * (d_unit - unit_rows * jnp.mean(d_unit * unit_rows, axis=-1, keepdims=True))
    d_h = d_h.reshape(row_total, model_width)
    d_send = d_h.astype(jnp.bfloat16)
    piece = d_send[:, early:]
    d_b = jnp.concatenate([piece] + [expert_xor(piece, k) for k in range(1, ep_size)])
    piece = d_send[:, :early]
    d_a = jnp.concatenate([piece] + [expert_xor(piece, k) for k in range(1, ep_size)])

    contract_rows = (((0,), (0,)), ((), ()))
    contract_cols = (((1,), (1,)), ((), ()))

    def chip_terms(left, right):
        part = lax.dot_general(left, right, contract_rows, preferred_element_type=jnp.float32)
        part = part.astype(jnp.bfloat16).reshape(-1, 2, slice_width, right.shape[1])
        return add_up(part[:, 0], core_swap(part[:, 1])).astype(jnp.bfloat16)

    def send_relay(term):
        return dp_pairs(term, RELAY_BACK) if relay else None

    def send_rest(terms, last, relayed):
        by_chip = {j: terms[i] for i, j in enumerate(order[:-1])}
        if not relay:
            by_chip[order[-1]] = last
            moved = [dp_shift(by_chip[j], nz - j) for j in range(1, nz)]
            return add_up(by_chip[0], *moved)
        zero = jnp.zeros_like(relayed)
        down = add_up(by_chip[1], jnp.where(z == 2, relayed, zero)).astype(jnp.bfloat16)
        up = add_up(by_chip[3], jnp.where(z == 1, relayed, zero)).astype(jnp.bfloat16)
        own = jnp.where((z == 0) | (z == 3), relayed, zero)
        moved = dp_shift(down, 3), dp_shift(up, 1)
        return add_up(by_chip[0], own, *moved)

    last_down = chip_terms(d_b, hidden_mix)[0]
    relay_down = send_relay(last_down)
    terms_down = chip_terms(d_a, hidden_mix)
    d_hidden = lax.dot_general(
        d_a, down_a, contract_cols, preferred_element_type=jnp.float32
    ) + lax.dot_general(d_b, down_b, contract_cols, preferred_element_type=jnp.float32)
    d_pre = jnp.concatenate(
        [
            (d_hidden * gate_slope.astype(jnp.float32)).astype(jnp.bfloat16),
            (d_hidden * up_slope.astype(jnp.float32)).astype(jnp.bfloat16),
        ],
        axis=1,
    )
    last_gu = chip_terms(rows_in[:, early:], d_pre)[0]
    relay_gu = send_relay(last_gu)
    sum_down = send_rest(terms_down, last_down, relay_down)
    terms_gu = chip_terms(rows_in[:, :early], d_pre)
    sum_gu = send_rest(terms_gu, last_gu, relay_gu)

    d_dense = jnp.zeros((row_total, experts), jnp.float32)
    lanes = jnp.arange(experts, dtype=jnp.int32)[None, :]
    for k, (a, b) in enumerate(zip(out_a, out_b)):
        dots = jnp.sum(d_h[:, :early] * a.astype(jnp.float32), axis=-1, keepdims=True)
        dots += jnp.sum(d_h[:, early:] * b.astype(jnp.float32), axis=-1, keepdims=True)
        d_dense = d_dense + jnp.where(lanes == (me_ep ^ k), dots, 0.0)
    mix_dot = jnp.sum(mix_dense * d_dense, axis=1, keepdims=True)
    aff_dense = jnp.sum(jnp.where(route_hot, affinity[:, :, None], 0.0), axis=1)
    d_logits = ((d_dense - mix_dot) / aff_total * aff_dense * (1.0 - aff_dense)).astype(
        jnp.bfloat16
    )
    arranged = lax.dot_general(d_logits, normed, contract_rows, preferred_element_type=jnp.float32)
    router_term = jnp.zeros_like(arranged)
    for i, (j, o) in enumerate(blocks):
        router_term = lax.dynamic_update_slice_in_dim(
            router_term,
            arranged[:, i * slice_width : (i + 1) * slice_width],
            block_index(j, o) * slice_width,
            1,
        )
    mask = 1
    while mask < ep_size:
        router_term = router_term + expert_xor(router_term, mask)
        mask *= 2
    mask = 1
    while mask < dp_size:
        router_term = router_term + dp_xor(router_term, mask)
        mask *= 2
    return (
        losses,
        sum_gu[:, :hidden_width][None],
        sum_gu[:, hidden_width:][None],
        sum_down.T[None],
        router_term.T,
    )


def solution(mesh):
    both = ("dp", "expert")
    placed = (
        P(both, None, None),
        P(both),
        P(both, None),
        P(both, None),
        P(both, None),
        P(both, None),
        P(),
        P("expert", "dp", None),
        P("expert", "dp", None),
        P("expert", None, "dp"),
        P(),
    )
    return jax.shard_map(
        local,
        mesh=mesh,
        in_specs=placed,
        out_specs=(
            P(both),
            P("expert", "dp", None),
            P("expert", "dp", None),
            P("expert", None, "dp"),
            P(),
        ),
        check_vma=False,
    )
```

profile of v0, /device:TPU:0, one launch (start us, length us, event | category | flops | bytes accessed | tf_op | source)
XLA Modules:
  0.0 303.7 jit_solution(2112982598044840295)
XLA Ops:
  0.6 2.0 pad_maximum_fusion.6
  2.7 3.1 %collective-permute-start.11 = (bf16[256,1536]{1,0:T(8,128)(2,1)}, bf16[256,1536]{1,0:T(8,128)(2,1)}, u32[]{:S(2)}, u32[]{:S(2)}) collective-permute-start(bf16[256,1536]{1,0:T(8,128)(2,1)} %pad_maximum_fusion.6), channel_id=1, source_target_pairs={{0,8},{4,12},{8,16},{12,20},{16,24},{20,28},{24,0},{28,4},{1,9},{5... | collective-permute-start | bytes 2359304 | tf_op jit(solution)/shard_map/ppermute | solution.py:29
  5.7 2.0 collective-permute-start.13
  7.8 1.7 collective-permute-start
  9.5 1.5 collective-permute-start.1
  12.7 5.6 %fusion.2 = f32[2,16,1,1024]{3,2,1,0:T(1,128)S(1)} fusion(bf16[2,16,128,1]{2,3,1,0:T(2,128)(2,1)S(1)} %reshape.436, bf16[2,1024,2048]{2,1,0:T(8,128)(2,1)} %param.11), kind=kOutput, calls=%fused_computation.3 | convolution fusion | flops 8388608 | bytes 8527872 | tf_op jit(solution)/shard_map/uhd,uthd->uht/dot_general | solution.py:136
  18.6 5.1 %fusion.4 = f32[2,16,1,128]{3,2,1,0:T(1,128)S(1)} fusion(bf16[2,16,1024,1]{2,1,0,3:T(8,128)(2,1)S(1)} %fusion.22, bf16[2,1024,2048]{2,1,0:T(8,128)(2,1)} %param.11), kind=kOutput, calls=%fused_computation.5 | convolution fusion | flops 8388608 | bytes 8470528 | tf_op jit(solution)/shard_map/uht,uthd->uhd/dot_general | solution.py:144
  26.0 2.6 collective-permute-start.4
  28.6 1.3 collective-permute-start.5
  30.0 13.9 %collective-permute-done.3 = bf16[4,2,2048]{2,1,0:T(2,128)(2,1)S(1)} collective-permute-done((bf16[4,2,2048]{2,1,0:T(2,128)(2,1)S(1)}, bf16[4,2,2048]{2,1,0:T(2,128)(2,1)S(1)}, u32[]{:S(2)}, u32[]{:S(2)}) %collective-permute-start.3) | collective-permute-done | bytes 32800 | tf_op jit(solution)/shard_map/ppermute | solution.py:29
  48.9 1.6 collective-permute-start.17
  50.5 1.5 collective-permute-start.18
  54.1 2.4 collective-permute-done.19
  56.5 2.2 collective-permute-start.23
  58.8 7.9 %collective-permute-done.21 = bf16[768,256]{1,0:T(8,128)(2,1)S(1)} collective-permute-done((bf16[768,256]{1,0:T(8,128)(2,1)}, bf16[768,256]{1,0:T(8,128)(2,1)S(1)}, u32[]{:S(2)}, u32[]{:S(2)}) %collective-permute-start.21) | collective-permute-done | bytes 393248 | tf_op jit(solution)/shard_map/ppermute | solution.py:29
  67.1 6.2 %collective-permute-done.23 = bf16[768,256]{1,0:T(8,128)(2,1)S(1)} collective-permute-done((bf16[768,256]{1,0:T(8,128)(2,1)}, bf16[768,256]{1,0:T(8,128)(2,1)S(1)}, u32[]{:S(2)}, u32[]{:S(2)}) %collective-permute-start.23) | collective-permute-done | bytes 393248 | tf_op jit(solution)/shard_map/ppermute | solution.py:29
  75.4 1.9 collective-permute-start.15
  78.4 1.2 constant_dynamic-update-slice_fusion.29
  79.6 1.6 collective-permute-start.7
  81.2 22.6 %collective-permute-done.28 = bf16[768,256]{1,0:T(8,128)(2,1)S(1)} collective-permute-done((bf16[768,256]{1,0:T(8,128)(2,1)S(1)}, bf16[768,256]{1,0:T(8,128)(2,1)S(1)}, u32[]{:S(2)}, u32[]{:S(2)}) %collective-permute-start.28) | collective-permute-done | bytes 393248 | tf_op jit(solution)/shard_map/ppermute | solution.py:35
  103.8 1.5 collective-permute-start.8
  106.0 1.5 collective-permute-start.9
  108.3 20.2 %collective-permute-done.8 = bf16[128,2048]{1,0:T(8,128)(2,1)S(1)} collective-permute-done((bf16[128,2048]{1,0:T(8,128)(2,1)S(1)}, bf16[128,2048]{1,0:T(8,128)(2,1)S(1)}, u32[]{:S(2)}, u32[]{:S(2)}) %collective-permute-start.8) | collective-permute-done | bytes 524320 | tf_op jit(solution)/shard_map/ppermute | solution.py:52
  128.5 3.4 %fusion.107 = f32[512,1536]{1,0:T(8,128)S(1)} fusion(bf16[2048,1536]{1,0:T(8,128)(2,1)S(1)} %constant_dynamic-update-slice_fusion.24, bf16[128,2048]{1,0:T(8,128)(2,1)S(1)} %collective-permute-done.9, bf16[128,2048]{1,0:T(8,128)(2,1)S(1)} %collective-permute-done.8, bf16[128,2048]{1,0:T(8,128)(2,1)S(1)} %collective-permute-done.7, ...), kind=kOutput, calls=%fused_computation.323 | convolution fusion | flops 3229614080 | bytes 11534336 | tf_op jit(solution)/shard_map/dot_general | solution.py:182
  131.9 2.3 multiply_convert_fusion.2
  134.2 1.4 convolution_convert_fusion.3
  136.2 1.6 collective-permute-start.30
  138.5 1.5 collective-permute-start.26
  140.0 1.4 collective-permute-start.27
  141.4 1.5 collective-permute-start.31
  143.0 2.2 collective-permute-start.32
  145.1 1.6 pad_maximum_fusion
  146.7 15.1 %collective-permute-done.31 = bf16[128,512]{1,0:T(8,128)(2,1)S(1)} collective-permute-done((bf16[128,512]{1,0:T(8,128)(2,1)S(1)}, bf16[128,512]{1,0:T(8,128)(2,1)S(1)}, u32[]{:S(2)}, u32[]{:S(2)}) %collective-permute-start.31) | collective-permute-done | bytes 131104 | tf_op jit(solution)/shard_map/ppermute | solution.py:52
  164.6 1.6 collective-permute-start.36
  166.2 1.5 collective-permute-start.37
  168.2 1.6 collective-permute-start.33
  169.8 1.5 collective-permute-start.34
  172.4 1.4 fusion.30
  180.1 1.5 collective-permute-start.49
  181.6 1.5 convolution_convert_fusion.4
  183.0 1.8 fusion.61
  184.9 3.5 %collective-permute-done.35 = bf16[128,1536]{1,0:T(8,128)(2,1)S(1)} collective-permute-done((bf16[128,1536]{1,0:T(8,128)(2,1)S(1)}, bf16[128,1536]{1,0:T(8,128)(2,1)S(1)}, u32[]{:S(2)}, u32[]{:S(2)}) %collective-permute-start.35) | collective-permute-done | bytes 393248 | tf_op jit(solution)/shard_map/ppermute | solution.py:52
  188.4 1.4 convolution_convert_fusion.1
  190.1 1.7 copy.50
  191.8 4.6 %multiply_convert_fusion.1 = (bf16[512,768]{1,0:T(8,128)(2,1)S(1)}, bf16[512,768]{1,0:T(8,128)(2,1)S(1)}) fusion(bf16[512,768]{1,0:T(8,128)(2,1)} %get-tuple-element.10, bf16[512,768]{1,0:T(8,128)(2,1)} %get-tuple-element.11, f32[512,768]{1,0:T(8,128)} %fusion.61, bf16[768,1536]{1,0:T(8,128)(2,1)} %copy-done.26, bf16[128,1536]{1,0:T(8,128)(2,1)} %copy-done.35, ...), kind=kOutput, calls=%fused_computation.33 | convolution fusion | flops 1217003520 | bytes 8650752 | tf_op jit(solution)/shard_map/dot_general | solution.py:254
  196.4 3.1 %convolution_convert_fusion = bf16[1536,1536]{1,0:T(8,128)(2,1)S(1)} fusion(bf16[512,2048]{1,0:T(8,128)(2,1)S(1)} %copy-done.2, bf16[512,768]{1,0:T(8,128)(2,1)S(1)} %get-tuple-element.44, bf16[512,768]{1,0:T(8,128)(2,1)S(1)} %get-tuple-element.43), kind=kOutput, calls=%fused_computation.7 | convolution fusion | flops 2421424128 | bytes 7864320 | tf_op jit(solution)/shard_map/dot_general | solution.py:231
  199.5 1.6 slice_bitcast_fusion
  201.1 1.2 copy-done
  207.2 1.5 collective-permute-start.50
  208.8 2.5 collective-permute-done.50
  212.5 1.5 collective-permute-start.52
  214.6 1.9 collective-permute-done.52
  217.1 2.8 collective-permute-start.53
  222.2 1.6 fusion.34
  223.7 1.4 collective-permute-start.41
  225.1 1.5 fusion.9
  226.7 3.0 fusion.8
  229.7 19.7 %collective-permute-done.41 = bf16[256,1536]{1,0:T(8,128)(2,1)S(1)} collective-permute-done((bf16[256,1536]{1,0:T(8,128)(2,1)S(1)}, bf16[256,1536]{1,0:T(8,128)(2,1)S(1)}, u32[]{:S(2)}, u32[]{:S(2)}) %collective-permute-start.41) | collective-permute-done | bytes 786464 | tf_op jit(solution)/shard_map/ppermute | solution.py:35
  249.8 1.4 collective-permute-start.42
  252.1 3.2 %collective-permute-start.47 = (bf16[256,768]{0,1:T(8,128)(2,1)S(1)}, bf16[256,768]{0,1:T(8,128)(2,1)S(1)}, u32[]{:S(2)}, u32[]{:S(2)}) collective-permute-start(bf16[256,768]{0,1:T(8,128)(2,1)S(1)} %get-tuple-element.39), channel_id=1, source_target_pairs={{0,24},{4,28},{8,0},{12,4},{16,8},{20,12},{24,16},{28,20},{1,25},{... | collective-permute-start | bytes 1179656 | tf_op jit(solution)/shard_map/ppermute | solution.py:29
  255.4 1.4 add_bitcast_fusion
  256.8 38.2 %collective-permute-done.47 = bf16[256,768]{0,1:T(8,128)(2,1)S(1)} collective-permute-done((bf16[256,768]{0,1:T(8,128)(2,1)S(1)}, bf16[256,768]{0,1:T(8,128)(2,1)S(1)}, u32[]{:S(2)}, u32[]{:S(2)}) %collective-permute-start.47) | collective-permute-done | bytes 393248 | tf_op jit(solution)/shard_map/ppermute | solution.py:29
  294.9 6.0 %collective-permute-done.48 = bf16[256,768]{0,1:T(8,128)(2,1)S(1)} collective-permute-done((bf16[256,768]{0,1:T(8,128)(2,1)S(1)}, bf16[256,768]{0,1:T(8,128)(2,1)S(1)}, u32[]{:S(2)}, u32[]{:S(2)}) %collective-permute-start.48) | collective-permute-done | bytes 393248 | tf_op jit(solution)/shard_map/ppermute | solution.py:29
  302.5 1.2 slice_bitcast_fusion.2
  (282 shorter events, 40.4 us)
Async XLA Ops:
  2.7 72.3 %collective-permute-start.11 = (bf16[256,1536]{1,0:T(8,128)(2,1)}, bf16[256,1536]{1,0:T(8,128)(2,1)}, u32[]{:S(2)}, u32[]{:S(2)}) collective-permute-start(bf16[256,1536]{1,0:T(8,128)(2,1)} %pad_maximum_fusion.6), channel_id=1, source_target_pairs={{0,8},{4,12},{8,16},{12,20},{16,24},{20,28},{24,0},{28,4},{1,9},{5... | collective-permute-start | bytes 2359304 | tf_op jit(solution)/shard_map/ppermute | solution.py:29
  5.7 69.3 %collective-permute-start.13 = (bf16[256,1536]{1,0:T(8,128)(2,1)}, bf16[256,1536]{1,0:T(8,128)(2,1)S(1)}, u32[]{:S(2)}, u32[]{:S(2)}) collective-permute-start(bf16[256,1536]{1,0:T(8,128)(2,1)} %pad_maximum_fusion.6), channel_id=1, source_target_pairs={{0,24},{4,28},{8,0},{12,4},{16,8},{20,12},{24,16},{28,20},{1,25},{... | collective-permute-start | bytes 2359304 | tf_op jit(solution)/shard_map/ppermute | solution.py:29
  7.8 18.1 %collective-permute-start = (bf16[2,2048]{1,0:T(2,128)(2,1)}, bf16[2,2048]{1,0:T(2,128)(2,1)S(1)}, u32[]{:S(2)}, u32[]{:S(2)}) collective-permute-start(bf16[2,2048]{1,0:T(2,128)(2,1)} %param.14), channel_id=1, source_target_pairs={{0,1},{1,0},{2,3},{3,2},{4,5},{5,4},{6,7},{7,6},{8,9},{9,8},{10,11... | collective-permute-start | bytes 24584 | tf_op jit(solution)/shard_map/ppermute | solution.py:52
  9.5 16.4 %collective-permute-start.1 = (bf16[2,2048]{1,0:T(2,128)(2,1)}, bf16[2,2048]{1,0:T(2,128)(2,1)S(1)}, u32[]{:S(2)}, u32[]{:S(2)}) collective-permute-start(bf16[2,2048]{1,0:T(2,128)(2,1)} %param.14), channel_id=1, source_target_pairs={{0,2},{1,3},{2,0},{3,1},{4,6},{5,7},{6,4},{7,5},{8,10},{9,11},{10,... | collective-permute-start | bytes 24584 | tf_op jit(solution)/shard_map/ppermute | solution.py:52
  11.0 14.9 %collective-permute-start.2 = (bf16[2,2048]{1,0:T(2,128)(2,1)}, bf16[2,2048]{1,0:T(2,128)(2,1)S(1)}, u32[]{:S(2)}, u32[]{:S(2)}) collective-permute-start(bf16[2,2048]{1,0:T(2,128)(2,1)} %param.14), channel_id=1, source_target_pairs={{0,3},{1,2},{2,1},{3,0},{4,7},{5,6},{6,5},{7,4},{8,11},{9,10},{10,... | collective-permute-start | bytes 24584 | tf_op jit(solution)/shard_map/ppermute | solution.py:52
  26.0 17.9 %collective-permute-start.3 = (bf16[4,2,2048]{2,1,0:T(2,128)(2,1)S(1)}, bf16[4,2,2048]{2,1,0:T(2,128)(2,1)S(1)}, u32[]{:S(2)}, u32[]{:S(2)}) collective-permute-start(bf16[4,2,2048]{2,1,0:T(2,128)(2,1)S(1)} %pad_maximum_fusion.14), channel_id=1, source_target_pairs={{0,8},{4,12},{8,16},{12,20},{16,24},{20,28},{24,0},{28,4},{1,9},{5... | collective-permute-start | bytes 98312 | tf_op jit(solution)/shard_map/ppermute | solution.py:29
  26.0 18.5 %collective-permute-start.4 = (bf16[4,2,2048]{2,1,0:T(2,128)(2,1)S(1)}, bf16[4,2,2048]{2,1,0:T(2,128)(2,1)S(1)}, u32[]{:S(2)}, u32[]{:S(2)}) collective-permute-start(bf16[4,2,2048]{2,1,0:T(2,128)(2,1)S(1)} %pad_maximum_fusion.14), channel_id=1, source_target_pairs={{0,16},{4,20},{8,24},{12,28},{16,0},{20,4},{24,8},{28,12},{1,17},{... | collective-permute-start | bytes 98312 | tf_op jit(solution)/shard_map/ppermute | solution.py:29
  28.6 15.9 %collective-permute-start.5 = (bf16[4,2,2048]{2,1,0:T(2,128)(2,1)S(1)}, bf16[4,2,2048]{2,1,0:T(2,128)(2,1)S(1)}, u32[]{:S(2)}, u32[]{:S(2)}) collective-permute-start(bf16[4,2,2048]{2,1,0:T(2,128)(2,1)S(1)} %pad_maximum_fusion.14), channel_id=1, source_target_pairs={{0,24},{4,28},{8,0},{12,4},{16,8},{20,12},{24,16},{28,20},{1,25},{... | collective-permute-start | bytes 98312 | tf_op jit(solution)/shard_map/ppermute | solution.py:29
  44.8 1.4 collective-permute-start.6
  48.0 27.0 %copy-start.3 = (bf16[1,256,768]{2,1,0:T(8,128)(2,1)S(1)}, bf16[1,256,768]{2,1,0:T(8,128)(2,1)}, u32[]{:S(2)}) copy-start(bf16[1,256,768]{2,1,0:T(8,128)(2,1)} %param.19) | copy-start | bytes 1179652
  48.3 26.7 %copy-start.4 = (bf16[1,256,768]{2,1,0:T(8,128)(2,1)S(1)}, bf16[1,256,768]{2,1,0:T(8,128)(2,1)}, u32[]{:S(2)}) copy-start(bf16[1,256,768]{2,1,0:T(8,128)(2,1)} %param.18) | copy-start | bytes 1179652
  48.9 3.7 %collective-permute-start.17 = (f32[4,128]{1,0:T(4,128)S(1)}, f32[4,128]{1,0:T(4,128)S(1)}, u32[]{:S(2)}, u32[]{:S(2)}) collective-permute-start(f32[4,128]{1,0:T(4,128)S(1)} %bitcast.200), channel_id=1, source_target_pairs={{0,1},{1,0},{2,3},{3,2},{4,5},{5,4},{6,7},{7,6},{8,9},{9,8},{10,11... | collective-permute-start | bytes 6152 | tf_op jit(solution)/shard_map/ppermute | solution.py:52
  50.5 3.6 %collective-permute-start.18 = (f32[4,128]{1,0:T(4,128)S(1)}, f32[4,128]{1,0:T(4,128)S(1)}, u32[]{:S(2)}, u32[]{:S(2)}) collective-permute-start(f32[4,128]{1,0:T(4,128)S(1)} %bitcast.201), channel_id=1, source_target_pairs={{0,2},{1,3},{2,0},{3,1},{4,6},{5,7},{6,4},{7,5},{8,10},{9,11},{10,... | collective-permute-start | bytes 6152 | tf_op jit(solution)/shard_map/ppermute | solution.py:52
  52.0 4.5 %collective-permute-start.19 = (f32[4,128]{1,0:T(4,128)S(1)}, f32[4,128]{1,0:T(4,128)S(1)}, u32[]{:S(2)}, u32[]{:S(2)}) collective-permute-start(f32[4,128]{1,0:T(4,128)S(1)} %bitcast.202), channel_id=1, source_target_pairs={{0,3},{1,2},{2,1},{3,0},{4,7},{5,6},{6,5},{7,4},{8,11},{9,10},{10,... | collective-permute-start | bytes 6152 | tf_op jit(solution)/shard_map/ppermute | solution.py:52
  52.6 14.0 %collective-permute-start.21 = (bf16[768,256]{1,0:T(8,128)(2,1)}, bf16[768,256]{1,0:T(8,128)(2,1)S(1)}, u32[]{:S(2)}, u32[]{:S(2)}) collective-permute-start(bf16[768,256]{1,0:T(8,128)(2,1)} %bitcast.178), channel_id=1, source_target_pairs={{0,8},{4,12},{8,16},{12,20},{16,24},{20,28},{24,0},{28,4},{1,9},{5... | collective-permute-start | bytes 1179656 | tf_op jit(solution)/shard_map/ppermute | solution.py:29
  54.1 12.6 %collective-permute-start.20 = (bf16[768,256]{1,0:T(8,128)(2,1)}, bf16[768,256]{1,0:T(8,128)(2,1)S(1)}, u32[]{:S(2)}, u32[]{:S(2)}) collective-permute-start(bf16[768,256]{1,0:T(8,128)(2,1)} %bitcast.179), channel_id=1, source_target_pairs={{0,4},{4,0},{8,12},{12,8},{16,20},{20,16},{24,28},{28,24},{1,5},{5... | collective-permute-start | bytes 1179656 | tf_op jit(solution)/shard_map/ppermute | solution.py:42
  56.5 16.9 %collective-permute-start.23 = (bf16[768,256]{1,0:T(8,128)(2,1)}, bf16[768,256]{1,0:T(8,128)(2,1)S(1)}, u32[]{:S(2)}, u32[]{:S(2)}) collective-permute-start(bf16[768,256]{1,0:T(8,128)(2,1)} %bitcast.180), channel_id=1, source_target_pairs={{0,24},{4,28},{8,0},{12,4},{16,8},{20,12},{24,16},{28,20},{1,25},{... | collective-permute-start | bytes 1179656 | tf_op jit(solution)/shard_map/ppermute | solution.py:29
  66.6 11.7 %collective-permute-start.10 = (bf16[256,1536]{1,0:T(8,128)(2,1)}, bf16[256,1536]{1,0:T(8,128)(2,1)S(1)}, u32[]{:S(2)}, u32[]{:S(2)}) collective-permute-start(bf16[256,1536]{1,0:T(8,128)(2,1)} %pad_maximum_fusion.6), channel_id=1, source_target_pairs={{0,4},{4,0},{8,12},{12,8},{16,20},{20,16},{24,28},{28,24},{1,5},{5... | collective-permute-start | bytes 2359304 | tf_op jit(solution)/shard_map/ppermute | solution.py:42
  66.6 10.9 %collective-permute-start.22 = (bf16[768,256]{1,0:T(8,128)(2,1)S(1)}, bf16[768,256]{1,0:T(8,128)(2,1)S(1)}, u32[]{:S(2)}, u32[]{:S(2)}) collective-permute-start(bf16[768,256]{1,0:T(8,128)(2,1)S(1)} %collective-permute-done.21), channel_id=1, source_target_pairs={{0,4},{4,0},{8,12},{12,8},{16,20},{20,16},{24,28},{28,24},{1,5},{5... | collective-permute-start | bytes 1179656 | tf_op jit(solution)/shard_map/ppermute | solution.py:42
  73.4 6.2 %collective-permute-start.24 = (bf16[768,256]{1,0:T(8,128)(2,1)S(1)}, bf16[768,256]{1,0:T(8,128)(2,1)S(1)}, u32[]{:S(2)}, u32[]{:S(2)}) collective-permute-start(bf16[768,256]{1,0:T(8,128)(2,1)S(1)} %collective-permute-done.23), channel_id=1, source_target_pairs={{0,4},{4,0},{8,12},{12,8},{16,20},{20,16},{24,28},{28,24},{1,5},{5... | collective-permute-start | bytes 1179656 | tf_op jit(solution)/shard_map/ppermute | solution.py:42
  75.4 30.1 %collective-permute-start.15 = (bf16[256,1536]{1,0:T(8,128)(2,1)S(1)}, bf16[256,1536]{1,0:T(8,128)(2,1)S(1)}, u32[]{:S(2)}, u32[]{:S(2)}) collective-permute-start(bf16[256,1536]{1,0:T(8,128)(2,1)S(1)} %get-tuple-element.50), channel_id=1, source_target_pairs={{0,16},{4,20},{8,0},{12,4},{16,24},{20,28},{24,8},{28,12},{1,17},{... | collective-permute-start | bytes 2359304 | tf_op jit(solution)/shard_map/ppermute | solution.py:35
  77.3 28.1 %collective-permute-start.12 = (bf16[256,1536]{1,0:T(8,128)(2,1)}, bf16[256,1536]{1,0:T(8,128)(2,1)S(1)}, u32[]{:S(2)}, u32[]{:S(2)}) collective-permute-start(bf16[256,1536]{1,0:T(8,128)(2,1)} %collective-permute-done.11), channel_id=1, source_target_pairs={{0,4},{4,0},{8,12},{12,8},{16,20},{20,16},{24,28},{28,24},{1,5},{5... | collective-permute-start | bytes 2359304 | tf_op jit(solution)/shard_map/ppermute | solution.py:42
  77.7 26.0 %collective-permute-start.28 = (bf16[768,256]{1,0:T(8,128)(2,1)S(1)}, bf16[768,256]{1,0:T(8,128)(2,1)S(1)}, u32[]{:S(2)}, u32[]{:S(2)}) collective-permute-start(bf16[768,256]{1,0:T(8,128)(2,1)S(1)} %get-tuple-element.58), channel_id=1, source_target_pairs={{0,16},{4,20},{8,0},{12,4},{16,24},{20,28},{24,8},{28,12},{1,17},{... | collective-permute-start | bytes 1179656 | tf_op jit(solution)/shard_map/ppermute | solution.py:35
  78.3 27.7 %collective-permute-start.14 = (bf16[256,1536]{1,0:T(8,128)(2,1)S(1)}, bf16[256,1536]{1,0:T(8,128)(2,1)S(1)}, u32[]{:S(2)}, u32[]{:S(2)}) collective-permute-start(bf16[256,1536]{1,0:T(8,128)(2,1)S(1)} %collective-permute-done.13), channel_id=1, source_target_pairs={{0,4},{4,0},{8,12},{12,8},{16,20},{20,16},{24,28},{28,24},{1,5},{5... | collective-permute-start | bytes 2359304 | tf_op jit(solution)/shard_map/ppermute | solution.py:42
  79.6 28.7 %collective-permute-start.7 = (bf16[128,2048]{1,0:T(8,128)(2,1)S(1)}, bf16[128,2048]{1,0:T(8,128)(2,1)S(1)}, u32[]{:S(2)}, u32[]{:S(2)}) collective-permute-start(bf16[128,2048]{1,0:T(8,128)(2,1)S(1)} %multiply_convert_fusion.6), channel_id=1, source_target_pairs={{0,1},{1,0},{2,3},{3,2},{4,5},{5,4},{6,7},{7,6},{8,9},{9,8},{10,11... | collective-permute-start | bytes 1572872 | tf_op jit(solution)/shard_map/ppermute | solution.py:52
  81.2 53.0 %copy-start.26 = (bf16[768,1536]{1,0:T(8,128)(2,1)}, bf16[768,1536]{1,0:T(8,128)(2,1)S(1)}, u32[]{:S(2)}) copy-start(bf16[768,1536]{1,0:T(8,128)(2,1)S(1)} %constant_dynamic-update-slice_fusion.32) | copy-start | bytes 7077892
  103.8 24.7 %collective-permute-start.8 = (bf16[128,2048]{1,0:T(8,128)(2,1)S(1)}, bf16[128,2048]{1,0:T(8,128)(2,1)S(1)}, u32[]{:S(2)}, u32[]{:S(2)}) collective-permute-start(bf16[128,2048]{1,0:T(8,128)(2,1)S(1)} %multiply_convert_fusion.6), channel_id=1, source_target_pairs={{0,2},{1,3},{2,0},{3,1},{4,6},{5,7},{6,4},{7,5},{8,10},{9,11},{10,... | collective-permute-start | bytes 1572872 | tf_op jit(solution)/shard_map/ppermute | solution.py:52
  105.3 2.3 collective-permute-start.29
  105.4 2.8 collective-permute-start.16
  106.0 22.4 %collective-permute-start.9 = (bf16[128,2048]{1,0:T(8,128)(2,1)S(1)}, bf16[128,2048]{1,0:T(8,128)(2,1)S(1)}, u32[]{:S(2)}, u32[]{:S(2)}) collective-permute-start(bf16[128,2048]{1,0:T(8,128)(2,1)S(1)} %multiply_convert_fusion.6), channel_id=1, source_target_pairs={{0,3},{1,2},{2,1},{3,0},{4,7},{5,6},{6,5},{7,4},{8,11},{9,10},{10,... | collective-permute-start | bytes 1572872 | tf_op jit(solution)/shard_map/ppermute | solution.py:52
  107.6 27.9 %copy-start.23 = (bf16[768,512]{1,0:T(8,128)(2,1)}, bf16[768,512]{1,0:T(8,128)(2,1)S(1)}, u32[]{:S(2)}) copy-start(bf16[768,512]{1,0:T(8,128)(2,1)S(1)} %constant_dynamic-update-slice_fusion.38) | copy-start | bytes 2359300
  108.3 36.8 %copy-start.15 = (bf16[128,2048]{1,0:T(8,128)(2,1)}, bf16[128,2048]{1,0:T(8,128)(2,1)S(1)}, u32[]{:S(2)}) copy-start(bf16[128,2048]{1,0:T(8,128)(2,1)S(1)} %collective-permute-done.7) | copy-start | bytes 1572868
  128.5 16.6 %copy-start.17 = (bf16[128,2048]{1,0:T(8,128)(2,1)}, bf16[128,2048]{1,0:T(8,128)(2,1)S(1)}, u32[]{:S(2)}) copy-start(bf16[128,2048]{1,0:T(8,128)(2,1)S(1)} %collective-permute-done.8) | copy-start | bytes 1572868
  135.6 27.3 %copy-start.1 = (bf16[512,1536]{1,0:T(8,128)(2,1)}, bf16[512,1536]{1,0:T(8,128)(2,1)S(1)}, u32[]{:S(2)}) copy-start(bf16[512,1536]{1,0:T(8,128)(2,1)S(1)} %convolution_convert_fusion.3) | copy-start | bytes 4718596
  136.2 25.6 %copy-start.12 = (bf16[512,512]{1,0:T(8,128)(2,1)}, bf16[512,512]{1,0:T(8,128)(2,1)S(1)}, u32[]{:S(2)}) copy-start(bf16[512,512]{1,0:T(8,128)(2,1)S(1)} %convolution_convert_fusion.5) | copy-start | bytes 1572868
  136.2 6.7 %collective-permute-start.30 = (bf16[128,512]{1,0:T(8,128)(2,1)S(1)}, bf16[128,512]{1,0:T(8,128)(2,1)S(1)}, u32[]{:S(2)}, u32[]{:S(2)}) collective-permute-start(bf16[128,512]{1,0:T(8,128)(2,1)S(1)} %get-tuple-element.56), channel_id=1, source_target_pairs={{0,1},{1,0},{2,3},{3,2},{4,5},{5,4},{6,7},{7,6},{8,9},{9,8},{10,11... | collective-permute-start | bytes 393224 | tf_op jit(solution)/shard_map/ppermute | solution.py:52
  137.9 24.1 %collective-permute-start.25 = (bf16[128,1536]{1,0:T(8,128)(2,1)S(1)}, bf16[128,1536]{1,0:T(8,128)(2,1)S(1)}, u32[]{:S(2)}, u32[]{:S(2)}) collective-permute-start(bf16[128,1536]{1,0:T(8,128)(2,1)S(1)} %get-tuple-element.47), channel_id=1, source_target_pairs={{0,1},{1,0},{2,3},{3,2},{4,5},{5,4},{6,7},{7,6},{8,9},{9,8},{10,11... | collective-permute-start | bytes 1179656 | tf_op jit(solution)/shard_map/ppermute | solution.py:52
  138.5 23.5 %collective-permute-start.26 = (bf16[128,1536]{1,0:T(8,128)(2,1)S(1)}, bf16[128,1536]{1,0:T(8,128)(2,1)S(1)}, u32[]{:S(2)}, u32[]{:S(2)}) collective-permute-start(bf16[128,1536]{1,0:T(8,128)(2,1)S(1)} %get-tuple-element.46), channel_id=1, source_target_pairs={{0,2},{1,3},{2,0},{3,1},{4,6},{5,7},{6,4},{7,5},{8,10},{9,11},{10,... | collective-permute-start | bytes 1179656 | tf_op jit(solution)/shard_map/ppermute | solution.py:52
  140.0 22.0 %collective-permute-start.27 = (bf16[128,1536]{1,0:T(8,128)(2,1)S(1)}, bf16[128,1536]{1,0:T(8,128)(2,1)S(1)}, u32[]{:S(2)}, u32[]{:S(2)}) collective-permute-start(bf16[128,1536]{1,0:T(8,128)(2,1)S(1)} %get-tuple-element.45), channel_id=1, source_target_pairs={{0,3},{1,2},{2,1},{3,0},{4,7},{5,6},{6,5},{7,4},{8,11},{9,10},{10,... | collective-permute-start | bytes 1179656 | tf_op jit(solution)/shard_map/ppermute | solution.py:52
  141.4 20.3 %collective-permute-start.31 = (bf16[128,512]{1,0:T(8,128)(2,1)S(1)}, bf16[128,512]{1,0:T(8,128)(2,1)S(1)}, u32[]{:S(2)}, u32[]{:S(2)}) collective-permute-start(bf16[128,512]{1,0:T(8,128)(2,1)S(1)} %get-tuple-element.55), channel_id=1, source_target_pairs={{0,2},{1,3},{2,0},{3,1},{4,6},{5,7},{6,4},{7,5},{8,10},{9,11},{10,... | collective-permute-start | bytes 393224 | tf_op jit(solution)/shard_map/ppermute | solution.py:52
  143.0 18.8 %collective-permute-start.32 = (bf16[128,512]{1,0:T(8,128)(2,1)S(1)}, bf16[128,512]{1,0:T(8,128)(2,1)S(1)}, u32[]{:S(2)}, u32[]{:S(2)}) collective-permute-start(bf16[128,512]{1,0:T(8,128)(2,1)S(1)} %get-tuple-element.54), channel_id=1, source_target_pairs={{0,3},{1,2},{2,1},{3,0},{4,7},{5,6},{6,5},{7,4},{8,11},{9,10},{10,... | collective-permute-start | bytes 393224 | tf_op jit(solution)/shard_map/ppermute | solution.py:52
  164.6 16.9 %copy-start.14 = (bf16[512,768]{1,0:T(8,128)(2,1)S(1)}, bf16[512,768]{1,0:T(8,128)(2,1)}, u32[]{:S(2)}) copy-start(bf16[512,768]{1,0:T(8,128)(2,1)} %get-tuple-element.12) | copy-start | bytes 2359300
  164.6 15.0 %collective-permute-start.36 = (bf16[128,512]{1,0:T(8,128)(2,1)S(1)}, bf16[128,512]{1,0:T(8,128)(2,1)S(1)}, u32[]{:S(2)}, u32[]{:S(2)}) collective-permute-start(bf16[128,512]{1,0:T(8,128)(2,1)S(1)} %slice.207), channel_id=1, source_target_pairs={{0,1},{1,0},{2,3},{3,2},{4,5},{5,4},{6,7},{7,6},{8,9},{9,8},{10,11... | collective-permute-start | bytes 393224 | tf_op jit(solution)/shard_map/ppermute | solution.py:52
  166.2 13.9 %collective-permute-start.37 = (bf16[128,512]{1,0:T(8,128)(2,1)S(1)}, bf16[128,512]{1,0:T(8,128)(2,1)S(1)}, u32[]{:S(2)}, u32[]{:S(2)}) collective-permute-start(bf16[128,512]{1,0:T(8,128)(2,1)S(1)} %slice.207), channel_id=1, source_target_pairs={{0,2},{1,3},{2,0},{3,1},{4,6},{5,7},{6,4},{7,5},{8,10},{9,11},{10,... | collective-permute-start | bytes 393224 | tf_op jit(solution)/shard_map/ppermute | solution.py:52
  167.7 13.8 %collective-permute-start.38 = (bf16[128,512]{1,0:T(8,128)(2,1)S(1)}, bf16[128,512]{1,0:T(8,128)(2,1)S(1)}, u32[]{:S(2)}, u32[]{:S(2)}) collective-permute-start(bf16[128,512]{1,0:T(8,128)(2,1)S(1)} %slice.207), channel_id=1, source_target_pairs={{0,3},{1,2},{2,1},{3,0},{4,7},{5,6},{6,5},{7,4},{8,11},{9,10},{10,... | collective-permute-start | bytes 393224 | tf_op jit(solution)/shard_map/ppermute | solution.py:52
  168.2 20.2 %copy-start.21 = (bf16[128,1536]{1,0:T(8,128)(2,1)}, bf16[128,1536]{1,0:T(8,128)(2,1)S(1)}, u32[]{:S(2)}) copy-start(bf16[128,1536]{1,0:T(8,128)(2,1)S(1)} %slice.206) | copy-start | bytes 1179652
  168.2 16.6 %collective-permute-start.33 = (bf16[128,1536]{1,0:T(8,128)(2,1)S(1)}, bf16[128,1536]{1,0:T(8,128)(2,1)S(1)}, u32[]{:S(2)}, u32[]{:S(2)}) collective-permute-start(bf16[128,1536]{1,0:T(8,128)(2,1)S(1)} %slice.206), channel_id=1, source_target_pairs={{0,1},{1,0},{2,3},{3,2},{4,5},{5,4},{6,7},{7,6},{8,9},{9,8},{10,11... | collective-permute-start | bytes 1179656 | tf_op jit(solution)/shard_map/ppermute | solution.py:52
  169.8 15.1 %collective-permute-start.34 = (bf16[128,1536]{1,0:T(8,128)(2,1)S(1)}, bf16[128,1536]{1,0:T(8,128)(2,1)S(1)}, u32[]{:S(2)}, u32[]{:S(2)}) collective-permute-start(bf16[128,1536]{1,0:T(8,128)(2,1)S(1)} %slice.206), channel_id=1, source_target_pairs={{0,2},{1,3},{2,0},{3,1},{4,6},{5,7},{6,4},{7,5},{8,10},{9,11},{10,... | collective-permute-start | bytes 1179656 | tf_op jit(solution)/shard_map/ppermute | solution.py:52
  179.6 8.8 %collective-permute-start.35 = (bf16[128,1536]{1,0:T(8,128)(2,1)S(1)}, bf16[128,1536]{1,0:T(8,128)(2,1)S(1)}, u32[]{:S(2)}, u32[]{:S(2)}) collective-permute-start(bf16[128,1536]{1,0:T(8,128)(2,1)S(1)} %slice.206), channel_id=1, source_target_pairs={{0,3},{1,2},{2,1},{3,0},{4,7},{5,6},{6,5},{7,4},{8,11},{9,10},{10,... | collective-permute-start | bytes 1179656 | tf_op jit(solution)/shard_map/ppermute | solution.py:52
  180.1 26.4 %collective-permute-start.49 = (f32[4,2048]{1,0:T(4,128)}, f32[4,2048]{1,0:T(4,128)}, u32[]{:S(2)}, u32[]{:S(2)}) collective-permute-start(f32[4,2048]{1,0:T(4,128)} %constant_dynamic-update-slice_fusion.56), channel_id=1, source_target_pairs={{0,1},{1,0},{2,3},{3,2},{4,5},{5,4},{6,7},{7,6},{8,9},{9,8},{10,11... | collective-permute-start | bytes 98312 | tf_op jit(solution)/shard_map/ppermute | solution.py:52
  191.8 33.4 %collective-permute-start.44 = (bf16[3,256,768]{1,2,0:T(8,128)(2,1)}, bf16[3,256,768]{1,2,0:T(8,128)(2,1)}, u32[]{:S(2)}, u32[]{:S(2)}) collective-permute-start(bf16[3,256,768]{1,2,0:T(8,128)(2,1)} %bitcast.183), channel_id=1, source_target_pairs={{0,4},{4,0},{8,12},{12,8},{16,20},{20,16},{24,28},{28,24},{1,5},{5... | collective-permute-start | bytes 3538952 | tf_op jit(solution)/shard_map/ppermute | solution.py:42
  202.3 24.4 %collective-permute-start.39 = (bf16[3,256,1536]{2,1,0:T(8,128)(2,1)}, bf16[3,256,1536]{2,1,0:T(8,128)(2,1)}, u32[]{:S(2)}, u32[]{:S(2)}) collective-permute-start(bf16[3,256,1536]{2,1,0:T(8,128)(2,1)} %slice_bitcast_fusion), channel_id=1, source_target_pairs={{0,4},{4,0},{8,12},{12,8},{16,20},{20,16},{24,28},{28,24},{1,5},{5... | collective-permute-start | bytes 7077896 | tf_op jit(solution)/shard_map/ppermute | solution.py:42
  204.9 17.3 %collective-permute-start.40 = (bf16[1,256,1536]{2,1,0:T(8,128)(2,1)S(1)}, bf16[1,256,1536]{2,1,0:T(8,128)(2,1)}, u32[]{:S(2)}, u32[]{:S(2)}) collective-permute-start(bf16[1,256,1536]{2,1,0:T(8,128)(2,1)S(1)} %slice_bitcast_fusion.6), channel_id=1, source_target_pairs={{0,4},{4,0},{8,12},{12,8},{16,20},{20,16},{24,28},{28,24},{1,5},{5... | collective-permute-start | bytes 2359304 | tf_op jit(solution)/shard_map/ppermute | solution.py:42
  206.1 14.7 %collective-permute-start.45 = (bf16[1,256,768]{1,2,0:T(8,128)(2,1)}, bf16[1,256,768]{1,2,0:T(8,128)(2,1)}, u32[]{:S(2)}, u32[]{:S(2)}) collective-permute-start(bf16[1,256,768]{1,2,0:T(8,128)(2,1)} %bitcast.50), channel_id=1, source_target_pairs={{0,4},{4,0},{8,12},{12,8},{16,20},{20,16},{24,28},{28,24},{1,5},{5... | collective-permute-start | bytes 1179656 | tf_op jit(solution)/shard_map/ppermute | solution.py:42
  207.2 4.0 %collective-permute-start.50 = (f32[4,2048]{1,0:T(4,128)S(1)}, f32[4,2048]{1,0:T(4,128)S(1)}, u32[]{:S(2)}, u32[]{:S(2)}) collective-permute-start(f32[4,2048]{1,0:T(4,128)S(1)} %add.500), channel_id=1, source_target_pairs={{0,2},{1,3},{2,0},{3,1},{4,6},{5,7},{6,4},{7,5},{8,10},{9,11},{10,... | collective-permute-start | bytes 98312 | tf_op jit(solution)/shard_map/ppermute | solution.py:52
  211.2 1.3 collective-permute-start.51
  212.5 4.0 %collective-permute-start.52 = (f32[4,2048]{1,0:T(4,128)S(1)}, f32[4,2048]{1,0:T(4,128)S(1)}, u32[]{:S(2)}, u32[]{:S(2)}) collective-permute-start(f32[4,2048]{1,0:T(4,128)S(1)} %add.502), channel_id=1, source_target_pairs={{0,8},{4,12},{8,0},{12,4},{16,24},{20,28},{24,16},{28,20},{1,9},{5... | collective-permute-start | bytes 98312 | tf_op jit(solution)/shard_map/ppermute | solution.py:47
  217.1 38.2 %collective-permute-start.53 = (f32[4,2048]{1,0:T(4,128)}, f32[4,2048]{1,0:T(4,128)}, u32[]{:S(2)}, u32[]{:S(2)}) collective-permute-start(f32[4,2048]{1,0:T(4,128)} %add.503), channel_id=1, source_target_pairs={{0,16},{4,20},{8,24},{12,28},{16,0},{20,4},{24,8},{28,12},{1,17},{... | collective-permute-start | bytes 98312 | tf_op jit(solution)/shard_map/ppermute | solution.py:47
  221.9 30.1 %collective-permute-start.46 = (bf16[256,768]{0,1:T(8,128)(2,1)S(1)}, bf16[256,768]{0,1:T(8,128)(2,1)S(1)}, u32[]{:S(2)}, u32[]{:S(2)}) collective-permute-start(bf16[256,768]{0,1:T(8,128)(2,1)S(1)} %fusion.48), channel_id=1, source_target_pairs={{0,8},{4,12},{8,24},{12,28},{16,0},{20,4},{24,16},{28,20},{1,9},{5... | collective-permute-start | bytes 1179656 | tf_op jit(solution)/shard_map/ppermute | solution.py:35
  223.7 25.7 %collective-permute-start.41 = (bf16[256,1536]{1,0:T(8,128)(2,1)S(1)}, bf16[256,1536]{1,0:T(8,128)(2,1)S(1)}, u32[]{:S(2)}, u32[]{:S(2)}) collective-permute-start(bf16[256,1536]{1,0:T(8,128)(2,1)S(1)} %fusion.34), channel_id=1, source_target_pairs={{0,8},{4,12},{8,24},{12,28},{16,0},{20,4},{24,16},{28,20},{1,9},{5... | collective-permute-start | bytes 2359304 | tf_op jit(solution)/shard_map/ppermute | solution.py:35
  249.8 52.2 %collective-permute-start.42 = (bf16[256,1536]{1,0:T(8,128)(2,1)S(1)}, bf16[256,1536]{1,0:T(8,128)(2,1)S(1)}, u32[]{:S(2)}, u32[]{:S(2)}) collective-permute-start(bf16[256,1536]{1,0:T(8,128)(2,1)S(1)} %get-tuple-element.35), channel_id=1, source_target_pairs={{0,24},{4,28},{8,0},{12,4},{16,8},{20,12},{24,16},{28,20},{1,25},{... | collective-permute-start | bytes 2359304 | tf_op jit(solution)/shard_map/ppermute | solution.py:29
  251.3 50.8 %collective-permute-start.43 = (bf16[256,1536]{1,0:T(8,128)(2,1)S(1)}, bf16[256,1536]{1,0:T(8,128)(2,1)S(1)}, u32[]{:S(2)}, u32[]{:S(2)}) collective-permute-start(bf16[256,1536]{1,0:T(8,128)(2,1)S(1)} %get-tuple-element.36), channel_id=1, source_target_pairs={{0,8},{4,12},{8,16},{12,20},{16,24},{20,28},{24,0},{28,4},{1,9},{5... | collective-permute-start | bytes 2359304 | tf_op jit(solution)/shard_map/ppermute | solution.py:29
  252.1 42.8 %collective-permute-start.47 = (bf16[256,768]{0,1:T(8,128)(2,1)S(1)}, bf16[256,768]{0,1:T(8,128)(2,1)S(1)}, u32[]{:S(2)}, u32[]{:S(2)}) collective-permute-start(bf16[256,768]{0,1:T(8,128)(2,1)S(1)} %get-tuple-element.39), channel_id=1, source_target_pairs={{0,24},{4,28},{8,0},{12,4},{16,8},{20,12},{24,16},{28,20},{1,25},{... | collective-permute-start | bytes 1179656 | tf_op jit(solution)/shard_map/ppermute | solution.py:29
  255.4 45.6 %collective-permute-start.48 = (bf16[256,768]{0,1:T(8,128)(2,1)S(1)}, bf16[256,768]{0,1:T(8,128)(2,1)S(1)}, u32[]{:S(2)}, u32[]{:S(2)}) collective-permute-start(bf16[256,768]{0,1:T(8,128)(2,1)S(1)} %get-tuple-element.40), channel_id=1, source_target_pairs={{0,8},{4,12},{8,16},{12,20},{16,24},{20,28},{24,0},{28,4},{1,9},{5... | collective-permute-start | bytes 1179656 | tf_op jit(solution)/shard_map/ppermute | solution.py:29
  (26 other events, 120.0 us)
where the time goes:
time: 304 us
  waiting for transfers between devices  164 us (54%)
  starting transfers between devices  59.3 us (20%)
  matrix products  30 us (10%)
  other arithmetic  26.4 us (9%)
  local copies, waits for them, and re-layouts  22.5 us (7%)
    ppermute x11, waiting for transfers between devices, dp_shift(): lax.ppermute(value, 'dp', [(2 * z + c, 2 * ((z + step) % nz) + c) for z i...  72.8 us
    ppermute x23, waiting for transfers between devices, expert_xor(): return lax.ppermute(value, 'expert', [(i, i ^ mask) for i in range(size)])  44 us
    ppermute x4, waiting for transfers between devices, dp_pairs(): lax.ppermute(value, 'dp', [(2 * z + c, 2 * t + c) for z, t in enumerate(t...  42.3 us
    ppermute x23, starting transfers between devices, expert_xor(): return lax.ppermute(value, 'expert', [(i, i ^ mask) for i in range(size)])  30.5 us
    ppermute x11, starting transfers between devices, dp_shift(): lax.ppermute(value, 'dp', [(2 * z + c, 2 * ((z + step) % nz) + c) for z i...  17.8 us
    unnamed x123, local copies, waits for them, and re-layouts  11.2 us
    dot_general x4, matrix products, chip_terms(): lax.dot_general(left, right, contract_rows, preferred_element_type=jnp.fl...  6.98 us
  transfers between devices with their start and end apart: 54, of which 18 were waited for; matrix products, arithmetic and copies ran while one was open for 21% of the time, Pallas kernels for 0%

commit v1 on v0

--- a/solution.py
+++ b/solution.py
@@ -83,7 +83,6 @@
     user_count, hist_len, model_width = history.shape
     head_count = model_width // HEAD
     experts = w_router.shape[1]
-    hidden_width = w_gate.shape[2]
     dp_size = lax.axis_size("dp")
     ep_size = lax.axis_size("expert")
     nz = dp_size // 2
@@ -95,8 +94,9 @@
     row_total = user_count * CANDS
     slice_width = model_width // dp_size
     order = column_order(nz)
-    blocks = [(j, o) for j in order for o in range(2)]
+    blocks = [(j, o) for o in range(2) for j in order[:-1]] + [(order[-1], o) for o in range(2)]
     early = model_width - 2 * slice_width
+    half = early // 2
 
     def block_index(j, other):
         return ((z - j) % nz) * 2 + (core ^ other)
@@ -123,12 +123,12 @@
         payload = jnp.where(z == 1, slots[3], jnp.where(z == 2, slots[1], slots[0]))
         return {**slots, 2: dp_pairs(payload, RELAY_OUT)}
 
-    items = jnp.stack([pos_item] + [expert_xor(pos_item, k) for k in range(1, ep_size)])
-    items = jnp.stack([items] + [dp_shift(items, j) for j in range(1, nz)])
+    items = jnp.stack([pos_item] + [dp_shift(pos_item, j) for j in range(1, nz)])
+    items = jnp.stack([items] + [expert_xor(items, k) for k in range(1, ep_size)])
     items = jnp.stack([items, core_swap(items)]).reshape(-1, model_width)
 
-    gu_own = jnp.concatenate([w_gate[0], w_up[0]], axis=1)
-    gu_slots = relays(shifts(gu_own))
+    gate_slots = relays(shifts(w_gate[0]))
+    up_slots = relays(shifts(w_up[0]))
     down_slots = relays(shifts(w_down[0]))
 
     query_heads = user_query.reshape(user_count, head_count, HEAD)
@@ -147,7 +147,7 @@
 
     owner = neg_index // user_count
     owner_dp, owner_ep = owner // ep_size, owner % ep_size
-    slot = (((owner_dp % 2) ^ core) * nz + (z - owner_dp // 2) % nz) * ep_size + (owner_ep ^ me_ep)
+    slot = (((owner_dp % 2) ^ core) * ep_size + (owner_ep ^ me_ep)) * nz + (z - owner_dp // 2) % nz
     table = arrange(items, 1)
     negatives = table[slot * user_count + neg_index % user_count]
     candidates = jnp.concatenate([table[:user_count, None, :], negatives], axis=1)
@@ -157,7 +157,9 @@
     gain = arrange(out_gain, 0)
     query_f = arrange(user_query, 1).astype(jnp.float32)
     router = arrange(w_router, 0)
-    rows_in = jnp.concatenate([normed] + [expert_xor(normed, k) for k in range(1, ep_size)])
+    rows_in = lax.optimization_barrier(
+        jnp.concatenate([normed] + [expert_xor(normed, k) for k in range(1, ep_size)])
+    )
 
     logits = jnp.dot(normed, router, preferred_element_type=jnp.float32)
     route_hot = routes[:, :, None] == jnp.arange(experts, dtype=jnp.int32)
@@ -174,13 +176,18 @@
     ]
 
     def lay(slots, js, axis):
-        return jnp.concatenate(
-            [part for j in js for part in (slots[j], core_swap(slots[j]))], axis=axis
-        )
-
-    gu_full = lay(gu_slots, order, 0)
-    pre = jnp.dot(rows_in, gu_full, preferred_element_type=jnp.float32)
-    gate_pre, up_pre = pre[:, :hidden_width], pre[:, hidden_width:]
+        return jnp.concatenate([slots[j] for j in js] + [core_swap(slots[j]) for j in js], axis=axis)
+
+    def lay_all(slots):
+        return jnp.concatenate([lay(slots, order[:-1], 0), lay(slots, order[-1:], 0)])
+
+    gate_slots[0], up_slots[0], down_slots[0], _ = lax.optimization_barrier(
+        (gate_slots[0], up_slots[0], down_slots[0], normed)
+    )
+    gate_full = lay_all(gate_slots)
+    up_full = lay_all(up_slots)
+    gate_pre = jnp.dot(rows_in, gate_full, preferred_element_type=jnp.float32)
+    up_pre = jnp.dot(rows_in, up_full, preferred_element_type=jnp.float32)
     silu_val, silu_grad = silu_pair(gate_pre)
     hidden = (silu_val * up_pre).astype(jnp.bfloat16)
     hidden_mix = (mix_here * hidden.astype(jnp.float32)).astype(jnp.bfloat16)
@@ -227,45 +234,53 @@
     contract_rows = (((0,), (0,)), ((), ()))
     contract_cols = (((1,), (1,)), ((), ()))
 
-    def chip_terms(left, right):
-        part = lax.dot_general(left, right, contract_rows, preferred_element_type=jnp.float32)
-        part = part.astype(jnp.bfloat16).reshape(-1, 2, slice_width, right.shape[1])
-        return add_up(part[:, 0], core_swap(part[:, 1])).astype(jnp.bfloat16)
+    def chip_terms(mine, other, right):
+        part = lax.dot_general(other, right, contract_rows, preferred_element_type=jnp.float32)
+        got = core_swap(part.astype(jnp.bfloat16))
+        part = lax.dot_general(mine, right, contract_rows, preferred_element_type=jnp.float32)
+        return (part + got.astype(jnp.float32)).astype(jnp.bfloat16)
 
     def send_relay(term):
         return dp_pairs(term, RELAY_BACK) if relay else None
 
     def send_rest(terms, last, relayed):
-        by_chip = {j: terms[i] for i, j in enumerate(order[:-1])}
+        by_chip = {
+            j: terms[i * slice_width : (i + 1) * slice_width] for i, j in enumerate(order[:-1])
+        }
         if not relay:
             by_chip[order[-1]] = last
             moved = [dp_shift(by_chip[j], nz - j) for j in range(1, nz)]
-            return add_up(by_chip[0], *moved)
+            return lambda: add_up(by_chip[0], *moved)
         zero = jnp.zeros_like(relayed)
         down = add_up(by_chip[1], jnp.where(z == 2, relayed, zero)).astype(jnp.bfloat16)
         up = add_up(by_chip[3], jnp.where(z == 1, relayed, zero)).astype(jnp.bfloat16)
-        own = jnp.where((z == 0) | (z == 3), relayed, zero)
         moved = dp_shift(down, 3), dp_shift(up, 1)
-        return add_up(by_chip[0], own, *moved)
-
-    last_down = chip_terms(d_b, hidden_mix)[0]
+        return lambda: add_up(
+            by_chip[0], jnp.where((z == 0) | (z == 3), relayed, zero), *moved
+        )
+
+    last_down = chip_terms(d_b[:, :slice_width], d_b[:, slice_width:], hidden_mix)
     relay_down = send_relay(last_down)
-    terms_down = chip_terms(d_a, hidden_mix)
+    terms_down = chip_terms(d_a[:, :half], d_a[:, half:], hidden_mix)
+    sum_down = send_rest(terms_down, last_down, relay_down)
     d_hidden = lax.dot_general(
         d_a, down_a, contract_cols, preferred_element_type=jnp.float32
     ) + lax.dot_general(d_b, down_b, contract_cols, preferred_element_type=jnp.float32)
-    d_pre = jnp.concatenate(
-        [
-            (d_hidden * gate_slope.astype(jnp.float32)).astype(jnp.bfloat16),
-            (d_hidden * up_slope.astype(jnp.float32)).astype(jnp.bfloat16),
-        ],
-        axis=1,
-    )
-    last_gu = chip_terms(rows_in[:, early:], d_pre)[0]
-    relay_gu = send_relay(last_gu)
-    sum_down = send_rest(terms_down, last_down, relay_down)
-    terms_gu = chip_terms(rows_in[:, :early], d_pre)
-    sum_gu = send_rest(terms_gu, last_gu, relay_gu)
+    d_gate = (d_hidden * gate_slope.astype(jnp.float32)).astype(jnp.bfloat16)
+    d_up = (d_hidden * up_slope.astype(jnp.float32)).astype(jnp.bfloat16)
+    mine_b = rows_in[:, early : early + slice_width]
+    other_b = rows_in[:, early + slice_width :]
+    last_gate = chip_terms(mine_b, other_b, d_gate)
+    relay_gate = send_relay(last_gate)
+    last_up = chip_terms(mine_b, other_b, d_up)
+    relay_up = send_relay(last_up)
+    terms_gate = chip_terms(rows_in[:, :half], rows_in[:, half:early], d_gate)
+    terms_up = chip_terms(rows_in[:, :half], rows_in[:, half:early], d_up)
+    sum_gate = send_rest(terms_gate, last_gate, relay_gate)
+    sum_up = send_rest(terms_up, last_up, relay_up)
+    sum_down = sum_down().T[None]
+    sum_gate = sum_gate()[None]
+    sum_up = sum_up()[None]
 
     d_dense = jnp.zeros((row_total, experts), jnp.float32)
     lanes = jnp.arange(experts, dtype=jnp.int32)[None, :]
@@ -287,19 +302,20 @@
             block_index(j, o) * slice_width,
             1,
         )
+    router_term = router_term + dp_xor(router_term, 1)
+    mask = 2
+    while mask < dp_size:
+        router_term = router_term + dp_xor(router_term, mask)
+        mask *= 2
     mask = 1
     while mask < ep_size:
         router_term = router_term + expert_xor(router_term, mask)
         mask *= 2
-    mask = 1
-    while mask < dp_size:
-        router_term = router_term + dp_xor(router_term, mask)
-        mask *= 2
     return (
         losses,
-        sum_gu[:, :hidden_width][None],
-        sum_gu[:, hidden_width:][None],
-        sum_down.T[None],
+        sum_gate,
+        sum_up,
+        sum_down,
         router_term.T,
     )
 

time: 304 us -> 286 us (0.941)
  waiting for transfers between devices: 164 us -> 150 us
  local copies, waits for them, and re-layouts: 22.5 us -> 11.7 us
  starting transfers between devices: 59.3 us -> 68.4 us
    ppermute x4 -> x6, waiting for transfers between devices: 42.3 us -> 26.3 us  [dp_pairs(): lax.ppermute(value, 'dp', [(2 * z + c, 2 * t + c) for z, t in enumerate(t...]
    ppermute x11 -> x15, starting transfers between devices: 17.8 us -> 31.6 us  [dp_shift(): lax.ppermute(value, 'dp', [(2 * z + c, 2 * ((z + step) % nz) + c) for z i...]
    ppermute x11 -> x15, waiting for transfers between devices: 72.8 us -> 62.2 us  [dp_shift(): lax.ppermute(value, 'dp', [(2 * z + c, 2 * ((z + step) % nz) + c) for z i...]
    unnamed x123 -> x138, local copies, waits for them, and re-layouts: 11.2 us -> 4.32 us
    convert_element_type x3 -> x0, other arithmetic: 6.84 us -> none  [the longest x2 4.54 us: chip_terms(): return add_up(part[:, 0], core_swap(part[:, 1])).astype(jnp.bfloat16)]
    ppermute x23, waiting for transfers between devices: 44 us -> 50.3 us  [expert_xor(): return lax.ppermute(value, 'expert', [(i, i ^ mask) for i in range(size)])]
    dynamic_update_slice x8, local copies, waits for them, and re-layouts: 4.74 us -> 0.1 us  [local(): lax.dynamic_update_slice_in_dim(router_term, arranged[:, i * slice_width:...]
    ppermute x23, starting transfers between devices: 30.5 us -> 26.1 us  [expert_xor(): return lax.ppermute(value, 'expert', [(i, i ^ mask) for i in range(size)])]
  transfers between devices with their start and end apart: 54 -> 66, of which waited for: 18 -> 29; matrix products, arithmetic and copies ran while one was open for 21% -> 18% of each run, Pallas kernels for 0% -> 0%
where the time goes in v1:
time: 286 us
  waiting for transfers between devices  150 us (52%)
  starting transfers between devices  68.4 us (24%)
  matrix products  29.6 us (10%)
  other arithmetic  24.2 us (8%)
  local copies, waits for them, and re-layouts  11.7 us (4%)
    ppermute x15, waiting for transfers between devices, dp_shift(): lax.ppermute(value, 'dp', [(2 * z + c, 2 * ((z + step) % nz) + c) for z i...  62.2 us
    ppermute x23, waiting for transfers between devices, expert_xor(): return lax.ppermute(value, 'expert', [(i, i ^ mask) for i in range(size)])  50.3 us
    ppermute x15, starting transfers between devices, dp_shift(): lax.ppermute(value, 'dp', [(2 * z + c, 2 * ((z + step) % nz) + c) for z i...  31.6 us
    ppermute x6, waiting for transfers between devices, dp_pairs(): lax.ppermute(value, 'dp', [(2 * z + c, 2 * t + c) for z, t in enumerate(t...  26.3 us
    ppermute x23, starting transfers between devices, expert_xor(): return lax.ppermute(value, 'expert', [(i, i ^ mask) for i in range(size)])  26.1 us
    ppermute x19, waiting for transfers between devices, core_swap(): return lax.ppermute(value, 'dp', [(i, i ^ 1) for i in range(size)])  5.78 us
    ppermute x6, starting transfers between devices, dp_pairs(): lax.ppermute(value, 'dp', [(2 * z + c, 2 * t + c) for z, t in enumerate(t...  5.73 us
  transfers between devices with their start and end apart: 66, of which 29 were waited for; matrix products, arithmetic and copies ran while one was open for 18% of the time, Pallas kernels for 0%

profile of v1, /device:TPU:0, one launch (start us, length us, event | category | flops | bytes accessed | tf_op | source)
XLA Modules:
  0.0 285.7 jit_solution(3036918944393965009)
XLA Ops:
  0.6 3.1 %collective-permute-start = (bf16[2,2048]{1,0:T(2,128)(2,1)}, bf16[2,2048]{1,0:T(2,128)(2,1)S(1)}, u32[]{:S(2)}, u32[]{:S(2)}) collective-permute-start(bf16[2,2048]{1,0:T(2,128)(2,1)} %param.14), channel_id=1, source_target_pairs={{0,8},{4,12},{8,16},{12,20},{16,24},{20,28},{24,0},{28,4},{1,9},{5... | collective-permute-start | bytes 24584 | tf_op jit(solution)/shard_map/ppermute | solution.py:29
  3.7 2.6 collective-permute-start.1
  6.3 1.3 collective-permute-start.2
  8.4 3.1 %collective-permute-start.28 = (bf16[768,256]{1,0:T(8,128)(2,1)}, bf16[768,256]{1,0:T(8,128)(2,1)S(1)}, u32[]{:S(2)}, u32[]{:S(2)}) collective-permute-start(bf16[768,256]{1,0:T(8,128)(2,1)} %bitcast.130), channel_id=1, source_target_pairs={{0,24},{4,28},{8,0},{12,4},{16,8},{20,12},{24,16},{28,20},{1,25},{... | collective-permute-start | bytes 1179656 | tf_op jit(solution)/shard_map/ppermute | solution.py:29
  12.9 5.6 %fusion.2 = f32[2,16,1,1024]{3,2,1,0:T(1,128)S(1)} fusion(bf16[2,16,128,1]{2,3,1,0:T(2,128)(2,1)S(1)} %reshape.366, bf16[2,1024,2048]{2,1,0:T(8,128)(2,1)} %param.11), kind=kOutput, calls=%fused_computation.3 | convolution fusion | flops 8388608 | bytes 8527872 | tf_op jit(solution)/shard_map/uhd,uthd->uht/dot_general | solution.py:136
  18.9 5.1 %fusion.4 = f32[2,16,1,128]{3,2,1,0:T(1,128)S(1)} fusion(bf16[2,16,1024,1]{2,1,0,3:T(8,128)(2,1)S(1)} %fusion.17, bf16[2,1024,2048]{2,1,0:T(8,128)(2,1)} %param.11), kind=kOutput, calls=%fused_computation.5 | convolution fusion | flops 8388608 | bytes 8470528 | tf_op jit(solution)/shard_map/uht,uthd->uhd/dot_general | solution.py:144
  27.1 1.6 collective-permute-start.3
  28.6 1.5 collective-permute-start.4
  31.3 1.3 collective-permute-done.4
  32.5 2.4 collective-permute-done.5
  40.9 2.4 collective-permute-start.26
  44.0 1.6 collective-permute-start.17
  45.6 2.2 collective-permute-start.11
  49.2 14.7 %collective-permute-done.18 = bf16[256,768]{1,0:T(8,128)(2,1)S(1)} collective-permute-done((bf16[256,768]{1,0:T(8,128)(2,1)S(1)}, bf16[256,768]{1,0:T(8,128)(2,1)S(1)}, u32[]{:S(2)}, u32[]{:S(2)}) %collective-permute-start.18) | collective-permute-done | bytes 393248 | tf_op jit(solution)/shard_map/ppermute | solution.py:29
  64.7 14.5 %collective-permute-done.11 = bf16[256,768]{1,0:T(8,128)(2,1)S(1)} collective-permute-done((bf16[256,768]{1,0:T(8,128)(2,1)S(1)}, bf16[256,768]{1,0:T(8,128)(2,1)S(1)}, u32[]{:S(2)}, u32[]{:S(2)}) %collective-permute-start.11) | collective-permute-done | bytes 393248 | tf_op jit(solution)/shard_map/ppermute | solution.py:29
  79.7 1.5 collective-permute-start.9
  81.6 1.5 collective-permute-done.29
  83.2 1.3 collective-permute-start.15
  84.4 12.1 %collective-permute-done.8 = bf16[128,2048]{1,0:T(8,128)(2,1)S(1)} collective-permute-done((bf16[128,2048]{1,0:T(8,128)(2,1)S(1)}, bf16[128,2048]{1,0:T(8,128)(2,1)S(1)}, u32[]{:S(2)}, u32[]{:S(2)}) %collective-permute-start.8) | collective-permute-done | bytes 524320 | tf_op jit(solution)/shard_map/ppermute | solution.py:52
  97.3 4.7 %collective-permute-done.35 = bf16[768,256]{1,0:T(8,128)(2,1)S(1)} collective-permute-done((bf16[768,256]{1,0:T(8,128)(2,1)S(1)}, bf16[768,256]{1,0:T(8,128)(2,1)S(1)}, u32[]{:S(2)}, u32[]{:S(2)}) %collective-permute-start.35) | collective-permute-done | bytes 393248 | tf_op jit(solution)/shard_map/ppermute | solution.py:35
  104.4 5.5 %collective-permute-done.15 = bf16[256,768]{1,0:T(8,128)(2,1)S(1)} collective-permute-done((bf16[256,768]{1,0:T(8,128)(2,1)S(1)}, bf16[256,768]{1,0:T(8,128)(2,1)S(1)}, u32[]{:S(2)}, u32[]{:S(2)}) %collective-permute-start.15) | collective-permute-done | bytes 393248 | tf_op jit(solution)/shard_map/ppermute | solution.py:35
  110.1 1.6 collective-permute-done.16
  111.7 1.8 fusion.102
  113.6 3.7 %multiply_convert_fusion.4 = (bf16[512,768]{1,0:T(8,128)(2,1)}, bf16[512,768]{1,0:T(8,128)(2,1)S(1)}, bf16[512,768]{1,0:T(8,128)(2,1)}, bf16[512,768]{1,0:T(8,128)(2,1)}) fusion(f32[512]{0:T(512)S(1)} %bitcast.161, f32[512,768]{1,0:T(8,128)S(1)} %fusion.102, bf16[512,2048]{1,0:T(8,128)(2,1)S(1)} %pad_maximum_fusion, ...), kind=kOutput, calls=%fused_computation.19 | convolution fusion | flops 1617690624 | bytes 9963520 | tf_op jit(solution)/shard_map/dot_general | solution.py:190
  117.2 1.4 convolution_convert_fusion
  119.3 1.6 collective-permute-start.37
  120.9 1.1 fusion.97
  123.0 2.4 collective-permute-start.34
  126.0 1.5 collective-permute-start.39
  128.7 1.2 sub.146
  129.9 1.3 sub.147
  132.1 15.3 %collective-permute-done.38 = bf16[128,512]{1,0:T(8,128)(2,1)S(1)} collective-permute-done((bf16[128,512]{1,0:T(8,128)(2,1)S(1)}, bf16[128,512]{1,0:T(8,128)(2,1)S(1)}, u32[]{:S(2)}, u32[]{:S(2)}) %collective-permute-start.38) | collective-permute-done | bytes 131104 | tf_op jit(solution)/shard_map/ppermute | solution.py:52
  148.1 1.6 fusion.24
  151.4 1.2 subtract_multiply_fusion
  155.4 1.6 fusion.25
  157.7 1.2 collective-permute-done.61
  159.4 1.6 collective-permute-start.43
  161.8 1.2 collective-permute-start.45
  163.0 1.6 collective-permute-start.40
  165.5 3.9 %collective-permute-done.63 = f32[4,2048]{1,0:T(4,128)S(1)} collective-permute-done((f32[4,2048]{1,0:T(4,128)S(1)}, f32[4,2048]{1,0:T(4,128)S(1)}, u32[]{:S(2)}, u32[]{:S(2)}) %collective-permute-start.63) | collective-permute-done | bytes 32800 | tf_op jit(solution)/shard_map/ppermute | solution.py:47
  170.0 1.2 add_subtract_fusion
  171.2 5.5 %collective-permute-done.64 = f32[4,2048]{1,0:T(4,128)S(1)} collective-permute-done((f32[4,2048]{1,0:T(4,128)S(1)}, f32[4,2048]{1,0:T(4,128)S(1)}, u32[]{:S(2)}, u32[]{:S(2)}) %collective-permute-start.64) | collective-permute-done | bytes 32800 | tf_op jit(solution)/shard_map/ppermute | solution.py:52
  177.6 2.2 collective-permute-start.42
  181.1 2.0 fusion.92
  183.1 12.6 %collective-permute-done.65 = f32[4,2048]{1,0:T(4,128)S(1)} collective-permute-done((f32[4,2048]{1,0:T(4,128)S(1)}, f32[4,2048]{1,0:T(4,128)S(1)}, u32[]{:S(2)}, u32[]{:S(2)}) %collective-permute-start.65) | collective-permute-done | bytes 32800 | tf_op jit(solution)/shard_map/ppermute | solution.py:52
  196.4 1.5 multiply_convert_fusion
  203.8 1.6 collective-permute-start.58
  206.0 1.6 collective-permute-start.53
  208.1 1.2 collective-permute-start.48
  210.1 6.6 %collective-permute-done.58 = bf16[256,768]{1,0:T(8,128)(2,1)S(1)} collective-permute-done((bf16[256,768]{1,0:T(8,128)(2,1)S(1)}, bf16[256,768]{1,0:T(8,128)(2,1)S(1)}, u32[]{:S(2)}, u32[]{:S(2)}) %collective-permute-start.58) | collective-permute-done | bytes 393248 | tf_op jit(solution)/shard_map/ppermute | solution.py:35
  216.9 2.3 collective-permute-start.59
  220.0 5.2 %collective-permute-done.53 = bf16[256,768]{1,0:T(8,128)(2,1)S(1)} collective-permute-done((bf16[256,768]{1,0:T(8,128)(2,1)S(1)}, bf16[256,768]{1,0:T(8,128)(2,1)S(1)}, u32[]{:S(2)}, u32[]{:S(2)}) %collective-permute-start.53) | collective-permute-done | bytes 393248 | tf_op jit(solution)/shard_map/ppermute | solution.py:35
  226.2 2.2 collective-permute-start.54
  229.2 4.4 %collective-permute-done.48 = bf16[256,768]{1,0:T(8,128)(2,1)S(1)} collective-permute-done((bf16[256,768]{1,0:T(8,128)(2,1)S(1)}, bf16[256,768]{1,0:T(8,128)(2,1)S(1)}, u32[]{:S(2)}, u32[]{:S(2)}) %collective-permute-start.48) | collective-permute-done | bytes 393248 | tf_op jit(solution)/shard_map/ppermute | solution.py:35
  234.7 10.3 %collective-permute-start.49 = (bf16[256,768]{1,0:T(8,128)(2,1)}, bf16[256,768]{1,0:T(8,128)(2,1)}, u32[]{:S(2)}, u32[]{:S(2)}) collective-permute-start(bf16[256,768]{1,0:T(8,128)(2,1)} %get-tuple-element.60), channel_id=1, source_target_pairs={{0,24},{4,28},{8,0},{12,4},{16,8},{20,12},{24,16},{28,20},{1,25},{... | collective-permute-start | bytes 1179656 | tf_op jit(solution)/shard_map/ppermute | solution.py:29
  245.0 4.0 %collective-permute-done.59 = bf16[256,768]{1,0:T(8,128)(2,1)S(1)} collective-permute-done((bf16[256,768]{1,0:T(8,128)(2,1)S(1)}, bf16[256,768]{1,0:T(8,128)(2,1)S(1)}, u32[]{:S(2)}, u32[]{:S(2)}) %collective-permute-start.59) | collective-permute-done | bytes 393248 | tf_op jit(solution)/shard_map/ppermute | solution.py:29
  249.0 2.0 collective-permute-start.50
  251.2 1.1 copy.25
  252.4 13.4 %collective-permute-done.54 = bf16[256,768]{1,0:T(8,128)(2,1)S(1)} collective-permute-done((bf16[256,768]{1,0:T(8,128)(2,1)}, bf16[256,768]{1,0:T(8,128)(2,1)S(1)}, u32[]{:S(2)}, u32[]{:S(2)}) %collective-permute-start.54) | collective-permute-done | bytes 393248 | tf_op jit(solution)/shard_map/ppermute | solution.py:29
  265.8 1.5 collective-permute-done.55
  267.3 2.1 add_bitcast_fusion.1
  269.4 6.4 %collective-permute-done.49 = bf16[256,768]{1,0:T(8,128)(2,1)} collective-permute-done((bf16[256,768]{1,0:T(8,128)(2,1)}, bf16[256,768]{1,0:T(8,128)(2,1)}, u32[]{:S(2)}, u32[]{:S(2)}) %collective-permute-start.49) | collective-permute-done | bytes 393248 | tf_op jit(solution)/shard_map/ppermute | solution.py:29
  275.8 7.6 %collective-permute-done.50 = bf16[256,768]{1,0:T(8,128)(2,1)} collective-permute-done((bf16[256,768]{1,0:T(8,128)(2,1)}, bf16[256,768]{1,0:T(8,128)(2,1)}, u32[]{:S(2)}, u32[]{:S(2)}) %collective-permute-start.50) | collective-permute-done | bytes 393248 | tf_op jit(solution)/shard_map/ppermute | solution.py:29
  283.4 2.3 add_bitcast_fusion.2
  (325 shorter events, 46.4 us)
Async XLA Ops:
  0.6 26.4 %collective-permute-start = (bf16[2,2048]{1,0:T(2,128)(2,1)}, bf16[2,2048]{1,0:T(2,128)(2,1)S(1)}, u32[]{:S(2)}, u32[]{:S(2)}) collective-permute-start(bf16[2,2048]{1,0:T(2,128)(2,1)} %param.14), channel_id=1, source_target_pairs={{0,8},{4,12},{8,16},{12,20},{16,24},{20,28},{24,0},{28,4},{1,9},{5... | collective-permute-start | bytes 24584 | tf_op jit(solution)/shard_map/ppermute | solution.py:29
  3.7 23.3 %collective-permute-start.1 = (bf16[2,2048]{1,0:T(2,128)(2,1)}, bf16[2,2048]{1,0:T(2,128)(2,1)S(1)}, u32[]{:S(2)}, u32[]{:S(2)}) collective-permute-start(bf16[2,2048]{1,0:T(2,128)(2,1)} %param.14), channel_id=1, source_target_pairs={{0,16},{4,20},{8,24},{12,28},{16,0},{20,4},{24,8},{28,12},{1,17},{... | collective-permute-start | bytes 24584 | tf_op jit(solution)/shard_map/ppermute | solution.py:29
  6.3 20.7 %collective-permute-start.2 = (bf16[2,2048]{1,0:T(2,128)(2,1)}, bf16[2,2048]{1,0:T(2,128)(2,1)S(1)}, u32[]{:S(2)}, u32[]{:S(2)}) collective-permute-start(bf16[2,2048]{1,0:T(2,128)(2,1)} %param.14), channel_id=1, source_target_pairs={{0,24},{4,28},{8,0},{12,4},{16,8},{20,12},{24,16},{28,20},{1,25},{... | collective-permute-start | bytes 24584 | tf_op jit(solution)/shard_map/ppermute | solution.py:29
  7.7 40.2 %collective-permute-start.27 = (bf16[768,256]{1,0:T(8,128)(2,1)}, bf16[768,256]{1,0:T(8,128)(2,1)}, u32[]{:S(2)}, u32[]{:S(2)}) collective-permute-start(bf16[768,256]{1,0:T(8,128)(2,1)} %bitcast.129), channel_id=1, source_target_pairs={{0,8},{4,12},{8,16},{12,20},{16,24},{20,28},{24,0},{28,4},{1,9},{5... | collective-permute-start | bytes 1179656 | tf_op jit(solution)/shard_map/ppermute | solution.py:29
  8.4 40.6 %collective-permute-start.28 = (bf16[768,256]{1,0:T(8,128)(2,1)}, bf16[768,256]{1,0:T(8,128)(2,1)S(1)}, u32[]{:S(2)}, u32[]{:S(2)}) collective-permute-start(bf16[768,256]{1,0:T(8,128)(2,1)} %bitcast.130), channel_id=1, source_target_pairs={{0,24},{4,28},{8,0},{12,4},{16,8},{20,12},{24,16},{28,20},{1,25},{... | collective-permute-start | bytes 1179656 | tf_op jit(solution)/shard_map/ppermute | solution.py:29
  27.1 4.2 %collective-permute-start.3 = (bf16[4,2,2048]{2,1,0:T(2,128)(2,1)S(1)}, bf16[4,2,2048]{2,1,0:T(2,128)(2,1)S(1)}, u32[]{:S(2)}, u32[]{:S(2)}) collective-permute-start(bf16[4,2,2048]{2,1,0:T(2,128)(2,1)S(1)} %pad_maximum_fusion.6), channel_id=1, source_target_pairs={{0,1},{1,0},{2,3},{3,2},{4,5},{5,4},{6,7},{7,6},{8,9},{9,8},{10,11... | collective-permute-start | bytes 98312 | tf_op jit(solution)/shard_map/ppermute | solution.py:52
  28.6 3.9 %collective-permute-start.4 = (bf16[4,2,2048]{2,1,0:T(2,128)(2,1)S(1)}, bf16[4,2,2048]{2,1,0:T(2,128)(2,1)S(1)}, u32[]{:S(2)}, u32[]{:S(2)}) collective-permute-start(bf16[4,2,2048]{2,1,0:T(2,128)(2,1)S(1)} %pad_maximum_fusion.6), channel_id=1, source_target_pairs={{0,2},{1,3},{2,0},{3,1},{4,6},{5,7},{6,4},{7,5},{8,10},{9,11},{10,... | collective-permute-start | bytes 98312 | tf_op jit(solution)/shard_map/ppermute | solution.py:52
  30.1 4.8 %collective-permute-start.5 = (bf16[4,2,2048]{2,1,0:T(2,128)(2,1)S(1)}, bf16[4,2,2048]{2,1,0:T(2,128)(2,1)S(1)}, u32[]{:S(2)}, u32[]{:S(2)}) collective-permute-start(bf16[4,2,2048]{2,1,0:T(2,128)(2,1)S(1)} %pad_maximum_fusion.6), channel_id=1, source_target_pairs={{0,3},{1,2},{2,1},{3,0},{4,7},{5,6},{6,5},{7,4},{8,11},{9,10},{10,... | collective-permute-start | bytes 98312 | tf_op jit(solution)/shard_map/ppermute | solution.py:52
  39.9 3.6 %collective-permute-start.24 = (f32[4,128]{1,0:T(4,128)S(1)}, f32[4,128]{1,0:T(4,128)S(1)}, u32[]{:S(2)}, u32[]{:S(2)}) collective-permute-start(f32[4,128]{1,0:T(4,128)S(1)} %bitcast.148), channel_id=1, source_target_pairs={{0,1},{1,0},{2,3},{3,2},{4,5},{5,4},{6,7},{7,6},{8,9},{9,8},{10,11... | collective-permute-start | bytes 6152 | tf_op jit(solution)/shard_map/ppermute | solution.py:52
  40.4 3.6 %collective-permute-start.25 = (f32[4,128]{1,0:T(4,128)S(1)}, f32[4,128]{1,0:T(4,128)S(1)}, u32[]{:S(2)}, u32[]{:S(2)}) collective-permute-start(f32[4,128]{1,0:T(4,128)S(1)} %bitcast.149), channel_id=1, source_target_pairs={{0,2},{1,3},{2,0},{3,1},{4,6},{5,7},{6,4},{7,5},{8,10},{9,11},{10,... | collective-permute-start | bytes 6152 | tf_op jit(solution)/shard_map/ppermute | solution.py:52
  40.9 4.7 %collective-permute-start.26 = (f32[4,128]{1,0:T(4,128)S(1)}, f32[4,128]{1,0:T(4,128)S(1)}, u32[]{:S(2)}, u32[]{:S(2)}) collective-permute-start(f32[4,128]{1,0:T(4,128)S(1)} %bitcast.150), channel_id=1, source_target_pairs={{0,3},{1,2},{2,1},{3,0},{4,7},{5,6},{6,5},{7,4},{8,11},{9,10},{10,... | collective-permute-start | bytes 6152 | tf_op jit(solution)/shard_map/ppermute | solution.py:52
  43.5 20.5 %collective-permute-start.18 = (bf16[256,768]{1,0:T(8,128)(2,1)S(1)}, bf16[256,768]{1,0:T(8,128)(2,1)S(1)}, u32[]{:S(2)}, u32[]{:S(2)}) collective-permute-start(bf16[256,768]{1,0:T(8,128)(2,1)S(1)} %bitcast.122), channel_id=1, source_target_pairs={{0,24},{4,28},{8,0},{12,4},{16,8},{20,12},{24,16},{28,20},{1,25},{... | collective-permute-start | bytes 1179656 | tf_op jit(solution)/shard_map/ppermute | solution.py:29
  44.0 20.0 %collective-permute-start.17 = (bf16[256,768]{1,0:T(8,128)(2,1)S(1)}, bf16[256,768]{1,0:T(8,128)(2,1)S(1)}, u32[]{:S(2)}, u32[]{:S(2)}) collective-permute-start(bf16[256,768]{1,0:T(8,128)(2,1)S(1)} %bitcast.123), channel_id=1, source_target_pairs={{0,8},{4,12},{8,16},{12,20},{16,24},{20,28},{24,0},{28,4},{1,9},{5... | collective-permute-start | bytes 1179656 | tf_op jit(solution)/shard_map/ppermute | solution.py:29
  45.6 33.6 %collective-permute-start.11 = (bf16[256,768]{1,0:T(8,128)(2,1)S(1)}, bf16[256,768]{1,0:T(8,128)(2,1)S(1)}, u32[]{:S(2)}, u32[]{:S(2)}) collective-permute-start(bf16[256,768]{1,0:T(8,128)(2,1)S(1)} %bitcast.126), channel_id=1, source_target_pairs={{0,24},{4,28},{8,0},{12,4},{16,8},{20,12},{24,16},{28,20},{1,25},{... | collective-permute-start | bytes 1179656 | tf_op jit(solution)/shard_map/ppermute | solution.py:29
  47.9 31.8 %collective-permute-start.10 = (bf16[256,768]{1,0:T(8,128)(2,1)S(1)}, bf16[256,768]{1,0:T(8,128)(2,1)S(1)}, u32[]{:S(2)}, u32[]{:S(2)}) collective-permute-start(bf16[256,768]{1,0:T(8,128)(2,1)S(1)} %bitcast.127), channel_id=1, source_target_pairs={{0,8},{4,12},{8,16},{12,20},{16,24},{20,28},{24,0},{28,4},{1,9},{5... | collective-permute-start | bytes 1179656 | tf_op jit(solution)/shard_map/ppermute | solution.py:29
  49.0 32.4 %collective-permute-start.19 = (bf16[256,768]{1,0:T(8,128)(2,1)S(1)}, bf16[256,768]{1,0:T(8,128)(2,1)S(1)}, u32[]{:S(2)}, u32[]{:S(2)}) collective-permute-start(bf16[256,768]{1,0:T(8,128)(2,1)S(1)} %bitcast.124), channel_id=1, source_target_pairs={{0,4},{4,0},{8,12},{12,8},{16,20},{20,16},{24,28},{28,24},{1,5},{5... | collective-permute-start | bytes 1179656 | tf_op jit(solution)/shard_map/ppermute | solution.py:42
  64.0 17.6 %collective-permute-start.12 = (bf16[256,768]{1,0:T(8,128)(2,1)S(1)}, bf16[256,768]{1,0:T(8,128)(2,1)S(1)}, u32[]{:S(2)}, u32[]{:S(2)}) collective-permute-start(bf16[256,768]{1,0:T(8,128)(2,1)S(1)} %bitcast.128), channel_id=1, source_target_pairs={{0,4},{4,0},{8,12},{12,8},{16,20},{20,16},{24,28},{28,24},{1,5},{5... | collective-permute-start | bytes 1179656 | tf_op jit(solution)/shard_map/ppermute | solution.py:42
  64.0 19.2 %collective-permute-start.7 = (bf16[128,2048]{1,0:T(8,128)(2,1)S(1)}, bf16[128,2048]{1,0:T(8,128)(2,1)S(1)}, u32[]{:S(2)}, u32[]{:S(2)}) collective-permute-start(bf16[128,2048]{1,0:T(8,128)(2,1)S(1)} %multiply_convert_fusion.6), channel_id=1, source_target_pairs={{0,1},{1,0},{2,3},{3,2},{4,5},{5,4},{6,7},{7,6},{8,9},{9,8},{10,11... | collective-permute-start | bytes 1572872 | tf_op jit(solution)/shard_map/ppermute | solution.py:52
  79.2 17.4 %collective-permute-start.8 = (bf16[128,2048]{1,0:T(8,128)(2,1)S(1)}, bf16[128,2048]{1,0:T(8,128)(2,1)S(1)}, u32[]{:S(2)}, u32[]{:S(2)}) collective-permute-start(bf16[128,2048]{1,0:T(8,128)(2,1)S(1)} %multiply_convert_fusion.6), channel_id=1, source_target_pairs={{0,2},{1,3},{2,0},{3,1},{4,6},{5,7},{6,4},{7,5},{8,10},{9,11},{10,... | collective-permute-start | bytes 1572872 | tf_op jit(solution)/shard_map/ppermute | solution.py:52
  79.7 16.9 %collective-permute-start.9 = (bf16[128,2048]{1,0:T(8,128)(2,1)S(1)}, bf16[128,2048]{1,0:T(8,128)(2,1)S(1)}, u32[]{:S(2)}, u32[]{:S(2)}) collective-permute-start(bf16[128,2048]{1,0:T(8,128)(2,1)S(1)} %multiply_convert_fusion.6), channel_id=1, source_target_pairs={{0,3},{1,2},{2,1},{3,0},{4,7},{5,6},{6,5},{7,4},{8,11},{9,10},{10,... | collective-permute-start | bytes 1572872 | tf_op jit(solution)/shard_map/ppermute | solution.py:52
  81.3 1.8 collective-permute-start.29
  81.5 21.2 %collective-permute-start.22 = (bf16[256,768]{1,0:T(8,128)(2,1)S(1)}, bf16[256,768]{1,0:T(8,128)(2,1)S(1)}, u32[]{:S(2)}, u32[]{:S(2)}) collective-permute-start(bf16[256,768]{1,0:T(8,128)(2,1)S(1)} %get-tuple-element.74), channel_id=1, source_target_pairs={{0,16},{4,20},{8,0},{12,4},{16,24},{20,28},{24,8},{28,12},{1,17},{... | collective-permute-start | bytes 1179656 | tf_op jit(solution)/shard_map/ppermute | solution.py:35
  83.1 18.9 %collective-permute-start.35 = (bf16[768,256]{1,0:T(8,128)(2,1)S(1)}, bf16[768,256]{1,0:T(8,128)(2,1)S(1)}, u32[]{:S(2)}, u32[]{:S(2)}) collective-permute-start(bf16[768,256]{1,0:T(8,128)(2,1)S(1)} %get-tuple-element.71), channel_id=1, source_target_pairs={{0,16},{4,20},{8,0},{12,4},{16,24},{20,28},{24,8},{28,12},{1,17},{... | collective-permute-start | bytes 1179656 | tf_op jit(solution)/shard_map/ppermute | solution.py:35
  83.2 26.8 %collective-permute-start.15 = (bf16[256,768]{1,0:T(8,128)(2,1)S(1)}, bf16[256,768]{1,0:T(8,128)(2,1)S(1)}, u32[]{:S(2)}, u32[]{:S(2)}) collective-permute-start(bf16[256,768]{1,0:T(8,128)(2,1)S(1)} %get-tuple-element.72), channel_id=1, source_target_pairs={{0,16},{4,20},{8,0},{12,4},{16,24},{20,28},{24,8},{28,12},{1,17},{... | collective-permute-start | bytes 1179656 | tf_op jit(solution)/shard_map/ppermute | solution.py:35
  96.6 5.5 %collective-permute-start.20 = (bf16[256,768]{1,0:T(8,128)(2,1)S(1)}, bf16[256,768]{1,0:T(8,128)(2,1)S(1)}, u32[]{:S(2)}, u32[]{:S(2)}) collective-permute-start(bf16[256,768]{1,0:T(8,128)(2,1)S(1)} %collective-permute-done.17), channel_id=1, source_target_pairs={{0,4},{4,0},{8,12},{12,8},{16,20},{20,16},{24,28},{28,24},{1,5},{5... | collective-permute-start | bytes 1179656 | tf_op jit(solution)/shard_map/ppermute | solution.py:42
  96.6 6.1 %collective-permute-start.21 = (bf16[256,768]{1,0:T(8,128)(2,1)S(1)}, bf16[256,768]{1,0:T(8,128)(2,1)S(1)}, u32[]{:S(2)}, u32[]{:S(2)}) collective-permute-start(bf16[256,768]{1,0:T(8,128)(2,1)S(1)} %collective-permute-done.18), channel_id=1, source_target_pairs={{0,4},{4,0},{8,12},{12,8},{16,20},{20,16},{24,28},{28,24},{1,5},{5... | collective-permute-start | bytes 1179656 | tf_op jit(solution)/shard_map/ppermute | solution.py:42
  102.0 1.7 collective-permute-start.13
  102.1 2.2 collective-permute-start.14
  102.7 7.4 %collective-permute-start.30 = (bf16[768,256]{1,0:T(8,128)(2,1)}, bf16[768,256]{1,0:T(8,128)(2,1)S(1)}, u32[]{:S(2)}, u32[]{:S(2)}) collective-permute-start(bf16[768,256]{1,0:T(8,128)(2,1)} %collective-permute-done.27), channel_id=1, source_target_pairs={{0,4},{4,0},{8,12},{12,8},{16,20},{20,16},{24,28},{28,24},{1,5},{5... | collective-permute-start | bytes 1179656 | tf_op jit(solution)/shard_map/ppermute | solution.py:42
  102.8 7.3 %collective-permute-start.31 = (bf16[768,256]{1,0:T(8,128)(2,1)S(1)}, bf16[768,256]{1,0:T(8,128)(2,1)S(1)}, u32[]{:S(2)}, u32[]{:S(2)}) collective-permute-start(bf16[768,256]{1,0:T(8,128)(2,1)S(1)} %collective-permute-done.28), channel_id=1, source_target_pairs={{0,4},{4,0},{8,12},{12,8},{16,20},{20,16},{24,28},{28,24},{1,5},{5... | collective-permute-start | bytes 1179656 | tf_op jit(solution)/shard_map/ppermute | solution.py:42
  103.7 9.8 %collective-permute-start.23 = (bf16[256,768]{1,0:T(8,128)(2,1)S(1)}, bf16[256,768]{1,0:T(8,128)(2,1)S(1)}, u32[]{:S(2)}, u32[]{:S(2)}) collective-permute-start(bf16[256,768]{1,0:T(8,128)(2,1)S(1)} %collective-permute-done.22), channel_id=1, source_target_pairs={{0,4},{4,0},{8,12},{12,8},{16,20},{20,16},{24,28},{28,24},{1,5},{5... | collective-permute-start | bytes 1179656 | tf_op jit(solution)/shard_map/ppermute | solution.py:42
  104.3 14.4 %collective-permute-start.36 = (bf16[768,256]{1,0:T(8,128)(2,1)S(1)}, bf16[768,256]{1,0:T(8,128)(2,1)S(1)}, u32[]{:S(2)}, u32[]{:S(2)}) collective-permute-start(bf16[768,256]{1,0:T(8,128)(2,1)S(1)} %collective-permute-done.35), channel_id=1, source_target_pairs={{0,4},{4,0},{8,12},{12,8},{16,20},{20,16},{24,28},{28,24},{1,5},{5... | collective-permute-start | bytes 1179656 | tf_op jit(solution)/shard_map/ppermute | solution.py:42
  110.0 1.7 collective-permute-start.16
  119.3 6.7 %collective-permute-start.37 = (bf16[128,512]{1,0:T(8,128)(2,1)S(1)}, bf16[128,512]{1,0:T(8,128)(2,1)S(1)}, u32[]{:S(2)}, u32[]{:S(2)}) collective-permute-start(bf16[128,512]{1,0:T(8,128)(2,1)S(1)} %get-tuple-element.69), channel_id=1, source_target_pairs={{0,1},{1,0},{2,3},{3,2},{4,5},{5,4},{6,7},{7,6},{8,9},{9,8},{10,11... | collective-permute-start | bytes 393224 | tf_op jit(solution)/shard_map/ppermute | solution.py:52
  122.0 25.6 %collective-permute-start.32 = (bf16[128,1536]{1,0:T(8,128)(2,1)}, bf16[128,1536]{1,0:T(8,128)(2,1)S(1)}, u32[]{:S(2)}, u32[]{:S(2)}) collective-permute-start(bf16[128,1536]{1,0:T(8,128)(2,1)} %get-tuple-element.64), channel_id=1, source_target_pairs={{0,1},{1,0},{2,3},{3,2},{4,5},{5,4},{6,7},{7,6},{8,9},{9,8},{10,11... | collective-permute-start | bytes 1179656 | tf_op jit(solution)/shard_map/ppermute | solution.py:52
  122.5 25.0 %collective-permute-start.33 = (bf16[128,1536]{1,0:T(8,128)(2,1)}, bf16[128,1536]{1,0:T(8,128)(2,1)S(1)}, u32[]{:S(2)}, u32[]{:S(2)}) collective-permute-start(bf16[128,1536]{1,0:T(8,128)(2,1)} %get-tuple-element.63), channel_id=1, source_target_pairs={{0,2},{1,3},{2,0},{3,1},{4,6},{5,7},{6,4},{7,5},{8,10},{9,11},{10,... | collective-permute-start | bytes 1179656 | tf_op jit(solution)/shard_map/ppermute | solution.py:52
  123.0 25.0 %collective-permute-start.34 = (bf16[128,1536]{1,0:T(8,128)(2,1)}, bf16[128,1536]{1,0:T(8,128)(2,1)}, u32[]{:S(2)}, u32[]{:S(2)}) collective-permute-start(bf16[128,1536]{1,0:T(8,128)(2,1)} %get-tuple-element.62), channel_id=1, source_target_pairs={{0,3},{1,2},{2,1},{3,0},{4,7},{5,6},{6,5},{7,4},{8,11},{9,10},{10,... | collective-permute-start | bytes 1179656 | tf_op jit(solution)/shard_map/ppermute | solution.py:52
  125.5 21.9 %collective-permute-start.38 = (bf16[128,512]{1,0:T(8,128)(2,1)S(1)}, bf16[128,512]{1,0:T(8,128)(2,1)S(1)}, u32[]{:S(2)}, u32[]{:S(2)}) collective-permute-start(bf16[128,512]{1,0:T(8,128)(2,1)S(1)} %get-tuple-element.68), channel_id=1, source_target_pairs={{0,2},{1,3},{2,0},{3,1},{4,6},{5,7},{6,4},{7,5},{8,10},{9,11},{10,... | collective-permute-start | bytes 393224 | tf_op jit(solution)/shard_map/ppermute | solution.py:52
  126.0 21.4 %collective-permute-start.39 = (bf16[128,512]{1,0:T(8,128)(2,1)S(1)}, bf16[128,512]{1,0:T(8,128)(2,1)S(1)}, u32[]{:S(2)}, u32[]{:S(2)}) collective-permute-start(bf16[128,512]{1,0:T(8,128)(2,1)S(1)} %get-tuple-element.67), channel_id=1, source_target_pairs={{0,3},{1,2},{2,1},{3,0},{4,7},{5,6},{6,5},{7,4},{8,11},{9,10},{10,... | collective-permute-start | bytes 393224 | tf_op jit(solution)/shard_map/ppermute | solution.py:52
  158.9 5.7 %collective-permute-start.62 = (f32[4,2048]{1,0:T(4,128)S(1)}, f32[4,2048]{1,0:T(4,128)S(1)}, u32[]{:S(2)}, u32[]{:S(2)}) collective-permute-start(f32[4,2048]{1,0:T(4,128)S(1)} %add.528), channel_id=1, source_target_pairs={{0,8},{4,12},{8,0},{12,4},{16,24},{20,28},{24,16},{28,20},{1,9},{5... | collective-permute-start | bytes 98312 | tf_op jit(solution)/shard_map/ppermute | solution.py:47
  159.4 18.2 %collective-permute-start.43 = (bf16[128,512]{1,0:T(8,128)(2,1)S(1)}, bf16[128,512]{1,0:T(8,128)(2,1)S(1)}, u32[]{:S(2)}, u32[]{:S(2)}) collective-permute-start(bf16[128,512]{1,0:T(8,128)(2,1)S(1)} %slice.195), channel_id=1, source_target_pairs={{0,1},{1,0},{2,3},{3,2},{4,5},{5,4},{6,7},{7,6},{8,9},{9,8},{10,11... | collective-permute-start | bytes 393224 | tf_op jit(solution)/shard_map/ppermute | solution.py:52
  161.0 18.8 %collective-permute-start.44 = (bf16[128,512]{1,0:T(8,128)(2,1)S(1)}, bf16[128,512]{1,0:T(8,128)(2,1)S(1)}, u32[]{:S(2)}, u32[]{:S(2)}) collective-permute-start(bf16[128,512]{1,0:T(8,128)(2,1)S(1)} %slice.195), channel_id=1, source_target_pairs={{0,2},{1,3},{2,0},{3,1},{4,6},{5,7},{6,4},{7,5},{8,10},{9,11},{10,... | collective-permute-start | bytes 393224 | tf_op jit(solution)/shard_map/ppermute | solution.py:52
  161.8 18.8 %collective-permute-start.45 = (bf16[128,512]{1,0:T(8,128)(2,1)S(1)}, bf16[128,512]{1,0:T(8,128)(2,1)S(1)}, u32[]{:S(2)}, u32[]{:S(2)}) collective-permute-start(bf16[128,512]{1,0:T(8,128)(2,1)S(1)} %slice.195), channel_id=1, source_target_pairs={{0,3},{1,2},{2,1},{3,0},{4,7},{5,6},{6,5},{7,4},{8,11},{9,10},{10,... | collective-permute-start | bytes 393224 | tf_op jit(solution)/shard_map/ppermute | solution.py:52
  163.0 33.4 %collective-permute-start.40 = (bf16[128,1536]{1,0:T(8,128)(2,1)S(1)}, bf16[128,1536]{1,0:T(8,128)(2,1)S(1)}, u32[]{:S(2)}, u32[]{:S(2)}) collective-permute-start(bf16[128,1536]{1,0:T(8,128)(2,1)S(1)} %slice.194), channel_id=1, source_target_pairs={{0,1},{1,0},{2,3},{3,2},{4,5},{5,4},{6,7},{7,6},{8,9},{9,8},{10,11... | collective-permute-start | bytes 1179656 | tf_op jit(solution)/shard_map/ppermute | solution.py:52
  164.6 4.9 %collective-permute-start.63 = (f32[4,2048]{1,0:T(4,128)S(1)}, f32[4,2048]{1,0:T(4,128)S(1)}, u32[]{:S(2)}, u32[]{:S(2)}) collective-permute-start(f32[4,2048]{1,0:T(4,128)S(1)} %add.529), channel_id=1, source_target_pairs={{0,16},{4,20},{8,24},{12,28},{16,0},{20,4},{24,8},{28,12},{1,17},{... | collective-permute-start | bytes 98312 | tf_op jit(solution)/shard_map/ppermute | solution.py:47
  169.4 7.3 %collective-permute-start.64 = (f32[4,2048]{1,0:T(4,128)S(1)}, f32[4,2048]{1,0:T(4,128)S(1)}, u32[]{:S(2)}, u32[]{:S(2)}) collective-permute-start(f32[4,2048]{1,0:T(4,128)S(1)} %add.530), channel_id=1, source_target_pairs={{0,1},{1,0},{2,3},{3,2},{4,5},{5,4},{6,7},{7,6},{8,9},{9,8},{10,11... | collective-permute-start | bytes 98312 | tf_op jit(solution)/shard_map/ppermute | solution.py:52
  176.7 19.7 %collective-permute-start.41 = (bf16[128,1536]{1,0:T(8,128)(2,1)S(1)}, bf16[128,1536]{1,0:T(8,128)(2,1)S(1)}, u32[]{:S(2)}, u32[]{:S(2)}) collective-permute-start(bf16[128,1536]{1,0:T(8,128)(2,1)S(1)} %slice.194), channel_id=1, source_target_pairs={{0,2},{1,3},{2,0},{3,1},{4,6},{5,7},{6,4},{7,5},{8,10},{9,11},{10,... | collective-permute-start | bytes 1179656 | tf_op jit(solution)/shard_map/ppermute | solution.py:52
  177.6 18.8 %collective-permute-start.42 = (bf16[128,1536]{1,0:T(8,128)(2,1)S(1)}, bf16[128,1536]{1,0:T(8,128)(2,1)S(1)}, u32[]{:S(2)}, u32[]{:S(2)}) collective-permute-start(bf16[128,1536]{1,0:T(8,128)(2,1)S(1)} %slice.194), channel_id=1, source_target_pairs={{0,3},{1,2},{2,1},{3,0},{4,7},{5,6},{6,5},{7,4},{8,11},{9,10},{10,... | collective-permute-start | bytes 1179656 | tf_op jit(solution)/shard_map/ppermute | solution.py:52
  179.7 16.0 %collective-permute-start.65 = (f32[4,2048]{1,0:T(4,128)S(1)}, f32[4,2048]{1,0:T(4,128)S(1)}, u32[]{:S(2)}, u32[]{:S(2)}) collective-permute-start(f32[4,2048]{1,0:T(4,128)S(1)} %add.531), channel_id=1, source_target_pairs={{0,2},{1,3},{2,0},{3,1},{4,6},{5,7},{6,4},{7,5},{8,10},{9,11},{10,... | collective-permute-start | bytes 98312 | tf_op jit(solution)/shard_map/ppermute | solution.py:52
  181.0 21.7 %collective-permute-start.57 = (bf16[256,768]{1,0:T(8,128)(2,1)S(1)}, bf16[256,768]{1,0:T(8,128)(2,1)S(1)}, u32[]{:S(2)}, u32[]{:S(2)}) collective-permute-start(bf16[256,768]{1,0:T(8,128)(2,1)S(1)} %convolution_convert_fusion.5), channel_id=1, source_target_pairs={{0,4},{4,0},{8,12},{12,8},{16,20},{20,16},{24,28},{28,24},{1,5},{5... | collective-permute-start | bytes 1179656 | tf_op jit(solution)/shard_map/ppermute | solution.py:42
  200.3 7.7 %collective-permute-start.56 = (bf16[768,768]{1,0:T(8,128)(2,1)S(1)}, bf16[768,768]{1,0:T(8,128)(2,1)S(1)}, u32[]{:S(2)}, u32[]{:S(2)}) collective-permute-start(bf16[768,768]{1,0:T(8,128)(2,1)S(1)} %convolution_convert_fusion.1), channel_id=1, source_target_pairs={{0,4},{4,0},{8,12},{12,8},{16,20},{20,16},{24,28},{28,24},{1,5},{5... | collective-permute-start | bytes 3538952 | tf_op jit(solution)/shard_map/ppermute | solution.py:42
  200.4 3.4 %collective-permute-start.52 = (bf16[256,768]{1,0:T(8,128)(2,1)S(1)}, bf16[256,768]{1,0:T(8,128)(2,1)S(1)}, u32[]{:S(2)}, u32[]{:S(2)}) collective-permute-start(bf16[256,768]{1,0:T(8,128)(2,1)S(1)} %convolution_convert_fusion.6), channel_id=1, source_target_pairs={{0,4},{4,0},{8,12},{12,8},{16,20},{20,16},{24,28},{28,24},{1,5},{5... | collective-permute-start | bytes 1179656 | tf_op jit(solution)/shard_map/ppermute | solution.py:42
  202.1 17.0 %collective-permute-start.51 = (bf16[768,768]{1,0:T(8,128)(2,1)S(1)}, bf16[768,768]{1,0:T(8,128)(2,1)S(1)}, u32[]{:S(2)}, u32[]{:S(2)}) collective-permute-start(bf16[768,768]{1,0:T(8,128)(2,1)S(1)} %convolution_convert_fusion.2), channel_id=1, source_target_pairs={{0,4},{4,0},{8,12},{12,8},{16,20},{20,16},{24,28},{28,24},{1,5},{5... | collective-permute-start | bytes 3538952 | tf_op jit(solution)/shard_map/ppermute | solution.py:42
  202.3 3.8 %collective-permute-start.47 = (bf16[256,768]{1,0:T(8,128)(2,1)S(1)}, bf16[256,768]{1,0:T(8,128)(2,1)S(1)}, u32[]{:S(2)}, u32[]{:S(2)}) collective-permute-start(bf16[256,768]{1,0:T(8,128)(2,1)S(1)} %convolution_convert_fusion.7), channel_id=1, source_target_pairs={{0,4},{4,0},{8,12},{12,8},{16,20},{20,16},{24,28},{28,24},{1,5},{5... | collective-permute-start | bytes 1179656 | tf_op jit(solution)/shard_map/ppermute | solution.py:42
  202.7 25.7 %collective-permute-start.46 = (bf16[768,768]{1,0:T(8,128)(2,1)S(1)}, bf16[768,768]{1,0:T(8,128)(2,1)S(1)}, u32[]{:S(2)}, u32[]{:S(2)}) collective-permute-start(bf16[768,768]{1,0:T(8,128)(2,1)S(1)} %convolution_convert_fusion.3), channel_id=1, source_target_pairs={{0,4},{4,0},{8,12},{12,8},{16,20},{20,16},{24,28},{28,24},{1,5},{5... | collective-permute-start | bytes 3538952 | tf_op jit(solution)/shard_map/ppermute | solution.py:42
  203.8 12.9 %collective-permute-start.58 = (bf16[256,768]{1,0:T(8,128)(2,1)S(1)}, bf16[256,768]{1,0:T(8,128)(2,1)S(1)}, u32[]{:S(2)}, u32[]{:S(2)}) collective-permute-start(bf16[256,768]{1,0:T(8,128)(2,1)S(1)} %fusion.11), channel_id=1, source_target_pairs={{0,8},{4,12},{8,24},{12,28},{16,0},{20,4},{24,16},{28,20},{1,9},{5... | collective-permute-start | bytes 1179656 | tf_op jit(solution)/shard_map/ppermute | solution.py:35
  206.0 19.2 %collective-permute-start.53 = (bf16[256,768]{1,0:T(8,128)(2,1)S(1)}, bf16[256,768]{1,0:T(8,128)(2,1)S(1)}, u32[]{:S(2)}, u32[]{:S(2)}) collective-permute-start(bf16[256,768]{1,0:T(8,128)(2,1)S(1)} %fusion.10), channel_id=1, source_target_pairs={{0,8},{4,12},{8,24},{12,28},{16,0},{20,4},{24,16},{28,20},{1,9},{5... | collective-permute-start | bytes 1179656 | tf_op jit(solution)/shard_map/ppermute | solution.py:35
  208.1 25.5 %collective-permute-start.48 = (bf16[256,768]{1,0:T(8,128)(2,1)S(1)}, bf16[256,768]{1,0:T(8,128)(2,1)S(1)}, u32[]{:S(2)}, u32[]{:S(2)}) collective-permute-start(bf16[256,768]{1,0:T(8,128)(2,1)S(1)} %fusion.9), channel_id=1, source_target_pairs={{0,8},{4,12},{8,24},{12,28},{16,0},{20,4},{24,16},{28,20},{1,9},{5... | collective-permute-start | bytes 1179656 | tf_op jit(solution)/shard_map/ppermute | solution.py:35
  216.9 32.1 %collective-permute-start.59 = (bf16[256,768]{1,0:T(8,128)(2,1)S(1)}, bf16[256,768]{1,0:T(8,128)(2,1)S(1)}, u32[]{:S(2)}, u32[]{:S(2)}) collective-permute-start(bf16[256,768]{1,0:T(8,128)(2,1)S(1)} %get-tuple-element.54), channel_id=1, source_target_pairs={{0,24},{4,28},{8,0},{12,4},{16,8},{20,12},{24,16},{28,20},{1,25},{... | collective-permute-start | bytes 1179656 | tf_op jit(solution)/shard_map/ppermute | solution.py:29
  219.2 31.8 %collective-permute-start.60 = (bf16[256,768]{1,0:T(8,128)(2,1)S(1)}, bf16[256,768]{1,0:T(8,128)(2,1)S(1)}, u32[]{:S(2)}, u32[]{:S(2)}) collective-permute-start(bf16[256,768]{1,0:T(8,128)(2,1)S(1)} %get-tuple-element.55), channel_id=1, source_target_pairs={{0,8},{4,12},{8,16},{12,20},{16,24},{20,28},{24,0},{28,4},{1,9},{5... | collective-permute-start | bytes 1179656 | tf_op jit(solution)/shard_map/ppermute | solution.py:29
  226.2 39.6 %collective-permute-start.54 = (bf16[256,768]{1,0:T(8,128)(2,1)}, bf16[256,768]{1,0:T(8,128)(2,1)S(1)}, u32[]{:S(2)}, u32[]{:S(2)}) collective-permute-start(bf16[256,768]{1,0:T(8,128)(2,1)} %get-tuple-element.56), channel_id=1, source_target_pairs={{0,24},{4,28},{8,0},{12,4},{16,8},{20,12},{24,16},{28,20},{1,25},{... | collective-permute-start | bytes 1179656 | tf_op jit(solution)/shard_map/ppermute | solution.py:29
  228.4 38.9 %collective-permute-start.55 = (bf16[256,768]{1,0:T(8,128)(2,1)S(1)}, bf16[256,768]{1,0:T(8,128)(2,1)}, u32[]{:S(2)}, u32[]{:S(2)}) collective-permute-start(bf16[256,768]{1,0:T(8,128)(2,1)S(1)} %get-tuple-element.57), channel_id=1, source_target_pairs={{0,8},{4,12},{8,16},{12,20},{16,24},{20,28},{24,0},{28,4},{1,9},{5... | collective-permute-start | bytes 1179656 | tf_op jit(solution)/shard_map/ppermute | solution.py:29
  234.7 41.1 %collective-permute-start.49 = (bf16[256,768]{1,0:T(8,128)(2,1)}, bf16[256,768]{1,0:T(8,128)(2,1)}, u32[]{:S(2)}, u32[]{:S(2)}) collective-permute-start(bf16[256,768]{1,0:T(8,128)(2,1)} %get-tuple-element.60), channel_id=1, source_target_pairs={{0,24},{4,28},{8,0},{12,4},{16,8},{20,12},{24,16},{28,20},{1,25},{... | collective-permute-start | bytes 1179656 | tf_op jit(solution)/shard_map/ppermute | solution.py:29
  249.0 34.4 %collective-permute-start.50 = (bf16[256,768]{1,0:T(8,128)(2,1)}, bf16[256,768]{1,0:T(8,128)(2,1)}, u32[]{:S(2)}, u32[]{:S(2)}) collective-permute-start(bf16[256,768]{1,0:T(8,128)(2,1)} %get-tuple-element.61), channel_id=1, source_target_pairs={{0,8},{4,12},{8,16},{12,20},{16,24},{20,28},{24,0},{28,4},{1,9},{5... | collective-permute-start | bytes 1179656 | tf_op jit(solution)/shard_map/ppermute | solution.py:29
  (44 other events, 316.2 us)

commit v2 on v1

v2 whole, which is shorter than its diff:
```python
import functools
import math

import jax
import jax.numpy as jnp
from jax import lax
from jax.experimental import pallas as pl
from jax.experimental.pallas import tpu as pltpu
from jax.sharding import PartitionSpec as P


CANDS = 64
HEAD = 128

norm_eps = 1e-06
loss_scale = 1024.0


def silu_pair(pre_act):
    sigma_val = jax.nn.sigmoid(pre_act)
    return (pre_act * sigma_val, sigma_val * (1.0 + pre_act * (1.0 - sigma_val)))


def dp_shift(value, step):
    size = lax.axis_size("dp")
    nz = size // 2
    return lax.ppermute(
        value, "dp", [(2 * z + c, 2 * ((z + step) % nz) + c) for z in range(nz) for c in range(2)]
    )


def dp_pairs(value, targets):
    return lax.ppermute(
        value, "dp", [(2 * z + c, 2 * t + c) for z, t in enumerate(targets) for c in range(2)]
    )


def core_swap(value):
    size = lax.axis_size("dp")
    return lax.ppermute(value, "dp", [(i, i ^ 1) for i in range(size)])


def dp_xor(value, mask):
    size = lax.axis_size("dp")
    return lax.ppermute(value, "dp", [(i, i ^ mask) for i in range(size)])


def expert_xor(value, mask):
    size = lax.axis_size("expert")
    return lax.ppermute(value, "expert", [(i, i ^ mask) for i in range(size)])


def expert_exchange(values):
    got = {0: values[0]}
    for k in sorted(range(1, len(values)), key=lambda k: -bin(k).count("1")):
        got[k] = expert_xor(values[k], k)
    return [got[k] for k in range(len(values))]


RELAY_OUT = (2, 0, 3, 1)
RELAY_BACK = (1, 3, 0, 2)


def slot_order(nz):
    return (0, 1, 3, 2) if nz == 4 else tuple(range(nz))


def add_up(*terms):
    total = terms[0].astype(jnp.float32)
    for term in terms[1:]:
        total = total + term.astype(jnp.float32)
    return total


VMEM = pl.BlockSpec(memory_space=pltpu.VMEM)
SMEM = pl.BlockSpec(memory_space=pltpu.SMEM)


def spans_of(index_ref, width):
    return [
        (pl.ds(i * width, width), pl.ds(pl.multiple_of(index_ref[i] * width, width), width))
        for i in range(index_ref.shape[0])
    ]


def arrange_kernel(width, index_ref, *refs):
    half = len(refs) // 2
    for here, there in spans_of(index_ref, width):
        for source, target in zip(refs[:half], refs[half:]):
            target[:, here] = source[:, there].astype(target.dtype)


def place_kernel(width, index_ref, source, target):
    for here, there in spans_of(index_ref, width):
        target[:, there] = source[:, here]


def rows_kernel(width, index_ref, slot_ref, table_ref, context_ref, x_ref, normed_ref):
    rows, depth = x_ref.shape
    users = context_ref.shape[0]
    slots = lax.broadcasted_iota(jnp.int32, (rows, table_ref.shape[0]), 1)
    chosen = (slots == slot_ref[...]).astype(jnp.float32).astype(jnp.bfloat16)
    squares = jnp.zeros((rows, 1), jnp.float32)
    for here, there in spans_of(index_ref, width):
        item = jnp.dot(chosen, table_ref[:, there], preferred_element_type=jnp.float32)
        context = context_ref[:, there]
        shared = jnp.concatenate(
            [jnp.broadcast_to(context[u : u + 1], (rows // users, width)) for u in range(users)]
        )
        value = item + shared
        x_ref[:, here] = value
        squares = squares + jnp.sum(value * value, axis=1, keepdims=True)
    scale = lax.rsqrt(squares / depth + norm_eps)
    for here, _ in spans_of(index_ref, width):
        normed_ref[:, here] = (x_ref[:, here] * scale).astype(jnp.bfloat16)


def like(*pairs):
    return [jax.ShapeDtypeStruct(shape, dtype) for shape, dtype in pairs]


def local(
    history,
    lengths,
    user_query,
    pos_item,
    neg_index,
    routes,
    w_router,
    w_gate,
    w_up,
    w_down,
    out_gain,
):
    user_count, hist_len, model_width = history.shape
    head_count = model_width // HEAD
    experts = w_router.shape[1]
    dp_size = lax.axis_size("dp")
    ep_size = lax.axis_size("expert")
    nz = dp_size // 2
    relay = nz == 4
    me_dp = lax.axis_index("dp")
    me_ep = lax.axis_index("expert")
    z = me_dp // 2
    core = me_dp % 2
    row_total = user_count * CANDS
    slice_width = model_width // dp_size
    order = slot_order(nz)
    last = order[-1]
    blocks = [(j, o) for j in order for o in range(2)]
    spans = {
        j: slice(2 * i * slice_width, 2 * (i + 1) * slice_width) for i, j in enumerate(order)
    }

    block_ids = ((z - jnp.array([j for j, _ in blocks], jnp.int32)) % nz) * 2 + (
        core ^ jnp.array([o for _, o in blocks], jnp.int32)
    )

    def shifts(own):
        if relay:
            return {0: own, 1: dp_shift(own, 1), 3: dp_shift(own, 3)}
        return {j: dp_shift(own, j) if j else own for j in range(nz)}

    def relays(slots):
        if not relay:
            return slots
        payload = jnp.where(z == 1, slots[3], jnp.where(z == 2, slots[1], slots[0]))
        return {**slots, 2: dp_pairs(payload, RELAY_OUT)}

    items = jnp.stack(expert_exchange([pos_item] * ep_size))
    items = jnp.stack([items] + [dp_shift(items, j) for j in range(1, nz)])
    items = jnp.stack([items, core_swap(items)]).reshape(-1, model_width)

    gate_slots = relays(shifts(w_gate[0]))
    up_slots = relays(shifts(w_up[0]))
    down_slots = relays(shifts(w_down[0]))

    query_heads = user_query.reshape(user_count, head_count, HEAD)
    key_heads = history.reshape(user_count, hist_len, head_count, HEAD)
    scores = jnp.einsum(
        "uhd,uthd->uht", query_heads, key_heads, preferred_element_type=jnp.float32
    ) / math.sqrt(HEAD)
    live_mask = jnp.arange(hist_len, dtype=jnp.int32)[None, None, :] < lengths[:, None, None]
    scores = jnp.where(live_mask, scores, -1e30)
    top_val = jnp.max(scores, axis=-1, keepdims=True)
    weights = jnp.where(live_mask, jnp.exp(scores - top_val), 0.0)
    attn_probs = (weights / jnp.sum(weights, axis=-1, keepdims=True)).astype(jnp.bfloat16)
    context = jnp.einsum(
        "uht,uthd->uhd", attn_probs, key_heads, preferred_element_type=jnp.float32
    ).reshape(user_count, model_width)

    query_f, gain, router = pl.pallas_call(
        functools.partial(arrange_kernel, slice_width),
        out_shape=like(
            (user_query.shape, jnp.float32),
            ((1, model_width), jnp.float32),
            ((experts, model_width), jnp.bfloat16),
        ),
        in_specs=[SMEM, VMEM, VMEM, VMEM],
        out_specs=[VMEM] * 3,
        compiler_params=pltpu.CompilerParams(vmem_limit_bytes=2 << 20),
    )(block_ids, user_query, out_gain[None], w_router.T)
    owner = neg_index // user_count
    owner_dp, owner_ep = owner // ep_size, owner % ep_size
    slot = (((owner_dp % 2) ^ core) * nz + (z - owner_dp // 2) % nz) * ep_size + (owner_ep ^ me_ep)
    slot = slot * user_count + neg_index % user_count
    mine = jnp.arange(user_count, dtype=jnp.int32)[:, None]
    slot = jnp.concatenate([mine, slot], axis=1).reshape(row_total, 1)
    x_sum, normed = pl.pallas_call(
        functools.partial(rows_kernel, slice_width),
        out_shape=like(
            ((row_total, model_width), jnp.float32),
            ((row_total, model_width), jnp.bfloat16),
        ),
        in_specs=[SMEM, VMEM, VMEM, VMEM],
        out_specs=[VMEM] * 2,
        compiler_params=pltpu.CompilerParams(vmem_limit_bytes=8 << 20),
    )(block_ids, slot, items, context)
    rows_in = lax.optimization_barrier(
        jnp.concatenate(expert_exchange([normed] * ep_size))
    )

    logits = lax.dot_general(
        normed, router, (((1,), (1,)), ((), ())), preferred_element_type=jnp.float32
    )
    route_hot = routes[:, :, None] == jnp.arange(experts, dtype=jnp.int32)
    affinity = jax.nn.sigmoid(jnp.sum(jnp.where(route_hot, logits[:, None, :], 0.0), axis=-1))
    aff_total = jnp.sum(affinity, axis=1, keepdims=True)
    mix = affinity / aff_total
    mix_dense = jnp.sum(jnp.where(route_hot, mix[:, :, None], 0.0), axis=1)
    mix_rows = mix_dense.T
    mix_slots = jnp.stack(expert_exchange([mix_rows] * ep_size))
    mix_here = lax.dynamic_index_in_dim(mix_slots, me_ep, 1, keepdims=False).reshape(-1, 1)
    mix_cols = [
        lax.dynamic_index_in_dim(mix_dense, me_ep ^ k, 1, keepdims=True)
        for k in range(ep_size)
    ]

    def lay(slots, j, axis):
        return jnp.concatenate([slots[j], core_swap(slots[j])], axis=axis)

    def lay_all(slots):
        return jnp.concatenate([lay(slots, j, 0) for j in order])

    for slots in (gate_slots, up_slots):
        for j in order[:-1]:
            slots[j], _ = lax.optimization_barrier((slots[j], logits))
    for j in order[:-1]:
        down_slots[j], _ = lax.optimization_barrier((down_slots[j], logits))
    gate_full = lay_all(gate_slots)
    up_full = lay_all(up_slots)
    gate_pre = jnp.dot(rows_in, gate_full, preferred_element_type=jnp.float32)
    up_pre = jnp.dot(rows_in, up_full, preferred_element_type=jnp.float32)
    silu_val, silu_grad = silu_pair(gate_pre)
    hidden = (silu_val * up_pre).astype(jnp.bfloat16)
    hidden_mix = (mix_here * hidden.astype(jnp.float32)).astype(jnp.bfloat16)
    gate_slope = (mix_here * (up_pre * silu_grad)).astype(jnp.bfloat16)
    up_slope = (mix_here * silu_val).astype(jnp.bfloat16)
    hidden, hidden_mix, gate_slope, up_slope = lax.optimization_barrier(
        (hidden, hidden_mix, gate_slope, up_slope)
    )

    def returned(columns):
        out = jnp.dot(hidden, columns, preferred_element_type=jnp.float32)
        out = out.astype(jnp.bfloat16).reshape(ep_size, row_total, columns.shape[1])
        return expert_exchange(list(out))

    downs, outs = {}, {}
    for j in order:
        downs[j] = lay(down_slots, j, 1)
        if relay:
            outs[j] = returned(downs[j])
    if not relay:
        full = jnp.concatenate([downs[j] for j in order], axis=1)
        parts = returned(full)
        outs = {j: [part[:, spans[j]] for part in parts] for j in order}
    moe = []
    for j in order:
        term = x_sum[:, spans[j]]
        for col, part in zip(mix_cols, outs[j]):
            term = term + col * part.astype(jnp.float32)
        moe.append(term)
    h_rows = jnp.concatenate(moe, axis=1).reshape(user_count, CANDS, model_width)
    inv_rms = lax.rsqrt(jnp.mean(h_rows * h_rows, axis=-1, keepdims=True) + norm_eps)
    unit_rows = h_rows * inv_rms
    scored = unit_rows * gain
    listwise = jnp.sum(scored * query_f[:, None, :], axis=-1) / math.sqrt(model_width)
    top_list = jnp.max(listwise, axis=-1, keepdims=True)
    expo = jnp.exp(listwise - top_list)
    expo_total = jnp.sum(expo, axis=-1, keepdims=True)
    losses = jnp.log(expo_total[:, 0]) + top_list[:, 0] - listwise[:, 0]
    first_one = (jnp.arange(CANDS, dtype=jnp.int32) == 0).astype(jnp.float32)[None, :]
    d_list = loss_scale * (expo / expo_total - first_one)
    d_scored = d_list[..., None] * query_f[:, None, :] / math.sqrt(model_width)
    d_unit = d_scored * gain
    d_h = inv_rms * (d_unit - unit_rows * jnp.mean(d_unit * unit_rows, axis=-1, keepdims=True))
    d_h = d_h.reshape(row_total, model_width)
    d_send = d_h.astype(jnp.bfloat16)
    d_parts = {}
    if relay:
        for j in order:
            piece = d_send[:, spans[j]]
            d_parts[j] = jnp.concatenate(expert_exchange([piece] * ep_size))
    else:
        full = jnp.concatenate(expert_exchange([d_send] * ep_size))
        d_parts = {j: full[:, spans[j]] for j in order}

    contract_rows = (((0,), (0,)), ((), ()))
    contract_cols = (((1,), (1,)), ((), ()))

    def chip_terms(left, right):
        half = left.shape[1] // 2
        mine, other = left[:, :half], left[:, half:]
        part = lax.dot_general(other, right, contract_rows, preferred_element_type=jnp.float32)
        got = core_swap(part.astype(jnp.bfloat16))
        part = lax.dot_general(mine, right, contract_rows, preferred_element_type=jnp.float32)
        return (part + got.astype(jnp.float32)).astype(jnp.bfloat16)

    def send_relay(term):
        return dp_pairs(term, RELAY_BACK) if relay else None

    def send_rest(terms, own, relayed):
        if not relay:
            moved = [dp_shift(terms[j], nz - j) for j in range(1, nz)]
            return add_up(own(), *moved)
        zero = jnp.zeros_like(relayed)
        down = add_up(terms[1], jnp.where(z == 2, relayed, zero)).astype(jnp.bfloat16)
        up = add_up(terms[3], jnp.where(z == 1, relayed, zero)).astype(jnp.bfloat16)
        moved = dp_shift(down, 3), dp_shift(up, 1)
        base = lax.optimization_barrier(
            add_up(own(), jnp.where((z == 0) | (z == 3), relayed, zero))
        )
        return add_up(base, *moved)

    row_parts = {j: rows_in[:, spans[j]] for j in order}
    sent = order[:0:-1]
    down_terms = {}
    for j in sent:
        down_terms[j] = chip_terms(d_parts[j], hidden_mix)
    relay_down = send_relay(down_terms[last])
    sum_down = send_rest(down_terms, lambda: chip_terms(d_parts[0], hidden_mix), relay_down)
    d_hidden = sum(
        lax.dot_general(d_parts[j], downs[j], contract_cols, preferred_element_type=jnp.float32)
        for j in order[::-1]
    )
    d_gate = (d_hidden * gate_slope.astype(jnp.float32)).astype(jnp.bfloat16)
    d_up = (d_hidden * up_slope.astype(jnp.float32)).astype(jnp.bfloat16)
    gate_terms, up_terms = {}, {}
    for j in sent:
        gate_terms[j] = chip_terms(row_parts[j], d_gate)
        up_terms[j] = chip_terms(row_parts[j], d_up)
    relay_gate = send_relay(gate_terms[last])
    relay_up = send_relay(up_terms[last])
    sum_gate = send_rest(gate_terms, lambda: chip_terms(row_parts[0], d_gate), relay_gate)
    sum_up = send_rest(up_terms, lambda: chip_terms(row_parts[0], d_up), relay_up)
    sum_down = sum_down.T[None]
    sum_gate = sum_gate[None]
    sum_up = sum_up[None]

    d_dense = jnp.zeros((row_total, experts), jnp.float32)
    lanes = jnp.arange(experts, dtype=jnp.int32)[None, :]
    for k in range(ep_size):
        dots = sum(
            jnp.sum(d_h[:, spans[j]] * outs[j][k].astype(jnp.float32), axis=-1, keepdims=True)
            for j in order
        )
        d_dense = d_dense + jnp.where(lanes == (me_ep ^ k), dots, 0.0)
    mix_dot = jnp.sum(mix_dense * d_dense, axis=1, keepdims=True)
    aff_dense = jnp.sum(jnp.where(route_hot, affinity[:, :, None], 0.0), axis=1)
    d_logits = ((d_dense - mix_dot) / aff_total * aff_dense * (1.0 - aff_dense)).astype(
        jnp.bfloat16
    )
    arranged = lax.dot_general(d_logits, normed, contract_rows, preferred_element_type=jnp.float32)
    router_term = pl.pallas_call(
        functools.partial(place_kernel, slice_width),
        out_shape=jax.ShapeDtypeStruct(arranged.shape, jnp.float32),
        in_specs=[SMEM, VMEM],
        out_specs=VMEM,
        compiler_params=pltpu.CompilerParams(vmem_limit_bytes=2 << 20),
    )(block_ids, arranged)
    router_term = router_term + dp_xor(router_term, 1)
    router_term = router_term + dp_xor(router_term, 2)
    mask = 4
    while mask < dp_size:
        router_term = router_term + dp_xor(router_term, mask)
        mask *= 2
    mask = 1
    while mask < ep_size:
        router_term = router_term + expert_xor(router_term, mask)
        mask *= 2
    grad_router = router_term.T
    return (
        losses,
        sum_gate,
        sum_up,
        sum_down,
        grad_router,
    )


def solution(mesh):
    both = ("dp", "expert")
    placed = (
        P(both, None, None),
        P(both),
        P(both, None),
        P(both, None),
        P(both, None),
        P(both, None),
        P(),
        P("expert", "dp", None),
        P("expert", "dp", None),
        P("expert", None, "dp"),
        P(),
    )
    return jax.shard_map(
        local,
        mesh=mesh,
        in_specs=placed,
        out_specs=(
            P(both),
            P("expert", "dp", None),
            P("expert", "dp", None),
            P("expert", None, "dp"),
            P(),
        ),
        check_vma=False,
    )
```

time: 286 us -> 290 us (1.014)
  starting transfers between devices: 68.4 us -> 98.8 us
  waiting for transfers between devices: 150 us -> 130 us
  other arithmetic: 24.2 us -> 14.2 us
  matrix products: 29.6 us -> 35.1 us
  local copies, waits for them, and re-layouts: 11.7 us -> 6.7 us
    ppermute x23 -> x35, starting transfers between devices: 26.1 us -> 44 us  [expert_xor(): return lax.ppermute(value, 'expert', [(i, i ^ mask) for i in range(size)])]
    ppermute x23 -> x35, waiting for transfers between devices: 50.3 us -> 33 us  [expert_xor(): return lax.ppermute(value, 'expert', [(i, i ^ mask) for i in range(size)])]
    ppermute x6, waiting for transfers between devices: 26.3 us -> 42.1 us  [dp_pairs(): lax.ppermute(value, 'dp', [(2 * z + c, 2 * t + c) for z, t in enumerate(t...]
    ppermute x15, waiting for transfers between devices: 62.2 us -> 48.8 us  [dp_shift(): lax.ppermute(value, 'dp', [(2 * z + c, 2 * ((z + step) % nz) + c) for z i...]
    dot_general x6 -> x12, matrix products: 3.68 us -> 8.74 us  [chip_terms(): lax.dot_general(mine, right, contract_rows, preferred_element_type=jnp.fl...]
    ppermute x3, starting transfers between devices: 1.41 us -> 5.43 us  [dp_xor(): return lax.ppermute(value, 'dp', [(i, i ^ mask) for i in range(size)])]
    ppermute x15, starting transfers between devices: 31.6 us -> 35.6 us  [dp_shift(): lax.ppermute(value, 'dp', [(2 * z + c, 2 * ((z + step) % nz) + c) for z i...]
    convert_element_type x5 -> x0, other arithmetic: 3.1 us -> none  [the longest x3 2.26 us: send_rest(): add_up(by_chip[1], jnp.where(z == 2, relayed, zero)).astype(jnp.bfloat16)]
  transfers between devices with their start and end apart: 66 -> 84, of which waited for: 29 -> 33; matrix products, arithmetic and copies ran while one was open for 18% -> 16% of each run, Pallas kernels for 0% -> 1%
where the time goes in v2:
time: 290 us; the launch traced here: 289 us
  waiting for transfers between devices  130 us (45%)
  starting transfers between devices  98.8 us (34%)
  matrix products  35.1 us (12%)
  other arithmetic  14.2 us (5%)
  local copies, waits for them, and re-layouts  6.7 us (2%)
    ppermute x15, waiting for transfers between devices, dp_shift(): lax.ppermute(value, 'dp', [(2 * z + c, 2 * ((z + step) % nz) + c) for z i...  48.8 us
    ppermute x35, starting transfers between devices, expert_xor(): return lax.ppermute(value, 'expert', [(i, i ^ mask) for i in range(size)])  44 us
    ppermute x6, waiting for transfers between devices, dp_pairs(): lax.ppermute(value, 'dp', [(2 * z + c, 2 * t + c) for z, t in enumerate(t...  42.1 us
    ppermute x15, starting transfers between devices, dp_shift(): lax.ppermute(value, 'dp', [(2 * z + c, 2 * ((z + step) % nz) + c) for z i...  35.6 us
    ppermute x35, waiting for transfers between devices, expert_xor(): return lax.ppermute(value, 'expert', [(i, i ^ mask) for i in range(size)])  33 us
    dot_general x12, matrix products, chip_terms(): lax.dot_general(mine, right, contract_rows, preferred_element_type=jnp.fl...  8.74 us
    ppermute x6, starting transfers between devices, dp_pairs(): lax.ppermute(value, 'dp', [(2 * z + c, 2 * t + c) for z, t in enumerate(t...  8.4 us
  transfers between devices with their start and end apart: 84, of which 33 were waited for; matrix products, arithmetic and copies ran while one was open for 16% of the time, Pallas kernels for 1%

profile of v2, /device:TPU:0, one launch (start us, length us, event | category | flops | bytes accessed | tf_op | source)
XLA Modules:
  0.0 289.4 jit_solution(6553725017148339160)
XLA Ops:
  0.6 3.0 %collective-permute-start = (bf16[2,2048]{1,0:T(2,128)(2,1)}, bf16[2,2048]{1,0:T(2,128)(2,1)S(1)}, u32[]{:S(2)}, u32[]{:S(2)}) collective-permute-start(bf16[2,2048]{1,0:T(2,128)(2,1)} %param.16), channel_id=1, source_target_pairs={{0,1},{1,0},{2,3},{3,2},{4,5},{5,4},{6,7},{7,6},{8,9},{9,8},{10,11... | collective-permute-start | bytes 24584 | tf_op jit(solution)/shard_map/ppermute | solution.py:50
  3.7 1.5 collective-permute-start.1
  5.2 2.0 collective-permute-start.31
  7.2 2.0 collective-permute-start.36
  10.7 5.6 %fusion.2 = f32[2,16,1,1024]{3,2,1,0:T(1,128)S(1)} fusion(bf16[2,16,128,1]{2,3,1,0:T(2,128)(2,1)S(1)} %reshape.337, bf16[2,1024,2048]{2,1,0:T(8,128)(2,1)} %param.13), kind=kOutput, calls=%fused_computation.2 | convolution fusion | flops 8388608 | bytes 8527872 | tf_op jit(solution)/shard_map/uhd,uthd->uht/dot_general | solution.py:180
  16.7 5.1 %fusion.4 = f32[2,16,1,128]{3,2,1,0:T(1,128)S(1)} fusion(bf16[2,16,1024,1]{2,1,0,3:T(8,128)(2,1)S(1)} %fusion.50, bf16[2,1024,2048]{2,1,0:T(8,128)(2,1)} %param.13), kind=kOutput, calls=%fused_computation.4 | convolution fusion | flops 8388608 | bytes 8470528 | tf_op jit(solution)/shard_map/uht,uthd->uhd/dot_general | solution.py:188
  25.2 2.6 collective-permute-start.4
  29.1 1.7 collective-permute-done.3
  35.7 1.5 collective-permute-start.24
  37.2 1.5 collective-permute-start.25
  39.3 3.5 %collective-permute-start.20 = (bf16[256,768]{1,0:T(8,128)(2,1)S(1)}, bf16[256,768]{1,0:T(8,128)(2,1)S(1)}, u32[]{:S(2)}, u32[]{:S(2)}) collective-permute-start(bf16[256,768]{1,0:T(8,128)(2,1)S(1)} %bitcast.149), channel_id=1, source_target_pairs={{0,24},{4,28},{8,0},{12,4},{16,8},{20,12},{24,16},{28,20},{1,25},{... | collective-permute-start | bytes 1179656 | tf_op jit(solution)/shard_map/ppermute | solution.py:27
  42.8 2.6 collective-permute-start.26
  45.4 1.9 collective-permute-done.26
  47.3 8.4 %collective-permute-start.11 = (bf16[256,768]{1,0:T(8,128)(2,1)S(1)}, bf16[256,768]{1,0:T(8,128)(2,1)S(1)}, u32[]{:S(2)}, u32[]{:S(2)}) collective-permute-start(bf16[256,768]{1,0:T(8,128)(2,1)S(1)} %bitcast.152), channel_id=1, source_target_pairs={{0,8},{4,12},{8,16},{12,20},{16,24},{20,28},{24,0},{28,4},{1,9},{5... | collective-permute-start | bytes 1179656 | tf_op jit(solution)/shard_map/ppermute | solution.py:27
  56.6 10.7 %collective-permute-done.20 = bf16[256,768]{1,0:T(8,128)(2,1)S(1)} collective-permute-done((bf16[256,768]{1,0:T(8,128)(2,1)S(1)}, bf16[256,768]{1,0:T(8,128)(2,1)S(1)}, u32[]{:S(2)}, u32[]{:S(2)}) %collective-permute-start.20) | collective-permute-done | bytes 393248 | tf_op jit(solution)/shard_map/ppermute | solution.py:27
  67.2 1.9 collective-permute-start.7
  69.2 1.6 collective-permute-start.8
  70.8 4.3 %collective-permute-done.13 = bf16[256,768]{1,0:T(8,128)(2,1)S(1)} collective-permute-done((bf16[256,768]{1,0:T(8,128)(2,1)S(1)}, bf16[256,768]{1,0:T(8,128)(2,1)S(1)}, u32[]{:S(2)}, u32[]{:S(2)}) %collective-permute-start.13) | collective-permute-done | bytes 393248 | tf_op jit(solution)/shard_map/ppermute | solution.py:27
  75.1 2.2 collective-permute-start.9
  80.9 9.7 %collective-permute-done.8 = bf16[128,2048]{1,0:T(8,128)(2,1)S(1)} collective-permute-done((bf16[128,2048]{1,0:T(8,128)(2,1)S(1)}, bf16[128,2048]{1,0:T(8,128)(2,1)S(1)}, u32[]{:S(2)}, u32[]{:S(2)}) %collective-permute-start.8) | collective-permute-done | bytes 524320 | tf_op jit(solution)/shard_map/ppermute | solution.py:50
  90.7 1.5 collective-permute-start.22
  92.6 3.2 %collective-permute-start.41 = (bf16[768,256]{1,0:T(8,128)(2,1)S(1)}, bf16[768,256]{1,0:T(8,128)(2,1)S(1)}, u32[]{:S(2)}, u32[]{:S(2)}) collective-permute-start(bf16[768,256]{1,0:T(8,128)(2,1)S(1)} %select_select_fusion), channel_id=1, source_target_pairs={{0,16},{4,20},{8,0},{12,4},{16,24},{20,28},{24,8},{28,12},{1,17},{... | collective-permute-start | bytes 1179656 | tf_op jit(solution)/shard_map/ppermute | solution.py:33
  96.0 5.6 %collective-permute-done.22 = bf16[256,768]{1,0:T(8,128)(2,1)S(1)} collective-permute-done((bf16[256,768]{1,0:T(8,128)(2,1)S(1)}, bf16[256,768]{1,0:T(8,128)(2,1)S(1)}, u32[]{:S(2)}, u32[]{:S(2)}) %collective-permute-start.22) | collective-permute-done | bytes 393248 | tf_op jit(solution)/shard_map/ppermute | solution.py:33
  101.6 13.7 %collective-permute-done.41 = bf16[768,256]{1,0:T(8,128)(2,1)S(1)} collective-permute-done((bf16[768,256]{1,0:T(8,128)(2,1)S(1)}, bf16[768,256]{1,0:T(8,128)(2,1)S(1)}, u32[]{:S(2)}, u32[]{:S(2)}) %collective-permute-start.41) | collective-permute-done | bytes 393248 | tf_op jit(solution)/shard_map/ppermute | solution.py:33
  116.2 2.0 collective-permute-done.16
  118.2 1.8 fusion.171
  120.0 3.5 %multiply_convert_fusion.4 = (bf16[512,768]{1,0:T(8,128)(2,1)S(1)}, bf16[512,768]{1,0:T(8,128)(2,1)S(1)}, bf16[512,768]{1,0:T(8,128)(2,1)}, bf16[512,768]{1,0:T(8,128)(2,1)}) fusion(f32[512]{0:T(512)S(1)} %bitcast.179, f32[512,768]{1,0:T(8,128)S(1)} %fusion.171, bf16[512,2048]{1,0:T(8,128)(2,1)S(1)} %pad_maximum_fusion, ...), kind=kOutput, calls=%fused_computation.14 | convolution fusion | flops 1617690624 | bytes 9963520 | tf_op jit(solution)/shard_map/dot_general | solution.py:253
  124.1 1.5 collective-permute-start.33
  128.3 1.5 collective-permute-start.38
  136.3 1.6 collective-permute-start.45
  137.9 2.0 collective-permute-done.39
  141.9 1.6 collective-permute-start.30
  143.7 1.8 collective-permute-done.44
  145.5 2.0 collective-permute-done.28
  147.6 3.0 %collective-permute-done.29 = bf16[128,512]{1,0:T(8,128)(2,1)S(1)} collective-permute-done((bf16[128,512]{1,0:T(8,128)(2,1)S(1)}, bf16[128,512]{1,0:T(8,128)(2,1)S(1)}, u32[]{:S(2)}, u32[]{:S(2)}) %collective-permute-start.29) | collective-permute-done | bytes 131104 | tf_op jit(solution)/shard_map/ppermute | solution.py:50
  153.1 1.7 fusion.66
  154.8 1.4 fusion.58
  159.2 1.7 collective-permute-start.51
  161.4 2.6 collective-permute-start.80
  164.1 1.8 collective-permute-done.80
  165.9 2.8 collective-permute-start.81
  169.2 1.6 collective-permute-done.81
  170.8 1.5 collective-permute-start.53
  172.3 1.5 collective-permute-start.54
  174.4 1.5 collective-permute-start.47
  178.1 1.8 collective-permute-start.56
  181.8 2.3 collective-permute-done.55
  184.1 1.4 collective-permute-start.48
  185.6 1.7 collective-permute-done.56
  188.6 1.4 collective-permute-done.48
  197.9 2.5 collective-permute-done.83
  201.9 1.8 collective-permute-start.74
  205.6 9.3 %collective-permute-done.74 = bf16[256,768]{1,0:T(8,128)(2,1)S(1)} collective-permute-done((bf16[256,768]{1,0:T(8,128)(2,1)S(1)}, bf16[256,768]{1,0:T(8,128)(2,1)S(1)}, u32[]{:S(2)}, u32[]{:S(2)}) %collective-permute-start.74) | collective-permute-done | bytes 393248 | tf_op jit(solution)/shard_map/ppermute | solution.py:33
  216.2 7.1 %collective-permute-done.67 = bf16[256,768]{1,0:T(8,128)(2,1)S(1)} collective-permute-done((bf16[256,768]{1,0:T(8,128)(2,1)S(1)}, bf16[256,768]{1,0:T(8,128)(2,1)S(1)}, u32[]{:S(2)}, u32[]{:S(2)}) %collective-permute-start.67) | collective-permute-done | bytes 393248 | tf_op jit(solution)/shard_map/ppermute | solution.py:33
  224.3 6.5 %collective-permute-done.60 = bf16[256,768]{1,0:T(8,128)(2,1)S(1)} collective-permute-done((bf16[256,768]{1,0:T(8,128)(2,1)S(1)}, bf16[256,768]{1,0:T(8,128)(2,1)S(1)}, u32[]{:S(2)}, u32[]{:S(2)}) %collective-permute-start.60) | collective-permute-done | bytes 393248 | tf_op jit(solution)/shard_map/ppermute | solution.py:33
  233.0 2.1 collective-permute-start.76
  236.8 3.8 %collective-permute-start.69 = (bf16[256,768]{1,0:T(8,128)(2,1)}, bf16[256,768]{1,0:T(8,128)(2,1)S(1)}, u32[]{:S(2)}, u32[]{:S(2)}) collective-permute-start(bf16[256,768]{1,0:T(8,128)(2,1)} %fusion.28), channel_id=1, source_target_pairs={{0,24},{4,28},{8,0},{12,4},{16,8},{20,12},{24,16},{28,20},{1,25},{... | collective-permute-start | bytes 1179656 | tf_op jit(solution)/shard_map/ppermute | solution.py:27
  242.9 3.8 %collective-permute-start.62 = (bf16[256,768]{1,0:T(8,128)(2,1)}, bf16[256,768]{1,0:T(8,128)(2,1)}, u32[]{:S(2)}, u32[]{:S(2)}) collective-permute-start(bf16[256,768]{1,0:T(8,128)(2,1)} %fusion.16), channel_id=1, source_target_pairs={{0,24},{4,28},{8,0},{12,4},{16,8},{20,12},{24,16},{28,20},{1,25},{... | collective-permute-start | bytes 1179656 | tf_op jit(solution)/shard_map/ppermute | solution.py:27
  247.9 5.8 %collective-permute-start.64 = (bf16[256,768]{1,0:T(8,128)(2,1)}, bf16[256,768]{1,0:T(8,128)(2,1)}, u32[]{:S(2)}, u32[]{:S(2)}) collective-permute-start(bf16[256,768]{1,0:T(8,128)(2,1)} %fusion.20), channel_id=1, source_target_pairs={{0,8},{4,12},{8,16},{12,20},{16,24},{20,28},{24,0},{28,4},{1,9},{5... | collective-permute-start | bytes 1179656 | tf_op jit(solution)/shard_map/ppermute | solution.py:27
  255.7 7.1 %collective-permute-done.69 = bf16[256,768]{1,0:T(8,128)(2,1)S(1)} collective-permute-done((bf16[256,768]{1,0:T(8,128)(2,1)}, bf16[256,768]{1,0:T(8,128)(2,1)S(1)}, u32[]{:S(2)}, u32[]{:S(2)}) %collective-permute-start.69) | collective-permute-done | bytes 393248 | tf_op jit(solution)/shard_map/ppermute | solution.py:27
  262.9 8.4 %collective-permute-done.71 = bf16[256,768]{1,0:T(8,128)(2,1)S(1)} collective-permute-done((bf16[256,768]{1,0:T(8,128)(2,1)}, bf16[256,768]{1,0:T(8,128)(2,1)S(1)}, u32[]{:S(2)}, u32[]{:S(2)}) %collective-permute-start.71) | collective-permute-done | bytes 393248 | tf_op jit(solution)/shard_map/ppermute | solution.py:27
  272.3 6.3 %collective-permute-done.62 = bf16[256,768]{1,0:T(8,128)(2,1)} collective-permute-done((bf16[256,768]{1,0:T(8,128)(2,1)}, bf16[256,768]{1,0:T(8,128)(2,1)}, u32[]{:S(2)}, u32[]{:S(2)}) %collective-permute-start.62) | collective-permute-done | bytes 393248 | tf_op jit(solution)/shard_map/ppermute | solution.py:27
  278.6 8.7 %collective-permute-done.64 = bf16[256,768]{1,0:T(8,128)(2,1)} collective-permute-done((bf16[256,768]{1,0:T(8,128)(2,1)}, bf16[256,768]{1,0:T(8,128)(2,1)}, u32[]{:S(2)}, u32[]{:S(2)}) %collective-permute-start.64) | collective-permute-done | bytes 393248 | tf_op jit(solution)/shard_map/ppermute | solution.py:27
  287.3 2.1 add_bitcast_fusion.2
  (347 shorter events, 65.5 us)
Async XLA Ops:
  0.6 24.4 %collective-permute-start = (bf16[2,2048]{1,0:T(2,128)(2,1)}, bf16[2,2048]{1,0:T(2,128)(2,1)S(1)}, u32[]{:S(2)}, u32[]{:S(2)}) collective-permute-start(bf16[2,2048]{1,0:T(2,128)(2,1)} %param.16), channel_id=1, source_target_pairs={{0,1},{1,0},{2,3},{3,2},{4,5},{5,4},{6,7},{7,6},{8,9},{9,8},{10,11... | collective-permute-start | bytes 24584 | tf_op jit(solution)/shard_map/ppermute | solution.py:50
  3.7 21.3 %collective-permute-start.1 = (bf16[2,2048]{1,0:T(2,128)(2,1)}, bf16[2,2048]{1,0:T(2,128)(2,1)S(1)}, u32[]{:S(2)}, u32[]{:S(2)}) collective-permute-start(bf16[2,2048]{1,0:T(2,128)(2,1)} %param.16), channel_id=1, source_target_pairs={{0,2},{1,3},{2,0},{3,1},{4,6},{5,7},{6,4},{7,5},{8,10},{9,11},{10,... | collective-permute-start | bytes 24584 | tf_op jit(solution)/shard_map/ppermute | solution.py:50
  5.2 19.8 %collective-permute-start.2 = (bf16[2,2048]{1,0:T(2,128)(2,1)}, bf16[2,2048]{1,0:T(2,128)(2,1)S(1)}, u32[]{:S(2)}, u32[]{:S(2)}) collective-permute-start(bf16[2,2048]{1,0:T(2,128)(2,1)} %param.16), channel_id=1, source_target_pairs={{0,3},{1,2},{2,1},{3,0},{4,7},{5,6},{6,5},{7,4},{8,11},{9,10},{10,... | collective-permute-start | bytes 24584 | tf_op jit(solution)/shard_map/ppermute | solution.py:50
  5.2 50.5 %collective-permute-start.31 = (bf16[768,256]{1,0:T(8,128)(2,1)}, bf16[768,256]{1,0:T(8,128)(2,1)}, u32[]{:S(2)}, u32[]{:S(2)}) collective-permute-start(bf16[768,256]{1,0:T(8,128)(2,1)} %bitcast.155), channel_id=1, source_target_pairs={{0,8},{4,12},{8,16},{12,20},{16,24},{20,28},{24,0},{28,4},{1,9},{5... | collective-permute-start | bytes 1179656 | tf_op jit(solution)/shard_map/ppermute | solution.py:27
  7.2 48.6 %collective-permute-start.36 = (bf16[768,256]{1,0:T(8,128)(2,1)}, bf16[768,256]{1,0:T(8,128)(2,1)S(1)}, u32[]{:S(2)}, u32[]{:S(2)}) collective-permute-start(bf16[768,256]{1,0:T(8,128)(2,1)} %bitcast.156), channel_id=1, source_target_pairs={{0,24},{4,28},{8,0},{12,4},{16,8},{20,12},{24,16},{28,20},{1,25},{... | collective-permute-start | bytes 1179656 | tf_op jit(solution)/shard_map/ppermute | solution.py:27
  30.9 25.1 %collective-permute-start.18 = (bf16[256,768]{1,0:T(8,128)(2,1)S(1)}, bf16[256,768]{1,0:T(8,128)(2,1)}, u32[]{:S(2)}, u32[]{:S(2)}) collective-permute-start(bf16[256,768]{1,0:T(8,128)(2,1)S(1)} %bitcast.147), channel_id=1, source_target_pairs={{0,8},{4,12},{8,16},{12,20},{16,24},{20,28},{24,0},{28,4},{1,9},{5... | collective-permute-start | bytes 1179656 | tf_op jit(solution)/shard_map/ppermute | solution.py:27
  39.3 27.9 %collective-permute-start.20 = (bf16[256,768]{1,0:T(8,128)(2,1)S(1)}, bf16[256,768]{1,0:T(8,128)(2,1)S(1)}, u32[]{:S(2)}, u32[]{:S(2)}) collective-permute-start(bf16[256,768]{1,0:T(8,128)(2,1)S(1)} %bitcast.149), channel_id=1, source_target_pairs={{0,24},{4,28},{8,0},{12,4},{16,8},{20,12},{24,16},{28,20},{1,25},{... | collective-permute-start | bytes 1179656 | tf_op jit(solution)/shard_map/ppermute | solution.py:27
  47.3 21.9 %collective-permute-start.11 = (bf16[256,768]{1,0:T(8,128)(2,1)S(1)}, bf16[256,768]{1,0:T(8,128)(2,1)S(1)}, u32[]{:S(2)}, u32[]{:S(2)}) collective-permute-start(bf16[256,768]{1,0:T(8,128)(2,1)S(1)} %bitcast.152), channel_id=1, source_target_pairs={{0,8},{4,12},{8,16},{12,20},{16,24},{20,28},{24,0},{28,4},{1,9},{5... | collective-permute-start | bytes 1179656 | tf_op jit(solution)/shard_map/ppermute | solution.py:27
  55.7 19.3 %collective-permute-start.13 = (bf16[256,768]{1,0:T(8,128)(2,1)S(1)}, bf16[256,768]{1,0:T(8,128)(2,1)S(1)}, u32[]{:S(2)}, u32[]{:S(2)}) collective-permute-start(bf16[256,768]{1,0:T(8,128)(2,1)S(1)} %bitcast.153), channel_id=1, source_target_pairs={{0,24},{4,28},{8,0},{12,4},{16,8},{20,12},{24,16},{28,20},{1,25},{... | collective-permute-start | bytes 1179656 | tf_op jit(solution)/shard_map/ppermute | solution.py:27
  55.8 22.6 %collective-permute-start.17 = (bf16[256,768]{1,0:T(8,128)(2,1)S(1)}, bf16[256,768]{1,0:T(8,128)(2,1)S(1)}, u32[]{:S(2)}, u32[]{:S(2)}) collective-permute-start(bf16[256,768]{1,0:T(8,128)(2,1)S(1)} %bitcast.150), channel_id=1, source_target_pairs={{0,4},{4,0},{8,12},{12,8},{16,20},{20,16},{24,28},{28,24},{1,5},{5... | collective-permute-start | bytes 1179656 | tf_op jit(solution)/shard_map/ppermute | solution.py:40
  56.0 23.6 %collective-permute-start.10 = (bf16[256,768]{1,0:T(8,128)(2,1)S(1)}, bf16[256,768]{1,0:T(8,128)(2,1)S(1)}, u32[]{:S(2)}, u32[]{:S(2)}) collective-permute-start(bf16[256,768]{1,0:T(8,128)(2,1)S(1)} %bitcast.154), channel_id=1, source_target_pairs={{0,4},{4,0},{8,12},{12,8},{16,20},{20,16},{24,28},{28,24},{1,5},{5... | collective-permute-start | bytes 1179656 | tf_op jit(solution)/shard_map/ppermute | solution.py:40
  67.2 13.2 %collective-permute-start.7 = (bf16[128,2048]{1,0:T(8,128)(2,1)S(1)}, bf16[128,2048]{1,0:T(8,128)(2,1)S(1)}, u32[]{:S(2)}, u32[]{:S(2)}) collective-permute-start(bf16[128,2048]{1,0:T(8,128)(2,1)S(1)} %get-tuple-element.24), channel_id=1, source_target_pairs={{0,1},{1,0},{2,3},{3,2},{4,5},{5,4},{6,7},{7,6},{8,9},{9,8},{10,11... | collective-permute-start | bytes 1572872 | tf_op jit(solution)/shard_map/ppermute | solution.py:50
  69.2 21.5 %collective-permute-start.8 = (bf16[128,2048]{1,0:T(8,128)(2,1)S(1)}, bf16[128,2048]{1,0:T(8,128)(2,1)S(1)}, u32[]{:S(2)}, u32[]{:S(2)}) collective-permute-start(bf16[128,2048]{1,0:T(8,128)(2,1)S(1)} %get-tuple-element.24), channel_id=1, source_target_pairs={{0,2},{1,3},{2,0},{3,1},{4,6},{5,7},{6,4},{7,5},{8,10},{9,11},{10,... | collective-permute-start | bytes 1572872 | tf_op jit(solution)/shard_map/ppermute | solution.py:50
  75.1 17.1 %collective-permute-start.9 = (bf16[128,2048]{1,0:T(8,128)(2,1)S(1)}, bf16[128,2048]{1,0:T(8,128)(2,1)S(1)}, u32[]{:S(2)}, u32[]{:S(2)}) collective-permute-start(bf16[128,2048]{1,0:T(8,128)(2,1)S(1)} %get-tuple-element.24), channel_id=1, source_target_pairs={{0,3},{1,2},{2,1},{3,0},{4,7},{5,6},{6,5},{7,4},{8,11},{9,10},{10,... | collective-permute-start | bytes 1572872 | tf_op jit(solution)/shard_map/ppermute | solution.py:50
  79.6 12.9 %collective-permute-start.19 = (bf16[256,768]{1,0:T(8,128)(2,1)}, bf16[256,768]{1,0:T(8,128)(2,1)S(1)}, u32[]{:S(2)}, u32[]{:S(2)}) collective-permute-start(bf16[256,768]{1,0:T(8,128)(2,1)} %collective-permute-done.18), channel_id=1, source_target_pairs={{0,4},{4,0},{8,12},{12,8},{16,20},{20,16},{24,28},{28,24},{1,5},{5... | collective-permute-start | bytes 1179656 | tf_op jit(solution)/shard_map/ppermute | solution.py:40
  80.2 12.4 %collective-permute-start.12 = (bf16[256,768]{1,0:T(8,128)(2,1)S(1)}, bf16[256,768]{1,0:T(8,128)(2,1)S(1)}, u32[]{:S(2)}, u32[]{:S(2)}) collective-permute-start(bf16[256,768]{1,0:T(8,128)(2,1)S(1)} %collective-permute-done.11), channel_id=1, source_target_pairs={{0,4},{4,0},{8,12},{12,8},{16,20},{20,16},{24,28},{28,24},{1,5},{5... | collective-permute-start | bytes 1179656 | tf_op jit(solution)/shard_map/ppermute | solution.py:40
  80.4 15.4 %collective-permute-start.21 = (bf16[256,768]{1,0:T(8,128)(2,1)S(1)}, bf16[256,768]{1,0:T(8,128)(2,1)S(1)}, u32[]{:S(2)}, u32[]{:S(2)}) collective-permute-start(bf16[256,768]{1,0:T(8,128)(2,1)S(1)} %collective-permute-done.20), channel_id=1, source_target_pairs={{0,4},{4,0},{8,12},{12,8},{16,20},{20,16},{24,28},{28,24},{1,5},{5... | collective-permute-start | bytes 1179656 | tf_op jit(solution)/shard_map/ppermute | solution.py:40
  90.7 10.9 %collective-permute-start.22 = (bf16[256,768]{1,0:T(8,128)(2,1)S(1)}, bf16[256,768]{1,0:T(8,128)(2,1)S(1)}, u32[]{:S(2)}, u32[]{:S(2)}) collective-permute-start(bf16[256,768]{1,0:T(8,128)(2,1)S(1)} %select_select_fusion.1), channel_id=1, source_target_pairs={{0,16},{4,20},{8,0},{12,4},{16,24},{20,28},{24,8},{28,12},{1,17},{... | collective-permute-start | bytes 1179656 | tf_op jit(solution)/shard_map/ppermute | solution.py:33
  92.2 23.1 %collective-permute-start.14 = (bf16[256,768]{1,0:T(8,128)(2,1)S(1)}, bf16[256,768]{1,0:T(8,128)(2,1)S(1)}, u32[]{:S(2)}, u32[]{:S(2)}) collective-permute-start(bf16[256,768]{1,0:T(8,128)(2,1)S(1)} %collective-permute-done.13), channel_id=1, source_target_pairs={{0,4},{4,0},{8,12},{12,8},{16,20},{20,16},{24,28},{28,24},{1,5},{5... | collective-permute-start | bytes 1179656 | tf_op jit(solution)/shard_map/ppermute | solution.py:40
  92.5 23.4 %collective-permute-start.15 = (bf16[256,768]{1,0:T(8,128)(2,1)S(1)}, bf16[256,768]{1,0:T(8,128)(2,1)S(1)}, u32[]{:S(2)}, u32[]{:S(2)}) collective-permute-start(bf16[256,768]{1,0:T(8,128)(2,1)S(1)} %select_select_fusion.2), channel_id=1, source_target_pairs={{0,16},{4,20},{8,0},{12,4},{16,24},{20,28},{24,8},{28,12},{1,17},{... | collective-permute-start | bytes 1179656 | tf_op jit(solution)/shard_map/ppermute | solution.py:33
  92.6 22.7 %collective-permute-start.41 = (bf16[768,256]{1,0:T(8,128)(2,1)S(1)}, bf16[768,256]{1,0:T(8,128)(2,1)S(1)}, u32[]{:S(2)}, u32[]{:S(2)}) collective-permute-start(bf16[768,256]{1,0:T(8,128)(2,1)S(1)} %select_select_fusion), channel_id=1, source_target_pairs={{0,16},{4,20},{8,0},{12,4},{16,24},{20,28},{24,8},{28,12},{1,17},{... | collective-permute-start | bytes 1179656 | tf_op jit(solution)/shard_map/ppermute | solution.py:33
  95.9 20.2 %collective-permute-start.32 = (bf16[768,256]{1,0:T(8,128)(2,1)}, bf16[768,256]{1,0:T(8,128)(2,1)S(1)}, u32[]{:S(2)}, u32[]{:S(2)}) collective-permute-start(bf16[768,256]{1,0:T(8,128)(2,1)} %collective-permute-done.31), channel_id=1, source_target_pairs={{0,4},{4,0},{8,12},{12,8},{16,20},{20,16},{24,28},{28,24},{1,5},{5... | collective-permute-start | bytes 1179656 | tf_op jit(solution)/shard_map/ppermute | solution.py:40
  101.6 14.6 %collective-permute-start.37 = (bf16[768,256]{1,0:T(8,128)(2,1)S(1)}, bf16[768,256]{1,0:T(8,128)(2,1)S(1)}, u32[]{:S(2)}, u32[]{:S(2)}) collective-permute-start(bf16[768,256]{1,0:T(8,128)(2,1)S(1)} %collective-permute-done.36), channel_id=1, source_target_pairs={{0,4},{4,0},{8,12},{12,8},{16,20},{20,16},{24,28},{28,24},{1,5},{5... | collective-permute-start | bytes 1179656 | tf_op jit(solution)/shard_map/ppermute | solution.py:40
  115.4 14.5 %collective-permute-start.42 = (bf16[768,256]{1,0:T(8,128)(2,1)S(1)}, bf16[768,256]{1,0:T(8,128)(2,1)S(1)}, u32[]{:S(2)}, u32[]{:S(2)}) collective-permute-start(bf16[768,256]{1,0:T(8,128)(2,1)S(1)} %collective-permute-done.41), channel_id=1, source_target_pairs={{0,4},{4,0},{8,12},{12,8},{16,20},{20,16},{24,28},{28,24},{1,5},{5... | collective-permute-start | bytes 1179656 | tf_op jit(solution)/shard_map/ppermute | solution.py:40
  124.1 7.7 %collective-permute-start.33 = (bf16[128,512]{1,0:T(8,128)(2,1)S(1)}, bf16[128,512]{1,0:T(8,128)(2,1)S(1)}, u32[]{:S(2)}, u32[]{:S(2)}) collective-permute-start(bf16[128,512]{1,0:T(8,128)(2,1)S(1)} %get-tuple-element.98), channel_id=1, source_target_pairs={{0,1},{1,0},{2,3},{3,2},{4,5},{5,4},{6,7},{7,6},{8,9},{9,8},{10,11... | collective-permute-start | bytes 393224 | tf_op jit(solution)/shard_map/ppermute | solution.py:50
  125.6 8.6 %collective-permute-start.34 = (bf16[128,512]{1,0:T(8,128)(2,1)S(1)}, bf16[128,512]{1,0:T(8,128)(2,1)S(1)}, u32[]{:S(2)}, u32[]{:S(2)}) collective-permute-start(bf16[128,512]{1,0:T(8,128)(2,1)S(1)} %get-tuple-element.97), channel_id=1, source_target_pairs={{0,2},{1,3},{2,0},{3,1},{4,6},{5,7},{6,4},{7,5},{8,10},{9,11},{10,... | collective-permute-start | bytes 393224 | tf_op jit(solution)/shard_map/ppermute | solution.py:50
  126.4 8.3 %collective-permute-start.35 = (bf16[128,512]{1,0:T(8,128)(2,1)S(1)}, bf16[128,512]{1,0:T(8,128)(2,1)S(1)}, u32[]{:S(2)}, u32[]{:S(2)}) collective-permute-start(bf16[128,512]{1,0:T(8,128)(2,1)S(1)} %get-tuple-element.96), channel_id=1, source_target_pairs={{0,3},{1,2},{2,1},{3,0},{4,7},{5,6},{6,5},{7,4},{8,11},{9,10},{10,... | collective-permute-start | bytes 393224 | tf_op jit(solution)/shard_map/ppermute | solution.py:50
  128.3 8.0 %collective-permute-start.38 = (bf16[128,512]{1,0:T(8,128)(2,1)S(1)}, bf16[128,512]{1,0:T(8,128)(2,1)S(1)}, u32[]{:S(2)}, u32[]{:S(2)}) collective-permute-start(bf16[128,512]{1,0:T(8,128)(2,1)S(1)} %get-tuple-element.101), channel_id=1, source_target_pairs={{0,1},{1,0},{2,3},{3,2},{4,5},{5,4},{6,7},{7,6},{8,9},{9,8},{10,11... | collective-permute-start | bytes 393224 | tf_op jit(solution)/shard_map/ppermute | solution.py:50
  129.8 10.1 %collective-permute-start.39 = (bf16[128,512]{1,0:T(8,128)(2,1)S(1)}, bf16[128,512]{1,0:T(8,128)(2,1)S(1)}, u32[]{:S(2)}, u32[]{:S(2)}) collective-permute-start(bf16[128,512]{1,0:T(8,128)(2,1)S(1)} %get-tuple-element.100), channel_id=1, source_target_pairs={{0,2},{1,3},{2,0},{3,1},{4,6},{5,7},{6,4},{7,5},{8,10},{9,11},{10,... | collective-permute-start | bytes 393224 | tf_op jit(solution)/shard_map/ppermute | solution.py:50
  131.9 8.0 %collective-permute-start.40 = (bf16[128,512]{1,0:T(8,128)(2,1)S(1)}, bf16[128,512]{1,0:T(8,128)(2,1)S(1)}, u32[]{:S(2)}, u32[]{:S(2)}) collective-permute-start(bf16[128,512]{1,0:T(8,128)(2,1)S(1)} %get-tuple-element.99), channel_id=1, source_target_pairs={{0,3},{1,2},{2,1},{3,0},{4,7},{5,6},{6,5},{7,4},{8,11},{9,10},{10,... | collective-permute-start | bytes 393224 | tf_op jit(solution)/shard_map/ppermute | solution.py:50
  134.3 7.7 %collective-permute-start.43 = (bf16[128,512]{1,0:T(8,128)(2,1)S(1)}, bf16[128,512]{1,0:T(8,128)(2,1)S(1)}, u32[]{:S(2)}, u32[]{:S(2)}) collective-permute-start(bf16[128,512]{1,0:T(8,128)(2,1)S(1)} %get-tuple-element.104), channel_id=1, source_target_pairs={{0,1},{1,0},{2,3},{3,2},{4,5},{5,4},{6,7},{7,6},{8,9},{9,8},{10,11... | collective-permute-start | bytes 393224 | tf_op jit(solution)/shard_map/ppermute | solution.py:50
  134.7 10.8 %collective-permute-start.44 = (bf16[128,512]{1,0:T(8,128)(2,1)S(1)}, bf16[128,512]{1,0:T(8,128)(2,1)S(1)}, u32[]{:S(2)}, u32[]{:S(2)}) collective-permute-start(bf16[128,512]{1,0:T(8,128)(2,1)S(1)} %get-tuple-element.103), channel_id=1, source_target_pairs={{0,2},{1,3},{2,0},{3,1},{4,6},{5,7},{6,4},{7,5},{8,10},{9,11},{10,... | collective-permute-start | bytes 393224 | tf_op jit(solution)/shard_map/ppermute | solution.py:50
  136.3 9.2 %collective-permute-start.45 = (bf16[128,512]{1,0:T(8,128)(2,1)S(1)}, bf16[128,512]{1,0:T(8,128)(2,1)S(1)}, u32[]{:S(2)}, u32[]{:S(2)}) collective-permute-start(bf16[128,512]{1,0:T(8,128)(2,1)S(1)} %get-tuple-element.102), channel_id=1, source_target_pairs={{0,3},{1,2},{2,1},{3,0},{4,7},{5,6},{6,5},{7,4},{8,11},{9,10},{10,... | collective-permute-start | bytes 393224 | tf_op jit(solution)/shard_map/ppermute | solution.py:50
  139.9 7.7 %collective-permute-start.28 = (bf16[128,512]{1,0:T(8,128)(2,1)S(1)}, bf16[128,512]{1,0:T(8,128)(2,1)S(1)}, u32[]{:S(2)}, u32[]{:S(2)}) collective-permute-start(bf16[128,512]{1,0:T(8,128)(2,1)S(1)} %get-tuple-element.95), channel_id=1, source_target_pairs={{0,1},{1,0},{2,3},{3,2},{4,5},{5,4},{6,7},{7,6},{8,9},{9,8},{10,11... | collective-permute-start | bytes 393224 | tf_op jit(solution)/shard_map/ppermute | solution.py:50
  139.9 10.6 %collective-permute-start.29 = (bf16[128,512]{1,0:T(8,128)(2,1)S(1)}, bf16[128,512]{1,0:T(8,128)(2,1)S(1)}, u32[]{:S(2)}, u32[]{:S(2)}) collective-permute-start(bf16[128,512]{1,0:T(8,128)(2,1)S(1)} %get-tuple-element.94), channel_id=1, source_target_pairs={{0,2},{1,3},{2,0},{3,1},{4,6},{5,7},{6,4},{7,5},{8,10},{9,11},{10,... | collective-permute-start | bytes 393224 | tf_op jit(solution)/shard_map/ppermute | solution.py:50
  141.9 8.6 %collective-permute-start.30 = (bf16[128,512]{1,0:T(8,128)(2,1)S(1)}, bf16[128,512]{1,0:T(8,128)(2,1)S(1)}, u32[]{:S(2)}, u32[]{:S(2)}) collective-permute-start(bf16[128,512]{1,0:T(8,128)(2,1)S(1)} %get-tuple-element.93), channel_id=1, source_target_pairs={{0,3},{1,2},{2,1},{3,0},{4,7},{5,6},{6,5},{7,4},{8,11},{9,10},{10,... | collective-permute-start | bytes 393224 | tf_op jit(solution)/shard_map/ppermute | solution.py:50
  157.3 15.0 %collective-permute-start.49 = (bf16[128,512]{1,0:T(8,128)(2,1)S(1)}, bf16[128,512]{1,0:T(8,128)(2,1)S(1)}, u32[]{:S(2)}, u32[]{:S(2)}) collective-permute-start(bf16[128,512]{1,0:T(8,128)(2,1)S(1)} %get-tuple-element.92), channel_id=1, source_target_pairs={{0,1},{1,0},{2,3},{3,2},{4,5},{5,4},{6,7},{7,6},{8,9},{9,8},{10,11... | collective-permute-start | bytes 393224 | tf_op jit(solution)/shard_map/ppermute | solution.py:50
  157.9 15.9 %collective-permute-start.50 = (bf16[128,512]{1,0:T(8,128)(2,1)S(1)}, bf16[128,512]{1,0:T(8,128)(2,1)S(1)}, u32[]{:S(2)}, u32[]{:S(2)}) collective-permute-start(bf16[128,512]{1,0:T(8,128)(2,1)S(1)} %get-tuple-element.92), channel_id=1, source_target_pairs={{0,2},{1,3},{2,0},{3,1},{4,6},{5,7},{6,4},{7,5},{8,10},{9,11},{10,... | collective-permute-start | bytes 393224 | tf_op jit(solution)/shard_map/ppermute | solution.py:50
  159.2 15.2 %collective-permute-start.51 = (bf16[128,512]{1,0:T(8,128)(2,1)S(1)}, bf16[128,512]{1,0:T(8,128)(2,1)S(1)}, u32[]{:S(2)}, u32[]{:S(2)}) collective-permute-start(bf16[128,512]{1,0:T(8,128)(2,1)S(1)} %get-tuple-element.92), channel_id=1, source_target_pairs={{0,3},{1,2},{2,1},{3,0},{4,7},{5,6},{6,5},{7,4},{8,11},{9,10},{10,... | collective-permute-start | bytes 393224 | tf_op jit(solution)/shard_map/ppermute | solution.py:50
  160.9 15.6 %collective-permute-start.52 = (bf16[128,512]{1,0:T(8,128)(2,1)S(1)}, bf16[128,512]{1,0:T(8,128)(2,1)S(1)}, u32[]{:S(2)}, u32[]{:S(2)}) collective-permute-start(bf16[128,512]{1,0:T(8,128)(2,1)S(1)} %get-tuple-element.91), channel_id=1, source_target_pairs={{0,1},{1,0},{2,3},{3,2},{4,5},{5,4},{6,7},{7,6},{8,9},{9,8},{10,11... | collective-permute-start | bytes 393224 | tf_op jit(solution)/shard_map/ppermute | solution.py:50
  173.8 14.8 %collective-permute-start.46 = (bf16[128,512]{1,0:T(8,128)(2,1)S(1)}, bf16[128,512]{1,0:T(8,128)(2,1)S(1)}, u32[]{:S(2)}, u32[]{:S(2)}) collective-permute-start(bf16[128,512]{1,0:T(8,128)(2,1)S(1)} %get-tuple-element.89), channel_id=1, source_target_pairs={{0,1},{1,0},{2,3},{3,2},{4,5},{5,4},{6,7},{7,6},{8,9},{9,8},{10,11... | collective-permute-start | bytes 393224 | tf_op jit(solution)/shard_map/ppermute | solution.py:50
  174.4 14.3 %collective-permute-start.47 = (bf16[128,512]{1,0:T(8,128)(2,1)S(1)}, bf16[128,512]{1,0:T(8,128)(2,1)S(1)}, u32[]{:S(2)}, u32[]{:S(2)}) collective-permute-start(bf16[128,512]{1,0:T(8,128)(2,1)S(1)} %get-tuple-element.89), channel_id=1, source_target_pairs={{0,2},{1,3},{2,0},{3,1},{4,6},{5,7},{6,4},{7,5},{8,10},{9,11},{10,... | collective-permute-start | bytes 393224 | tf_op jit(solution)/shard_map/ppermute | solution.py:50
  176.5 7.6 %collective-permute-start.55 = (bf16[128,512]{1,0:T(8,128)(2,1)S(1)}, bf16[128,512]{1,0:T(8,128)(2,1)S(1)}, u32[]{:S(2)}, u32[]{:S(2)}) collective-permute-start(bf16[128,512]{1,0:T(8,128)(2,1)S(1)} %get-tuple-element.90), channel_id=1, source_target_pairs={{0,1},{1,0},{2,3},{3,2},{4,5},{5,4},{6,7},{7,6},{8,9},{9,8},{10,11... | collective-permute-start | bytes 393224 | tf_op jit(solution)/shard_map/ppermute | solution.py:50
  178.1 9.2 %collective-permute-start.56 = (bf16[128,512]{1,0:T(8,128)(2,1)S(1)}, bf16[128,512]{1,0:T(8,128)(2,1)S(1)}, u32[]{:S(2)}, u32[]{:S(2)}) collective-permute-start(bf16[128,512]{1,0:T(8,128)(2,1)S(1)} %get-tuple-element.90), channel_id=1, source_target_pairs={{0,2},{1,3},{2,0},{3,1},{4,6},{5,7},{6,4},{7,5},{8,10},{9,11},{10,... | collective-permute-start | bytes 393224 | tf_op jit(solution)/shard_map/ppermute | solution.py:50
  179.9 8.1 %collective-permute-start.57 = (bf16[128,512]{1,0:T(8,128)(2,1)S(1)}, bf16[128,512]{1,0:T(8,128)(2,1)S(1)}, u32[]{:S(2)}, u32[]{:S(2)}) collective-permute-start(bf16[128,512]{1,0:T(8,128)(2,1)S(1)} %get-tuple-element.90), channel_id=1, source_target_pairs={{0,3},{1,2},{2,1},{3,0},{4,7},{5,6},{6,5},{7,4},{8,11},{9,10},{10,... | collective-permute-start | bytes 393224 | tf_op jit(solution)/shard_map/ppermute | solution.py:50
  187.3 9.1 %collective-permute-start.82 = (f32[4,2048]{1,0:T(4,128)S(1)}, f32[4,2048]{1,0:T(4,128)S(1)}, u32[]{:S(2)}, u32[]{:S(2)}) collective-permute-start(f32[4,2048]{1,0:T(4,128)S(1)} %add.432), channel_id=1, source_target_pairs={{0,1},{1,0},{2,3},{3,2},{4,5},{5,4},{6,7},{7,6},{8,9},{9,8},{10,11... | collective-permute-start | bytes 98312 | tf_op jit(solution)/shard_map/ppermute | solution.py:50
  194.8 37.3 %collective-permute-start.75 = (bf16[256,768]{1,0:T(8,128)(2,1)S(1)}, bf16[256,768]{1,0:T(8,128)(2,1)S(1)}, u32[]{:S(2)}, u32[]{:S(2)}) collective-permute-start(bf16[256,768]{1,0:T(8,128)(2,1)S(1)} %convolution_convert_fusion.5), channel_id=1, source_target_pairs={{0,4},{4,0},{8,12},{12,8},{16,20},{20,16},{24,28},{28,24},{1,5},{5... | collective-permute-start | bytes 1179656 | tf_op jit(solution)/shard_map/ppermute | solution.py:40
  196.3 9.3 %collective-permute-start.72 = (bf16[256,768]{1,0:T(8,128)(2,1)S(1)}, bf16[256,768]{1,0:T(8,128)(2,1)S(1)}, u32[]{:S(2)}, u32[]{:S(2)}) collective-permute-start(bf16[256,768]{1,0:T(8,128)(2,1)S(1)} %convolution_convert_fusion.7), channel_id=1, source_target_pairs={{0,4},{4,0},{8,12},{12,8},{16,20},{20,16},{24,28},{28,24},{1,5},{5... | collective-permute-start | bytes 1179656 | tf_op jit(solution)/shard_map/ppermute | solution.py:40
  200.4 15.8 %collective-permute-start.65 = (bf16[256,768]{1,0:T(8,128)(2,1)S(1)}, bf16[256,768]{1,0:T(8,128)(2,1)S(1)}, u32[]{:S(2)}, u32[]{:S(2)}) collective-permute-start(bf16[256,768]{1,0:T(8,128)(2,1)S(1)} %convolution_convert_fusion.11), channel_id=1, source_target_pairs={{0,4},{4,0},{8,12},{12,8},{16,20},{20,16},{24,28},{28,24},{1,5},{5... | collective-permute-start | bytes 1179656 | tf_op jit(solution)/shard_map/ppermute | solution.py:40
  201.9 12.9 %collective-permute-start.74 = (bf16[256,768]{1,0:T(8,128)(2,1)S(1)}, bf16[256,768]{1,0:T(8,128)(2,1)S(1)}, u32[]{:S(2)}, u32[]{:S(2)}) collective-permute-start(bf16[256,768]{1,0:T(8,128)(2,1)S(1)} %fusion.36), channel_id=1, source_target_pairs={{0,8},{4,12},{8,24},{12,28},{16,0},{20,4},{24,16},{28,20},{1,9},{5... | collective-permute-start | bytes 1179656 | tf_op jit(solution)/shard_map/ppermute | solution.py:33
  204.2 19.1 %collective-permute-start.67 = (bf16[256,768]{1,0:T(8,128)(2,1)S(1)}, bf16[256,768]{1,0:T(8,128)(2,1)S(1)}, u32[]{:S(2)}, u32[]{:S(2)}) collective-permute-start(bf16[256,768]{1,0:T(8,128)(2,1)S(1)} %fusion.24), channel_id=1, source_target_pairs={{0,8},{4,12},{8,24},{12,28},{16,0},{20,4},{24,16},{28,20},{1,9},{5... | collective-permute-start | bytes 1179656 | tf_op jit(solution)/shard_map/ppermute | solution.py:33
  205.5 18.2 %collective-permute-start.58 = (bf16[256,768]{1,0:T(8,128)(2,1)S(1)}, bf16[256,768]{1,0:T(8,128)(2,1)S(1)}, u32[]{:S(2)}, u32[]{:S(2)}) collective-permute-start(bf16[256,768]{1,0:T(8,128)(2,1)S(1)} %convolution_convert_fusion.15), channel_id=1, source_target_pairs={{0,4},{4,0},{8,12},{12,8},{16,20},{20,16},{24,28},{28,24},{1,5},{5... | collective-permute-start | bytes 1179656 | tf_op jit(solution)/shard_map/ppermute | solution.py:40
  214.9 15.9 %collective-permute-start.60 = (bf16[256,768]{1,0:T(8,128)(2,1)S(1)}, bf16[256,768]{1,0:T(8,128)(2,1)S(1)}, u32[]{:S(2)}, u32[]{:S(2)}) collective-permute-start(bf16[256,768]{1,0:T(8,128)(2,1)S(1)} %fusion.12), channel_id=1, source_target_pairs={{0,8},{4,12},{8,24},{12,28},{16,0},{20,4},{24,16},{28,20},{1,9},{5... | collective-permute-start | bytes 1179656 | tf_op jit(solution)/shard_map/ppermute | solution.py:33
  216.2 16.8 %collective-permute-start.77 = (bf16[256,768]{1,0:T(8,128)(2,1)S(1)}, bf16[256,768]{1,0:T(8,128)(2,1)S(1)}, u32[]{:S(2)}, u32[]{:S(2)}) collective-permute-start(bf16[256,768]{1,0:T(8,128)(2,1)S(1)} %convolution_convert_fusion.4), channel_id=1, source_target_pairs={{0,4},{4,0},{8,12},{12,8},{16,20},{20,16},{24,28},{28,24},{1,5},{5... | collective-permute-start | bytes 1179656 | tf_op jit(solution)/shard_map/ppermute | solution.py:40
  223.3 12.2 %collective-permute-start.68 = (bf16[256,768]{1,0:T(8,128)(2,1)S(1)}, bf16[256,768]{1,0:T(8,128)(2,1)S(1)}, u32[]{:S(2)}, u32[]{:S(2)}) collective-permute-start(bf16[256,768]{1,0:T(8,128)(2,1)S(1)} %convolution_convert_fusion.9), channel_id=1, source_target_pairs={{0,4},{4,0},{8,12},{12,8},{16,20},{20,16},{24,28},{28,24},{1,5},{5... | collective-permute-start | bytes 1179656 | tf_op jit(solution)/shard_map/ppermute | solution.py:40
  223.7 13.0 %collective-permute-start.70 = (bf16[256,768]{1,0:T(8,128)(2,1)S(1)}, bf16[256,768]{1,0:T(8,128)(2,1)S(1)}, u32[]{:S(2)}, u32[]{:S(2)}) collective-permute-start(bf16[256,768]{1,0:T(8,128)(2,1)S(1)} %convolution_convert_fusion.8), channel_id=1, source_target_pairs={{0,4},{4,0},{8,12},{12,8},{16,20},{20,16},{24,28},{28,24},{1,5},{5... | collective-permute-start | bytes 1179656 | tf_op jit(solution)/shard_map/ppermute | solution.py:40
  230.8 11.0 %collective-permute-start.61 = (bf16[256,768]{1,0:T(8,128)(2,1)S(1)}, bf16[256,768]{1,0:T(8,128)(2,1)S(1)}, u32[]{:S(2)}, u32[]{:S(2)}) collective-permute-start(bf16[256,768]{1,0:T(8,128)(2,1)S(1)} %convolution_convert_fusion.13), channel_id=1, source_target_pairs={{0,4},{4,0},{8,12},{12,8},{16,20},{20,16},{24,28},{28,24},{1,5},{5... | collective-permute-start | bytes 1179656 | tf_op jit(solution)/shard_map/ppermute | solution.py:40
  232.1 10.9 %collective-permute-start.63 = (bf16[256,768]{1,0:T(8,128)(2,1)S(1)}, bf16[256,768]{1,0:T(8,128)(2,1)S(1)}, u32[]{:S(2)}, u32[]{:S(2)}) collective-permute-start(bf16[256,768]{1,0:T(8,128)(2,1)S(1)} %convolution_convert_fusion.12), channel_id=1, source_target_pairs={{0,4},{4,0},{8,12},{12,8},{16,20},{20,16},{24,28},{28,24},{1,5},{5... | collective-permute-start | bytes 1179656 | tf_op jit(solution)/shard_map/ppermute | solution.py:40
  233.0 14.9 %collective-permute-start.76 = (bf16[256,768]{1,0:T(8,128)(2,1)S(1)}, bf16[256,768]{1,0:T(8,128)(2,1)S(1)}, u32[]{:S(2)}, u32[]{:S(2)}) collective-permute-start(bf16[256,768]{1,0:T(8,128)(2,1)S(1)} %fusion.40), channel_id=1, source_target_pairs={{0,24},{4,28},{8,0},{12,4},{16,8},{20,12},{24,16},{28,20},{1,25},{... | collective-permute-start | bytes 1179656 | tf_op jit(solution)/shard_map/ppermute | solution.py:27
  235.5 18.9 %collective-permute-start.78 = (bf16[256,768]{1,0:T(8,128)(2,1)S(1)}, bf16[256,768]{1,0:T(8,128)(2,1)S(1)}, u32[]{:S(2)}, u32[]{:S(2)}) collective-permute-start(bf16[256,768]{1,0:T(8,128)(2,1)S(1)} %fusion.44), channel_id=1, source_target_pairs={{0,8},{4,12},{8,16},{12,20},{16,24},{20,28},{24,0},{28,4},{1,9},{5... | collective-permute-start | bytes 1179656 | tf_op jit(solution)/shard_map/ppermute | solution.py:27
  236.8 26.1 %collective-permute-start.69 = (bf16[256,768]{1,0:T(8,128)(2,1)}, bf16[256,768]{1,0:T(8,128)(2,1)S(1)}, u32[]{:S(2)}, u32[]{:S(2)}) collective-permute-start(bf16[256,768]{1,0:T(8,128)(2,1)} %fusion.28), channel_id=1, source_target_pairs={{0,24},{4,28},{8,0},{12,4},{16,8},{20,12},{24,16},{28,20},{1,25},{... | collective-permute-start | bytes 1179656 | tf_op jit(solution)/shard_map/ppermute | solution.py:27
  241.7 29.6 %collective-permute-start.71 = (bf16[256,768]{1,0:T(8,128)(2,1)}, bf16[256,768]{1,0:T(8,128)(2,1)S(1)}, u32[]{:S(2)}, u32[]{:S(2)}) collective-permute-start(bf16[256,768]{1,0:T(8,128)(2,1)} %fusion.32), channel_id=1, source_target_pairs={{0,8},{4,12},{8,16},{12,20},{16,24},{20,28},{24,0},{28,4},{1,9},{5... | collective-permute-start | bytes 1179656 | tf_op jit(solution)/shard_map/ppermute | solution.py:27
  242.9 35.7 %collective-permute-start.62 = (bf16[256,768]{1,0:T(8,128)(2,1)}, bf16[256,768]{1,0:T(8,128)(2,1)}, u32[]{:S(2)}, u32[]{:S(2)}) collective-permute-start(bf16[256,768]{1,0:T(8,128)(2,1)} %fusion.16), channel_id=1, source_target_pairs={{0,24},{4,28},{8,0},{12,4},{16,8},{20,12},{24,16},{28,20},{1,25},{... | collective-permute-start | bytes 1179656 | tf_op jit(solution)/shard_map/ppermute | solution.py:27
  247.9 39.4 %collective-permute-start.64 = (bf16[256,768]{1,0:T(8,128)(2,1)}, bf16[256,768]{1,0:T(8,128)(2,1)}, u32[]{:S(2)}, u32[]{:S(2)}) collective-permute-start(bf16[256,768]{1,0:T(8,128)(2,1)} %fusion.20), channel_id=1, source_target_pairs={{0,8},{4,12},{8,16},{12,20},{16,24},{20,28},{24,0},{28,4},{1,9},{5... | collective-permute-start | bytes 1179656 | tf_op jit(solution)/shard_map/ppermute | solution.py:27
  (73 other events, 655.0 us)
